TPU v7x, 32 devices: a whole 2x2x4 slice. The times are simulated.
32 devices in a mesh: exp: 8 (over z, y), hid: 4 (over x, core).
Axes of the slice: x: 2, y: 2, z: 4, core: 2. Of those that a mesh axis runs over, the one named last changes fastest.
Arguments:
- patches: bfloat16 [8192, 768], P(('exp', 'hid')), may hold values from -6 to 6
- cotangent: bfloat16 [8192, 768], P(('exp', 'hid')), may hold values from -6 to 6
- timesteps: int32 [32], P(('exp', 'hid')), may hold values from 0 to 999
- labels: int32 [32], P(('exp', 'hid')), may hold values from 0 to 1000
- routes: int32 [8192, 2], P(('exp', 'hid')), may hold values from 0 to 7, as said below
- slot_index: int32 [8192, 2], P(('exp', 'hid')), may hold values from 0 to 72, as said below
- time_weight: bfloat16 [256, 768], replicated, may hold values from -0.375 to 0.375
- time_bias: float32 [768], replicated, may hold values from -3 to 3
- class_table: bfloat16 [1001, 768], replicated, may hold values from -3 to 3
- ada_weight: bfloat16 [768, 4608], replicated, may hold values from -0.21875 to 0.21875
- ada_bias: float32 [4608], replicated, may hold values from -3 to 3
- qkv_weight: bfloat16 [768, 2304], replicated, may hold values from -0.21875 to 0.21875
- proj_weight: bfloat16 [768, 768], replicated, may hold values from -1.25 to 1.25
- router_weight: bfloat16 [768, 8], replicated, may hold values from -0.4375 to 0.4375
- shared_in: bfloat16 [768, 3072], P(None, 'hid'), may hold values from -0.21875 to 0.21875
- shared_out: bfloat16 [3072, 768], P('hid'), may hold values from -0.109375 to 0.109375
- expert_in: bfloat16 [8, 768, 3072], P('exp', None, 'hid'), may hold values from -0.21875 to 0.21875
- expert_out: bfloat16 [8, 3072, 768], P('exp', 'hid'), may hold values from -0.109375 to 0.109375
Outputs:
- output: bfloat16 [8192, 768], P(('exp', 'hid'))
- grad_patches: bfloat16 [8192, 768], P(('exp', 'hid'))
- grad_time_weight: float32 [256, 768], P('exp')
- grad_time_bias: float32 [768], replicated
- grad_class_table: float32 [1001, 768], replicated
- grad_ada_weight: float32 [768, 4608], P('exp')
- grad_ada_bias: float32 [4608], replicated
- grad_qkv_weight: float32 [768, 2304], P('exp')
- grad_proj_weight: float32 [768, 768], P('exp')
- grad_router_weight: float32 [768, 8], P('exp')
- grad_shared_in: float32 [768, 3072], P('exp', 'hid')
- grad_shared_out: float32 [3072, 768], P('hid', 'exp')
- grad_expert_in: float32 [8, 768, 3072], P('exp', None, 'hid')
- grad_expert_out: float32 [8, 3072, 768], P('exp', 'hid')
- expert_counts: float32 [8], replicated
Inputs may be any that keep to these rules, and one draw needn't show every extreme that they name: `routes`: each patch names two different experts, its first and second choice. On every device the first 72 patches name the same expert first. `slot_index`: for each pair of a patch and a choice: the number of earlier pairs of the same device (patch order, first choice before second) that name the same expert, or 72 where that number is 72 or more (the pair is dropped).
All inputs are finite; a program needn't handle non-finite values.
Results may differ from a plain program's by a relative error of at most 0.028.
Values may be sent and summed in bfloat16 or wider, within the bound.
No kernel may reach another device: no remote copies, remote signals or barrier semaphores. Data moves between devices by JAX's collectives and lax.ppermute only.
A program may use at most 192 MiB of HBM per device.

v0:
```python
import math

import jax
import jax.numpy as jnp
from jax import lax
from jax.sharding import PartitionSpec as P

HEADS = 12
HDIM = 64
SEQ = 256


eps_norm = 1e-06
highest = lax.Precision.HIGHEST


def mat_prod(left_side, right_side):
    return jnp.dot(left_side, right_side, preferred_element_type=jnp.float32)


def prod_rows(left_side, right_side):
    return lax.dot_general(
        left_side, right_side, (((0,), (0,)), ((), ())), preferred_element_type=jnp.float32
    )


def prod_cols(left_side, right_side):
    return lax.dot_general(
        left_side, right_side, (((1,), (1,)), ((), ())), preferred_element_type=jnp.float32
    )


def sinus_table(timesteps, columns):
    half_cols = columns // 2
    freqs = jnp.exp(-math.log(10000.0) * jnp.arange(half_cols, dtype=jnp.float32) / half_cols)
    angles = timesteps.astype(jnp.float32)[:, None] * freqs[None, :]
    return jnp.concatenate([jnp.cos(angles), jnp.sin(angles)], axis=1)


def normalize(inputs):
    center = inputs - jnp.mean(inputs, axis=-1, keepdims=True)
    inverse = lax.rsqrt(jnp.mean(center * center, axis=-1, keepdims=True) + eps_norm)
    return (center * inverse, inverse)


def normalize_back(normed, inverse, grad_normed):
    return inverse * (
        grad_normed
        - jnp.mean(grad_normed, axis=-1, keepdims=True)
        - normed * jnp.mean(grad_normed * normed, axis=-1, keepdims=True)
    )


def gelu_back(pre_act, grad_act):
    return jax.vjp(jax.nn.gelu, pre_act)[1](grad_act)[0]


def attention_weights(queries, key_rows, score_scale):
    scores = (
        jnp.einsum("bqhd,bkhd->bhqk", queries, key_rows, preferred_element_type=jnp.float32)
        * score_scale
    )
    row_max = jnp.max(scores, axis=-1, keepdims=True)
    log_total = row_max + jnp.log(jnp.sum(jnp.exp(scores - row_max), axis=-1, keepdims=True))
    return jnp.exp(scores - log_total)


def block_terms(
    first_row,
    row_count,
    per_rows,
    routed_rows,
    token_rows,
    routed,
    shared,
    routed_weight,
    shared_weight,
    product,
):
    pieces = []
    for offset in range(row_count // per_rows):
        block_index = first_row // per_rows + offset
        routed_part = lax.dynamic_slice_in_dim(routed, block_index * routed_rows, routed_rows, 0)
        shared_part = lax.dynamic_slice_in_dim(shared, block_index * token_rows, token_rows, 0)
        pieces.append(product(routed_part, routed_weight))
        pieces.append(product(shared_part, shared_weight))
    return jnp.concatenate(pieces, axis=0)


def per_device(
    patches,
    cotangent,
    timesteps,
    labels,
    routes,
    slot_index,
    time_weight,
    time_bias,
    class_table,
    ada_weight,
    ada_bias,
    qkv_weight,
    proj_weight,
    router_weight,
    shared_in,
    shared_out,
    expert_in,
    expert_out,
):
    tokens, model_dim = patches.shape
    item_count = timesteps.shape[0]
    experts = lax.axis_size("exp")
    capacity = 9 * tokens // (4 * experts)
    slots_all = experts * capacity
    per_rows = slots_all + tokens
    score_scale = 1.0 / math.sqrt(HDIM)
    freq_emb = sinus_table(timesteps, time_weight.shape[0]).astype(jnp.bfloat16)
    label_hot = (
        labels[:, None] == jnp.arange(class_table.shape[0], dtype=jnp.int32)[None, :]
    ).astype(jnp.bfloat16)
    condition = mat_prod(freq_emb, time_weight) + time_bias + mat_prod(label_hot, class_table)
    silu_cond = jax.nn.silu(condition).astype(jnp.bfloat16)
    modulate = mat_prod(silu_cond, ada_weight) + ada_bias
    shift_one, scale_one, gate_one, shift_two, scale_two, gate_two = [
        modulate[:, None, block_index * model_dim : (block_index + 1) * model_dim]
        for block_index in range(6)
    ]
    residual = patches.astype(jnp.float32).reshape(item_count, SEQ, model_dim)
    normed_one, inverse_one = normalize(residual)
    flat_one = (
        (normed_one * (1.0 + scale_one) + shift_one).astype(jnp.bfloat16).reshape(tokens, model_dim)
    )
    qkv_rows = (
        mat_prod(flat_one, qkv_weight).astype(jnp.bfloat16).reshape(item_count, SEQ, 3, HEADS, HDIM)
    )
    queries, key_rows, value_rows = (qkv_rows[:, :, 0], qkv_rows[:, :, 1], qkv_rows[:, :, 2])
    attention_low = attention_weights(queries, key_rows, score_scale).astype(jnp.bfloat16)
    attended = jnp.einsum(
        "bhqk,bkhd->bqhd", attention_low, value_rows, preferred_element_type=jnp.float32
    )
    attended_low = attended.astype(jnp.bfloat16).reshape(tokens, model_dim)
    branch_one = mat_prod(attended_low, proj_weight).reshape(item_count, SEQ, model_dim)
    residual_one = residual + gate_one * branch_one
    normed_two, inverse_two = normalize(residual_one)
    hidden_two = (
        (normed_two * (1.0 + scale_two) + shift_two).astype(jnp.bfloat16).reshape(tokens, model_dim)
    )
    logits = mat_prod(hidden_two, router_weight)
    expert_ids = jnp.arange(experts, dtype=jnp.int32)[None, :]
    first_hot = (routes[:, 0:1] == expert_ids).astype(jnp.float32)
    second_hot = (routes[:, 1:2] == expert_ids).astype(jnp.float32)
    logit_gap = jnp.sum(logits * first_hot, axis=1) - jnp.sum(logits * second_hot, axis=1)
    gate_first = jax.nn.sigmoid(logit_gap)[:, None]
    gate_second = 1.0 - gate_first
    slot_ids = jnp.arange(slots_all, dtype=jnp.int32)[None, :]
    kept_first = slot_index[:, 0:1] < capacity
    kept_second = slot_index[:, 1:2] < capacity
    dispatch_first = (
        (routes[:, 0:1] * capacity + slot_index[:, 0:1] == slot_ids) & kept_first
    ).astype(jnp.bfloat16)
    dispatch_second = (
        (routes[:, 1:2] * capacity + slot_index[:, 1:2] == slot_ids) & kept_second
    ).astype(jnp.bfloat16)
    dispatch_both = dispatch_first + dispatch_second
    send_rows = prod_rows(dispatch_both, hidden_two).astype(jnp.bfloat16)
    recv_rows = lax.all_to_all(send_rows, "exp", split_axis=0, concat_axis=0, tiled=True)
    rows_all, tokens_all = (
        lax.all_gather(recv_rows, "hid", axis=0, tiled=True),
        lax.all_gather(hidden_two, "hid", axis=0, tiled=True),
    )
    pre_routed = mat_prod(rows_all, expert_in[0])
    act_routed = jax.nn.gelu(pre_routed).astype(jnp.bfloat16)
    pre_shared = mat_prod(tokens_all, shared_in)
    act_shared = jax.nn.gelu(pre_shared).astype(jnp.bfloat16)
    summed = lax.psum_scatter(
        block_terms(
            jnp.int32(0),
            per_rows * lax.axis_size("hid"),
            per_rows,
            slots_all,
            tokens,
            act_routed,
            act_shared,
            expert_out[0],
            shared_out,
            mat_prod,
        ).astype(jnp.bfloat16),
        "hid",
        scatter_dimension=0,
        tiled=True,
    ).astype(jnp.float32)
    routed_out = summed[:slots_all].astype(jnp.bfloat16)
    shared_sum = summed[slots_all:]
    back_rows = lax.all_to_all(routed_out, "exp", split_axis=0, concat_axis=0, tiled=True)
    picked_first = mat_prod(dispatch_first, back_rows)
    picked_second = mat_prod(dispatch_second, back_rows)
    moe_out = gate_first * picked_first + gate_second * picked_second
    branch_two = (shared_sum + moe_out).reshape(item_count, SEQ, model_dim)
    result = residual_one + gate_two * branch_two
    output = result.reshape(tokens, model_dim).astype(jnp.bfloat16)
    grad_result = cotangent.astype(jnp.float32).reshape(item_count, SEQ, model_dim)
    grad_gate_two = jnp.sum(branch_two * grad_result, axis=1)
    grad_branch = (gate_two * grad_result).reshape(tokens, model_dim)
    grad_branch_low = grad_branch.astype(jnp.bfloat16)
    grad_gate_first = jnp.sum(grad_branch * picked_first, axis=1)
    grad_gate_second = jnp.sum(grad_branch * picked_second, axis=1)
    grad_gap = (grad_gate_first - grad_gate_second) * gate_first[:, 0] * gate_second[:, 0]
    grad_logits = (grad_gap[:, None] * (first_hot - second_hot)).astype(jnp.bfloat16)
    weight_router = prod_rows(hidden_two, grad_logits)
    grad_hidden = prod_cols(grad_logits, router_weight)
    weighted = (
        dispatch_first.astype(jnp.float32) * gate_first
        + dispatch_second.astype(jnp.float32) * gate_second
    )
    grad_rows = lax.dot_general(
        weighted,
        grad_branch,
        (((0,), (0,)), ((), ())),
        precision=highest,
        preferred_element_type=jnp.float32,
    ).astype(jnp.bfloat16)
    grad_recv = lax.all_to_all(grad_rows, "exp", split_axis=0, concat_axis=0, tiled=True)
    grad_routed_all, grad_shared_all = (
        lax.all_gather(grad_recv, "hid", axis=0, tiled=True),
        lax.all_gather(grad_branch_low, "hid", axis=0, tiled=True),
    )
    grad_pre_routed = gelu_back(pre_routed, prod_cols(grad_routed_all, expert_out[0])).astype(
        jnp.bfloat16
    )
    weight_expert_out = prod_rows(act_routed, grad_routed_all)
    weight_expert_in = prod_rows(rows_all, grad_pre_routed)
    grad_pre_shared = gelu_back(pre_shared, prod_cols(grad_shared_all, shared_out)).astype(
        jnp.bfloat16
    )
    weight_shared_out = prod_rows(act_shared, grad_shared_all)
    weight_shared_in = prod_rows(tokens_all, grad_pre_shared)
    back_sum = lax.psum_scatter(
        block_terms(
            jnp.int32(0),
            per_rows * lax.axis_size("hid"),
            per_rows,
            slots_all,
            tokens,
            grad_pre_routed,
            grad_pre_shared,
            expert_in[0],
            shared_in,
            prod_cols,
        ).astype(jnp.bfloat16),
        "hid",
        scatter_dimension=0,
        tiled=True,
    ).astype(jnp.float32)
    grad_send = back_sum[:slots_all].astype(jnp.bfloat16)
    shared_input_term = back_sum[slots_all:]
    grad_dispatch = lax.all_to_all(grad_send, "exp", split_axis=0, concat_axis=0, tiled=True)
    grad_hidden = grad_hidden + shared_input_term + mat_prod(dispatch_both, grad_dispatch)
    grad_hidden = grad_hidden.reshape(item_count, SEQ, model_dim)
    grad_shift_two = jnp.sum(grad_hidden, axis=1)
    grad_scale_two = jnp.sum(grad_hidden * normed_two, axis=1)
    grad_residual = grad_result + normalize_back(
        normed_two, inverse_two, grad_hidden * (1.0 + scale_two)
    )
    grad_gate_one = jnp.sum(branch_one * grad_residual, axis=1)
    grad_branch_one = (gate_one * grad_residual).reshape(tokens, model_dim).astype(jnp.bfloat16)
    weight_proj = prod_rows(attended_low, grad_branch_one)
    grad_attended = (
        prod_cols(grad_branch_one, proj_weight)
        .astype(jnp.bfloat16)
        .reshape(item_count, SEQ, HEADS, HDIM)
    )
    attention = attention_weights(queries, key_rows, score_scale)
    attention_low = attention.astype(jnp.bfloat16)
    grad_probs = jnp.einsum(
        "bqhd,bkhd->bhqk", grad_attended, value_rows, preferred_element_type=jnp.float32
    )
    grad_values = jnp.einsum(
        "bhqk,bqhd->bkhd", attention_low, grad_attended, preferred_element_type=jnp.float32
    )
    grad_scores = attention * (grad_probs - jnp.sum(attention * grad_probs, axis=-1, keepdims=True))
    grad_scores_low = (grad_scores * score_scale).astype(jnp.bfloat16)
    grad_queries = jnp.einsum(
        "bhqk,bkhd->bqhd", grad_scores_low, key_rows, preferred_element_type=jnp.float32
    )
    grad_keys = jnp.einsum(
        "bhqk,bqhd->bkhd", grad_scores_low, queries, preferred_element_type=jnp.float32
    )
    grad_qkv = (
        jnp.stack([grad_queries, grad_keys, grad_values], axis=2)
        .reshape(tokens, 3 * model_dim)
        .astype(jnp.bfloat16)
    )
    weight_qkv = prod_rows(flat_one, grad_qkv)
    grad_hidden_one = prod_cols(grad_qkv, qkv_weight).reshape(item_count, SEQ, model_dim)
    grad_shift_one = jnp.sum(grad_hidden_one, axis=1)
    grad_scale_one = jnp.sum(grad_hidden_one * normed_one, axis=1)
    grad_input = grad_residual + normalize_back(
        normed_one, inverse_one, grad_hidden_one * (1.0 + scale_one)
    )
    grad_patches = grad_input.reshape(tokens, model_dim).astype(jnp.bfloat16)
    grad_modulate = jnp.concatenate(
        [
            grad_shift_one,
            grad_scale_one,
            grad_gate_one,
            grad_shift_two,
            grad_scale_two,
            grad_gate_two,
        ],
        axis=1,
    )
    bias_ada = jnp.sum(grad_modulate, axis=0)
    grad_mod_low = grad_modulate.astype(jnp.bfloat16)
    weight_ada = prod_rows(silu_cond, grad_mod_low)
    grad_condition = jax.vjp(jax.nn.silu, condition)[1](prod_cols(grad_mod_low, ada_weight))[0]
    bias_time = jnp.sum(grad_condition, axis=0)
    table_grad = lax.dot_general(
        label_hot.astype(jnp.float32),
        grad_condition,
        (((0,), (0,)), ((), ())),
        precision=highest,
        preferred_element_type=jnp.float32,
    )
    weight_time = prod_rows(freq_emb, grad_condition.astype(jnp.bfloat16))
    counts_local = jnp.sum(
        first_hot * kept_first.astype(jnp.float32) + second_hot * kept_second.astype(jnp.float32),
        axis=0,
    )
    bias_time, bias_ada, table_grad, expert_counts = lax.psum(
        (bias_time, bias_ada, table_grad, counts_local), ("exp", "hid")
    )
    reduced = (
        lax.psum_scatter(weight_qkv, "exp", scatter_dimension=0, tiled=True),
        lax.psum_scatter(weight_proj, "exp", scatter_dimension=0, tiled=True),
        lax.psum_scatter(weight_ada, "exp", scatter_dimension=0, tiled=True),
        lax.psum_scatter(weight_time, "exp", scatter_dimension=0, tiled=True),
        lax.psum_scatter(weight_router, "exp", scatter_dimension=0, tiled=True),
        lax.psum_scatter(weight_shared_in, "exp", scatter_dimension=0, tiled=True),
        lax.psum_scatter(weight_shared_out, "exp", scatter_dimension=1, tiled=True),
    )
    dense = (
        lax.psum(reduced[0].astype(jnp.bfloat16), "hid").astype(jnp.float32),
        lax.psum(reduced[1].astype(jnp.bfloat16), "hid").astype(jnp.float32),
        lax.psum(reduced[2].astype(jnp.bfloat16), "hid").astype(jnp.float32),
        lax.psum(reduced[3].astype(jnp.bfloat16), "hid").astype(jnp.float32),
        lax.psum(reduced[4].astype(jnp.bfloat16), "hid").astype(jnp.float32),
    )
    return (
        output,
        grad_patches,
        dense[3],
        bias_time,
        table_grad,
        dense[2],
        bias_ada,
        dense[0],
        dense[1],
        dense[4],
        reduced[5],
        reduced[6],
        weight_expert_in[None],
        weight_expert_out[None],
        expert_counts,
    )


def solution(mesh):
    placed = (
        P(("exp", "hid"), None),
        P(("exp", "hid"), None),
        P(("exp", "hid")),
        P(("exp", "hid")),
        P(("exp", "hid"), None),
        P(("exp", "hid"), None),
        P(),
        P(),
        P(),
        P(),
        P(),
        P(),
        P(),
        P(),
        P(None, "hid"),
        P("hid", None),
        P("exp", None, "hid"),
        P("exp", "hid", None),
    )
    return jax.shard_map(
        per_device,
        mesh=mesh,
        in_specs=placed,
        out_specs=(
            P(("exp", "hid"), None),
            P(("exp", "hid"), None),
            P("exp", None),
            P(),
            P(),
            P("exp", None),
            P(),
            P("exp", None),
            P("exp", None),
            P("exp", None),
            P("exp", "hid"),
            P("hid", "exp"),
            P("exp", None, "hid"),
            P("exp", "hid", None),
            P(),
        ),
        check_vma=False,
    )
```

profile of v0, /device:TPU:0, one launch (start us, length us, event | category | flops | bytes accessed | tf_op | source)
XLA Modules:
  0.0 1208.4 jit_solution(5032542164118355768)
XLA Ops:
  14.4 4.1 convolution_reduce_fusion
  23.6 3.2 convolution_convert_fusion
  26.8 2.4 copy.48
  29.1 1.8 multiply_reduce_fusion.1
  31.5 2.7 convolution_convert_fusion.21
  41.5 30.0 %all_to_all.48 = bf16[8,72,768]{2,1,0:T(8,128)(2,1)} all-to-all(bf16[8,72,768]{2,1,0:T(8,128)(2,1)S(1)} %bitcast.151), channel_id=1, replica_groups=mesh['exp'=8,'hid'=4] {'exp'}, dimensions={0} | all-to-all | bytes 1769472 | tf_op jit(solution)/shard_map/all_to_all | solution.py:166
  72.8 2.0 select_reduce_fusion
  74.8 3.0 convolution_convert_fusion.6
  77.8 25.5 %all_to_all.49 = bf16[8,72,768]{2,1,0:T(8,128)(2,1)} all-to-all(bf16[8,72,768]{2,1,0:T(8,128)(2,1)S(1)} %bitcast.152), channel_id=1, replica_groups=mesh['exp'=8,'hid'=4] {'exp'}, dimensions={0} | all-to-all | bytes 1769472 | tf_op jit(solution)/shard_map/all_to_all | solution.py:222
  104.0 4.8 fusion.170
  108.8 8.2 fusion.14
  117.0 10.4 multiply_convert_fusion
  127.4 5.6 all-gather.9.cloned.1.call-done
  133.1 9.4 fusion.7
  142.5 1.8 fusion.30
  147.1 1.8 fusion.29
  150.2 1.8 fusion.28
  153.3 1.9 fusion.27
  156.6 3.5 fusion.34
  161.3 1.8 fusion.33
  164.3 1.8 fusion.32
  167.3 1.8 fusion.31
  170.4 36.8 %reduce-scatter.14.cloned.1.call-done = bf16[832,768]{1,0:T(8,128)(2,1)} async-done(((bf16[3328,768]{1,0:T(8,128)(2,1)}), bf16[832,768]{1,0:T(8,128)(2,1)}) %reduce-scatter.14.cloned.1.call-update) | async-done | bytes 1277968 | tf_op jit(solution)/shard_map/reduce_scatter | solution.py:237
  207.2 2.1 slice.110
  209.3 5.5 all-to-all-start.3
  214.8 45.3 %reduce-scatter.12.cloned.1.call-done = bf16[832,768]{1,0:T(8,128)(2,1)} async-done(((bf16[3328,768]{1,0:T(8,128)(2,1)}), bf16[832,768]{1,0:T(8,128)(2,1)}) %reduce-scatter.12.cloned.1.call-update) | async-done | bytes 1277968 | tf_op jit(solution)/shard_map/reduce_scatter | solution.py:175
  260.1 2.1 slice.108
  262.2 5.5 all-to-all-start.1
  268.0 2.7 fusion.137
  270.7 19.4 %all-to-all-done.1 = bf16[8,72,768]{2,1,0:T(8,128)(2,1)} async-done(((bf16[8,72,768]{2,1,0:T(8,128)(2,1)}), bf16[8,72,768]{2,1,0:T(8,128)(2,1)}, u32[]{:S(2)}, u32[]{:S(2)}) %all-to-all-start.1) | async-done | bytes 884768 | tf_op jit(solution)/shard_map/all_to_all | solution.py:194
  290.2 1.8 fusion.106
  292.0 3.9 fusion.99
  295.9 2.3 multiply_reduce_fusion.2
  300.1 1.9 fusion.142
  302.1 2.8 convolution_convert_fusion.12
  304.9 1.9 copy.50
  306.8 3.4 fusion.125
  310.2 7.1 fusion.54
  317.3 7.3 fusion.51
  324.6 2.8 fusion.50
  328.6 4.1 fusion.163
  338.3 4.2 fusion.95
  348.7 7.5 broadcast_multiply_fusion
  356.3 5.0 convolution_reduce_fusion.2
  363.7 6.1 reduce-scatter.22.cloned.1.call-done
  371.4 130.1 %reduce-scatter.20.cloned.1.call-done = f32[96,2304]{1,0:T(8,128)} async-done(((f32[768,2304]{1,0:T(8,128)}), f32[96,2304]{1,0:T(8,128)}) %reduce-scatter.20.cloned.1.call-update) | async-done | bytes 884752 | tf_op jit(solution)/shard_map/reduce_scatter | solution.py:333
  501.5 2.0 convert_element_type.196
  503.5 230.6 %reduce-scatter.18.cloned.1.call-done = f32[96,4608]{1,0:T(8,128)} async-done(((f32[768,4608]{1,0:T(8,128)}), f32[96,4608]{1,0:T(8,128)}) %reduce-scatter.18.cloned.1.call-update) | async-done | bytes 1769488 | tf_op jit(solution)/shard_map/reduce_scatter | solution.py:335
  734.1 2.5 convert_element_type.194
  736.6 4.7 fusion.171
  741.4 4.7 fusion.172
  746.4 7.5 convolution_bitcast_fusion
  753.9 1.9 broadcast_multiply_fusion.1
  755.9 7.5 convolution_bitcast_fusion.1
  768.3 40.1 %all-reduce = (f32[768]{0:T(1024)}, f32[4608]{0:T(1024)}, f32[8]{0:T(128)}) all-reduce(f32[768]{0:T(1024)S(1)} %get-tuple-element.50, f32[4608]{0:T(1024)} %reduce.46, f32[8]{0:T(128)} %get-tuple-element.34), channel_id=1, replica_groups=mesh['exp'=8,'hid'=4] {'exp','hid'}, use_global_device_ids=true, to_apply=%region_25.26 | all-reduce | flops 5384 | bytes 43072 | tf_op jit(solution)/shard_map/psum | solution.py:329
  809.7 2.5 fusion.94
  813.1 51.0 %reduce-scatter.16.cloned.1.call-done = f32[32,768]{1,0:T(8,128)} async-done(((f32[256,768]{1,0:T(8,128)}), f32[32,768]{1,0:T(8,128)}) %reduce-scatter.16.cloned.1.call-update) | async-done | bytes 98320 | tf_op jit(solution)/shard_map/reduce_scatter | solution.py:336
  865.6 12.8 %all-reduce.1 = (bf16[32,768]{1,0:T(8,128)(2,1)}, bf16[96,8]{0,1:T(8,128)(2,1)S(1)}) all-reduce(bf16[32,768]{1,0:T(8,128)(2,1)} %convert_element_type.192, bf16[96,8]{0,1:T(8,128)(2,1)S(1)} %copy.59), channel_id=1, replica_groups=mesh['exp'=8,'hid'=4] {'hid'}, use_global_device_ids=true, to_apply=%region_24.25 | all-reduce | flops 25344 | bytes 101376 | tf_op jit(solution)/shard_map/psum | solution.py:345
  880.4 27.9 %all-reduce.8.cloned.1.call-done = (bf16[96,4608]{1,0:T(8,128)(2,1)}, bf16[96,2304]{1,0:T(8,128)(2,1)}, bf16[96,768]{1,0:T(8,128)(2,1)}) async-done(((bf16[96,4608]{1,0:T(8,128)(2,1)}, bf16[96,2304]{1,0:T(8,128)(2,1)}, bf16[96,768]{1,0:T(8,128)(2,1)}), (bf16[96,4608]{1,0:T(8,128)(2,1)}, bf16[96,2304]{1,0:T(8,128)(2,1)}, bf16[96,768]{1,0:T(8,128)(2,1)})) %all-reduce.8.cloned.1.call-update) | async-done | bytes 1474576 | tf_op jit(solution)/shard_map/psum | solution.py:344
  910.0 2.5 convert_element_type.195
  913.5 69.1 %reduce-scatter.24.cloned.1.call-done = f32[96,768]{1,0:T(8,128)} async-done(((f32[768,768]{1,0:T(8,128)}), f32[96,768]{1,0:T(8,128)}) %reduce-scatter.24.cloned.1.call-update) | async-done | bytes 294928 | tf_op jit(solution)/shard_map/reduce_scatter | solution.py:338
  982.6 72.7 %reduce-scatter.26.cloned.1.call-done = f32[768,96]{0,1:T(8,128)} async-done(((f32[768,768]{0,1:T(8,128)}), f32[768,96]{0,1:T(8,128)}) %reduce-scatter.26.cloned.1.call-update) | async-done | bytes 294928 | tf_op jit(solution)/shard_map/reduce_scatter | solution.py:339
  1055.3 142.6 %all-reduce.6.cloned.1.call-done = f32[1001,768]{1,0:T(8,128)} async-done(((f32[1001,768]{1,0:T(8,128)}), f32[1001,768]{1,0:T(8,128)}) %all-reduce.6.cloned.1.call-update) | async-done | bytes 3075088 | tf_op jit(solution)/shard_map/psum | solution.py:329
  1197.9 3.7 copy.91
  (252 shorter events, 64.6 us)
Async XLA Ops:
  7.2 16.4 %copy-start = (bf16[768,2304]{1,0:T(8,128)(2,1)S(1)}, bf16[768,2304]{1,0:T(8,128)(2,1)}, u32[]{:S(2)}) copy-start(bf16[768,2304]{1,0:T(8,128)(2,1)} %param.29) | copy-start | bytes 10616836
  7.2 96.8 %all-gather.11.cloned.1.call-start = ((), (), s32[]{:S(2)}) async-start(), calls=%async_computation.17 | async-start | bytes 1966080 | tf_op jit(solution)/shard_map/all_gather | solution.py:225
  14.3 4.1 copy-start.33
  14.3 5.4 copy-start.13
  20.6 88.2 %all-gather.7.cloned.1.call-start = ((), (), s32[]{:S(2)}) async-start(), calls=%async_computation.14 | async-start | bytes 1966080 | tf_op jit(solution)/shard_map/all_gather | solution.py:169
  31.5 4.2 copy-start.19
  37.6 79.4 %all-gather.5.cloned.1.call-start = ((), (), s32[]{:S(2)}) async-start(), calls=%async_computation.13 | async-start | bytes 4423680 | tf_op jit(solution)/shard_map/all_gather | solution.py:168
  38.4 33.0 %copy-start.58 = (pred[256]{0:T(512)(128)(4,1)}, pred[256]{0:T(512)(128)(4,1)S(1)}, u32[]{:S(2)}) copy-start(pred[256]{0:T(512)(128)(4,1)S(1)} %get-tuple-element.35) | copy-start | bytes 772
  38.4 33.0 %copy-start.61 = (pred[256]{0:T(512)(128)(4,1)}, pred[256]{0:T(512)(128)(4,1)S(1)}, u32[]{:S(2)}) copy-start(pred[256]{0:T(512)(128)(4,1)S(1)} %get-tuple-element.36) | copy-start | bytes 772
  39.8 31.6 %copy-start.57 = (s32[256,1]{0,1:T(1,128)}, s32[256,1]{0,1:T(1,128)S(1)}, u32[]{:S(2)}) copy-start(s32[256,1]{0,1:T(1,128)S(1)} %get-tuple-element.60) | copy-start | bytes 3076
  39.8 31.6 %copy-start.60 = (s32[256,1]{0,1:T(1,128)}, s32[256,1]{0,1:T(1,128)S(1)}, u32[]{:S(2)}) copy-start(s32[256,1]{0,1:T(1,128)S(1)} %get-tuple-element.61) | copy-start | bytes 3076
  71.5 61.6 %all-gather.9.cloned.1.call-start = ((), (), s32[]{:S(2)}) async-start(), calls=%async_computation.16 | async-start | bytes 4423680 | tf_op jit(solution)/shard_map/all_gather | solution.py:224
  74.8 28.6 %copy-start.55 = (f32[256]{0:T(256)}, f32[256]{0:T(256)S(1)}, u32[]{:S(2)}) copy-start(f32[256]{0:T(256)S(1)} %get-tuple-element.54) | copy-start | bytes 3076
  74.8 28.6 %copy-start.59 = (f32[256]{0:T(256)}, f32[256]{0:T(256)S(1)}, u32[]{:S(2)}) copy-start(f32[256]{0:T(256)S(1)} %get-tuple-element.53) | copy-start | bytes 3076
  103.4 103.8 %reduce-scatter.14.cloned.1.call-start = ((), (), s32[]{:S(2)}) async-start(), calls=%async_computation.18 | async-start | bytes 6389760 | tf_op jit(solution)/shard_map/reduce_scatter | solution.py:237
  133.1 9.4 copy-start.62
  142.5 10.9 copy-start.68
  156.5 103.6 %reduce-scatter.12.cloned.1.call-start = ((), (), s32[]{:S(2)}) async-start(), calls=%async_computation.15 | async-start | bytes 6389760 | tf_op jit(solution)/shard_map/reduce_scatter | solution.py:175
  156.5 3.5 copy-start.65
  156.6 4.7 copy-start.64
  156.6 4.7 copy-start.69
  209.3 53.0 %all-to-all-start.3 = ((bf16[8,72,768]{2,1,0:T(8,128)(2,1)}), bf16[8,72,768]{2,1,0:T(8,128)(2,1)}, u32[]{:S(2)}, u32[]{:S(2)}) async-start(bf16[8,72,768]{2,1,0:T(8,128)(2,1)} %bitcast.146), calls=%async_computation.5 | async-start | bytes 1769472 | tf_op jit(solution)/shard_map/all_to_all | solution.py:256
  262.2 27.9 %all-to-all-start.1 = ((bf16[8,72,768]{2,1,0:T(8,128)(2,1)}), bf16[8,72,768]{2,1,0:T(8,128)(2,1)}, u32[]{:S(2)}, u32[]{:S(2)}) async-start(bf16[8,72,768]{2,1,0:T(8,128)(2,1)} %bitcast.145), calls=%async_computation.2 | async-start | bytes 1769472 | tf_op jit(solution)/shard_map/all_to_all | solution.py:194
  267.8 102.0 %reduce-scatter.22.cloned.1.call-start = ((), (), s32[]{:S(2)}) async-start(), calls=%async_computation.23 | async-start | bytes 2654208 | tf_op jit(solution)/shard_map/reduce_scatter | solution.py:334
  290.1 5.7 copy-start.56
  290.1 5.8 copy-start.3
  290.1 5.8 copy-start.15
  290.1 5.8 copy-start.20
  290.1 5.8 copy-start.32
  290.1 5.8 copy-start.37
  290.1 5.8 copy-start.39
  290.1 5.8 copy-start.51
  292.0 6.3 copy-start.12
  292.0 6.3 copy-start.14
  295.9 4.2 copy-start.11
  302.0 199.5 %reduce-scatter.20.cloned.1.call-start = ((), (), s32[]{:S(2)}) async-start(), calls=%async_computation.22 | async-start | bytes 7962624 | tf_op jit(solution)/shard_map/reduce_scatter | solution.py:333
  324.6 4.0 copy-start.6
  324.6 4.0 copy-start.29
  324.6 4.0 copy-start.35
  332.8 401.3 %reduce-scatter.18.cloned.1.call-start = ((), (), s32[]{:S(2)}) async-start(), calls=%async_computation.21 | async-start | bytes 15925248 | tf_op jit(solution)/shard_map/reduce_scatter | solution.py:335
  356.2 456.1 %reduce-scatter.28.cloned.1.call-start = ((), (), s32[]{:S(2)}) async-start(), calls=%async_computation.26 | async-start | bytes 442368
  356.2 5.1 copy-start.24
  356.3 5.1 copy-start.26
  356.3 5.1 copy-start.49
  356.3 5.1 copy-start.7
  356.3 5.1 copy-start.38
  356.3 5.1 copy-start.40
  356.3 5.1 copy-start.53
  356.3 6.2 copy-start.54
  362.5 501.6 %reduce-scatter.16.cloned.1.call-start = ((), (), s32[]{:S(2)}) async-start(), calls=%async_computation.19 | async-start | bytes 884736 | tf_op jit(solution)/shard_map/reduce_scatter | solution.py:336
  363.6 544.7 %all-reduce.8.cloned.1.call-start = ((), (), s32[]{:S(2)}) async-start(), calls=%async_computation.27 | async-start | bytes 2949120 | tf_op jit(solution)/shard_map/psum | solution.py:344
  736.6 246.0 %reduce-scatter.24.cloned.1.call-start = ((), (), s32[]{:S(2)}) async-start(), calls=%async_computation.24 | async-start | bytes 2654208 | tf_op jit(solution)/shard_map/reduce_scatter | solution.py:338
  741.4 313.9 %reduce-scatter.26.cloned.1.call-start = ((), (), s32[]{:S(2)}) async-start(), calls=%async_computation.25 | async-start | bytes 2654208 | tf_op jit(solution)/shard_map/reduce_scatter | solution.py:339
  746.2 7.7 copy-start.41
  746.2 451.7 %all-reduce.6.cloned.1.call-start = ((), (), s32[]{:S(2)}) async-start(), calls=%async_computation.20 | async-start | bytes 6193152 | tf_op jit(solution)/shard_map/psum | solution.py:329
  755.8 7.6 copy-start.48
  755.9 8.1 copy-start.46
  755.9 8.7 copy-start.27
  755.9 9.3 copy-start.22
  755.9 9.9 copy-start.21
  755.9 10.4 copy-start.44
  755.9 53.8 %copy-start.30 = (f32[256]{0:T(256)S(1)}, f32[256]{0:T(256)}, u32[]{:S(2)}) copy-start(f32[256]{0:T(256)} %copy-done.28) | copy-start | bytes 3076
  755.9 53.8 %copy-start.36 = (f32[256]{0:T(256)S(1)}, f32[256]{0:T(256)}, u32[]{:S(2)}) copy-start(f32[256]{0:T(256)} %copy-done.34) | copy-start | bytes 3076
  908.3 4.2 copy-start.16
  (23 other events, 43.2 us)
Sparse Core Ops, SparseCore 0:
  20.7 22.3 all-gather.10
  45.2 19.6 all-gather.6
  71.6 29.2 all-gather.4
  103.5 29.5 all-gather.8
  156.6 50.4 reduce-scatter.13
  209.6 50.4 reduce-scatter.11
  302.2 67.5 reduce-scatter.21
  373.4 128.0 reduce-scatter.19
  505.2 228.8 reduce-scatter.17
  737.2 61.2 reduce-scatter.27
  801.8 62.2 reduce-scatter.15
  867.7 40.6 all-reduce.7
  912.4 70.1 reduce-scatter.23
  986.5 68.7 reduce-scatter.25
  1061.2 136.6 all-reduce.5
where the time goes:
time: 1220 us; the launch traced here: 1210 us
  waiting for transfers between devices  837 us (69%)
  matrix products  156 us (13%)
  blocking collectives  108 us (9%)
  other arithmetic  49.2 us (4%)
  local copies, waits for them, and re-layouts  27.3 us (2%)
  between operations  16.6 us (1%)
  starting transfers between devices  13 us (1%)
    reduce_scatter x1, waiting for transfers between devices, per_device(): lax.psum_scatter(weight_ada, 'exp', scatter_dimension=0, tiled=True)  231 us
    psum x1, waiting for transfers between devices, per_device(): lax.psum((bias_time, bias_ada, table_grad, counts_local), ('exp', 'hid'))  143 us
    reduce_scatter x1, waiting for transfers between devices, per_device(): lax.psum_scatter(weight_qkv, 'exp', scatter_dimension=0, tiled=True)  130 us
    reduce_scatter x2, waiting for transfers between devices, per_device(): lax.psum_scatter(block_terms(jnp.int32(0), per_rows * lax.axis_size('hid'...  82.1 us
    reduce_scatter x1, waiting for transfers between devices, per_device(): lax.psum_scatter(weight_shared_out, 'exp', scatter_dimension=1, tiled=True)  72.7 us
    reduce_scatter x1, waiting for transfers between devices, per_device(): lax.psum_scatter(weight_shared_in, 'exp', scatter_dimension=0, tiled=True)  69.1 us
    dot_general x19, matrix products, mat_prod(): return jnp.dot(left_side, right_side, preferred_element_type=jnp.float32)  54.3 us
    reduce_scatter x1, waiting for transfers between devices, per_device(): lax.psum_scatter(weight_time, 'exp', scatter_dimension=0, tiled=True)  51 us
  transfers between devices with their start and end apart: 17, of which 12 were waited for; matrix products, arithmetic and copies ran while one was open for 15% of the time, Pallas kernels for 0%

commit v1 on v0

v1 whole, which is shorter than its diff:
```python
import math

import jax
import jax.numpy as jnp
from jax import lax
from jax.sharding import PartitionSpec as P

HEADS = 12
HDIM = 64
SEQ = 256


eps_norm = 1e-06
highest = lax.Precision.HIGHEST


def mat_prod(left_side, right_side):
    return jnp.dot(left_side, right_side, preferred_element_type=jnp.float32)


def prod_rows(left_side, right_side):
    return lax.dot_general(
        left_side, right_side, (((0,), (0,)), ((), ())), preferred_element_type=jnp.float32
    )


def prod_cols(left_side, right_side):
    return lax.dot_general(
        left_side, right_side, (((1,), (1,)), ((), ())), preferred_element_type=jnp.float32
    )


def sinus_table(timesteps, columns):
    half_cols = columns // 2
    freqs = jnp.exp(-math.log(10000.0) * jnp.arange(half_cols, dtype=jnp.float32) / half_cols)
    angles = timesteps.astype(jnp.float32)[:, None] * freqs[None, :]
    return jnp.concatenate([jnp.cos(angles), jnp.sin(angles)], axis=1)


def normalize(inputs):
    center = inputs - jnp.mean(inputs, axis=-1, keepdims=True)
    inverse = lax.rsqrt(jnp.mean(center * center, axis=-1, keepdims=True) + eps_norm)
    return (center * inverse, inverse)


def normalize_back(normed, inverse, grad_normed):
    return inverse * (
        grad_normed
        - jnp.mean(grad_normed, axis=-1, keepdims=True)
        - normed * jnp.mean(grad_normed * normed, axis=-1, keepdims=True)
    )


def gelu_back(pre_act, grad_act):
    return jax.vjp(jax.nn.gelu, pre_act)[1](grad_act)[0]


def attention_weights(queries, key_rows, score_scale):
    scores = (
        jnp.einsum("bqhd,bkhd->bhqk", queries, key_rows, preferred_element_type=jnp.float32)
        * score_scale
    )
    row_max = jnp.max(scores, axis=-1, keepdims=True)
    log_total = row_max + jnp.log(jnp.sum(jnp.exp(scores - row_max), axis=-1, keepdims=True))
    return jnp.exp(scores - log_total)


def pairs_of(size, mask):
    return [(index, index ^ mask) for index in range(size)]


def swap(values, axis, mask):
    return lax.ppermute(values, axis, pairs_of(lax.axis_size(axis), mask))


def low(values):
    return values.astype(jnp.bfloat16)


def bits_of(axis):
    masks = [1]
    while masks[-1] * 2 < lax.axis_size(axis):
        masks.append(masks[-1] * 2)
    return masks


def gather_hid(own):
    blocks = {0: own}
    for mask in reversed(bits_of("hid")):
        for index in list(blocks):
            blocks[index ^ mask] = swap(blocks[index], "hid", mask)
    return [blocks[index] for index in range(lax.axis_size("hid"))]


def reduce_hid(blocks):
    blocks = dict(enumerate(blocks))
    for mask in bits_of("hid"):
        moved = {
            index: swap(low(blocks[index | mask]), "hid", mask)
            for index in blocks
            if not index & mask
        }
        blocks = {
            index: blocks[index].astype(jnp.float32) + moved[index].astype(jnp.float32)
            for index in moved
        }
    return blocks[0]


def pick_bit(values, bit):
    return lax.dynamic_index_in_dim(values, bit, 1, keepdims=False)


def reduce_axis(values, axis):
    place = lax.axis_index(axis)
    for step, mask in enumerate(bits_of(axis)):
        bit = (place >> step) & 1
        halves = values.reshape((values.shape[0] // 2, 2) + values.shape[1:])
        moved = swap(low(pick_bit(halves, 1 - bit)), axis, mask)
        values = pick_bit(halves, bit).astype(jnp.float32) + moved.astype(jnp.float32)
    return values[0]


def small_exp():
    return lax.axis_size("exp") <= 8


def exchange(rows):
    size = lax.axis_size("exp")
    if not small_exp():
        return lax.all_to_all(rows, "exp", split_axis=0, concat_axis=0, tiled=True)
    per = rows.shape[0] // size
    chunks = [rows[index * per : (index + 1) * per] for index in range(size)]
    moved = [chunks[0]] + [swap(chunks[index], "exp", index) for index in range(1, size)]
    return jnp.concatenate(moved, axis=0)


def gather_items(own):
    size = lax.axis_size("exp")
    width = lax.axis_size("hid")
    if not small_exp():
        return lax.all_gather(own, ("exp", "hid"), axis=0, tiled=True)
    near = jnp.concatenate([own] + [swap(own, "hid", mask) for mask in range(1, width)], axis=0)
    rows = jnp.concatenate([near] + [swap(near, "exp", mask) for mask in range(1, size)], axis=0)
    count = own.shape[0]
    place = lax.axis_index("exp") * width + lax.axis_index("hid")
    target = jnp.arange(size * width * count, dtype=jnp.int32)
    source = (target // count ^ place) * count + target % count
    hot = source[:, None] == target[None, :]
    if own.dtype == jnp.bfloat16:
        return low(mat_prod(low(hot), rows))
    return jnp.sum(jnp.where(hot[:, :, None], rows[None, :, :], 0), axis=1)


def sum_all(partial, columns):
    size = lax.axis_size("exp")
    width = lax.axis_size("hid")
    share = partial.shape[0] // (size * width)
    values = partial.reshape(size, width, share, columns)
    place = lax.axis_index("hid")
    for step, mask in enumerate(bits_of("hid")):
        bit = (place >> step) & 1
        halves = values.reshape(size, values.shape[1] // 2, 2, share, columns)
        kept = lax.dynamic_index_in_dim(halves, bit, 2, keepdims=False)
        sent = lax.dynamic_index_in_dim(halves, 1 - bit, 2, keepdims=False)
        moved = swap(low(sent), "hid", mask)
        values = kept.astype(jnp.float32) + moved.astype(jnp.float32)
    mine = low(reduce_axis(values.reshape(size, share, columns), "exp"))
    for step, mask in enumerate(bits_of("hid")):
        bit = (place >> step) & 1
        other = swap(mine, "hid", mask)
        mine = jnp.where(
            bit == 0,
            jnp.concatenate([mine, other], axis=0),
            jnp.concatenate([other, mine], axis=0),
        )
    return mine.astype(jnp.float32)


def condition_of(timesteps, labels, time_weight, time_bias, class_table):
    freq_emb = low(sinus_table(timesteps, time_weight.shape[0]))
    label_hot = low(
        labels[:, None] == jnp.arange(class_table.shape[0], dtype=jnp.int32)[None, :]
    )
    condition = mat_prod(freq_emb, time_weight) + time_bias + mat_prod(label_hot, class_table)
    return freq_emb, label_hot, condition, low(jax.nn.silu(condition))


def per_device(
    patches,
    cotangent,
    timesteps,
    labels,
    routes,
    slot_index,
    time_weight,
    time_bias,
    class_table,
    ada_weight,
    ada_bias,
    qkv_weight,
    proj_weight,
    router_weight,
    shared_in,
    shared_out,
    expert_in,
    expert_out,
):
    tokens, model_dim = patches.shape
    item_count = timesteps.shape[0]
    experts = lax.axis_size("exp")
    place_exp = lax.axis_index("exp")
    capacity = 9 * tokens // (4 * experts)
    slots_all = experts * capacity
    score_scale = 1.0 / math.sqrt(HDIM)

    blocks_in = gather_hid(expert_in[0])
    blocks_out = gather_hid(expert_out[0])
    numbers = gather_items(jnp.stack([timesteps, labels], axis=1))

    freq_emb, label_hot, condition, silu_cond = condition_of(
        timesteps, labels, time_weight, time_bias, class_table
    )
    modulate = mat_prod(silu_cond, ada_weight) + ada_bias
    shift_one, scale_one, gate_one, shift_two, scale_two, gate_two = [
        modulate[:, None, block_index * model_dim : (block_index + 1) * model_dim]
        for block_index in range(6)
    ]
    grad_result = cotangent.astype(jnp.float32).reshape(item_count, SEQ, model_dim)
    grad_branch = (gate_two * grad_result).reshape(tokens, model_dim)
    grad_branch_low = low(grad_branch)

    first_route, second_route = routes[:, 0:1], routes[:, 1:2]
    kept_first = slot_index[:, 0:1] < capacity
    kept_second = slot_index[:, 1:2] < capacity
    slot_ids = jnp.arange(slots_all, dtype=jnp.int32)[None, :]
    first_chunk, second_chunk = first_route, second_route
    if small_exp():
        first_chunk, second_chunk = first_route ^ place_exp, second_route ^ place_exp
    dispatch_first = low(
        (first_chunk * capacity + slot_index[:, 0:1] == slot_ids) & kept_first
    )
    dispatch_second = low(
        (second_chunk * capacity + slot_index[:, 1:2] == slot_ids) & kept_second
    )
    dispatch_both = dispatch_first + dispatch_second
    picks = jnp.concatenate([dispatch_first, dispatch_second], axis=0)
    grad_rows = exchange(low(prod_rows(dispatch_both, grad_branch_low)))
    grad_tokens = jnp.concatenate(gather_hid(grad_branch_low), axis=0)

    residual = patches.astype(jnp.float32).reshape(item_count, SEQ, model_dim)
    normed_one, inverse_one = normalize(residual)
    flat_one = low(normed_one * (1.0 + scale_one) + shift_one).reshape(tokens, model_dim)
    qkv_rows = low(mat_prod(flat_one, qkv_weight)).reshape(item_count, SEQ, 3, HEADS, HDIM)
    queries, key_rows, value_rows = (qkv_rows[:, :, 0], qkv_rows[:, :, 1], qkv_rows[:, :, 2])
    attention = attention_weights(queries, key_rows, score_scale)
    attention_low = low(attention)
    attended = jnp.einsum(
        "bhqk,bkhd->bqhd", attention_low, value_rows, preferred_element_type=jnp.float32
    )
    attended_low = low(attended).reshape(tokens, model_dim)
    branch_one = mat_prod(attended_low, proj_weight).reshape(item_count, SEQ, model_dim)
    residual_one = residual + gate_one * branch_one
    normed_two, inverse_two = normalize(residual_one)
    hidden_two = low(normed_two * (1.0 + scale_two) + shift_two).reshape(tokens, model_dim)
    logits = mat_prod(hidden_two, router_weight)
    expert_ids = jnp.arange(experts, dtype=jnp.int32)[None, :]
    first_hot = (first_route == expert_ids).astype(jnp.float32)
    second_hot = (second_route == expert_ids).astype(jnp.float32)
    logit_gap = jnp.sum(logits * first_hot, axis=1) - jnp.sum(logits * second_hot, axis=1)
    gate_first = jax.nn.sigmoid(logit_gap)[:, None]
    gate_second = 1.0 - gate_first

    lane = jnp.arange(128, dtype=jnp.int32)[None, :]

    def gate_lanes(gate):
        high = low(gate).astype(jnp.float32)
        return low(jnp.where(lane == 0, high, jnp.where(lane == 1, gate - high, 0.0)))

    carried = jnp.concatenate(
        [
            jnp.concatenate([hidden_two, hidden_two], axis=0),
            jnp.concatenate([gate_lanes(gate_first), gate_lanes(gate_second)], axis=0),
        ],
        axis=1,
    )
    received = exchange(low(prod_rows(picks, carried)))
    tokens_all = jnp.concatenate(gather_hid(hidden_two), axis=0)
    rows = received[:, :model_dim]
    gate_rows = (
        received[:, model_dim : model_dim + 1].astype(jnp.float32)
        + received[:, model_dim + 1 : model_dim + 2].astype(jnp.float32)
    )

    pre_shared = mat_prod(tokens_all, shared_in)
    act_shared = low(jax.nn.gelu(pre_shared))
    grad_pre_shared = low(gelu_back(pre_shared, prod_cols(grad_tokens, shared_out)))

    def split(values):
        return [
            values[index * tokens : (index + 1) * tokens] for index in range(lax.axis_size("hid"))
        ]

    shared_term = reduce_hid(split(prod_cols(grad_pre_shared, shared_in)))
    shared_sum = reduce_hid(split(mat_prod(act_shared, shared_out)))

    pre_blocks = [mat_prod(rows, block) for block in blocks_in]
    act_blocks = [low(jax.nn.gelu(block)) for block in pre_blocks]
    expert_rows = low(
        sum(mat_prod(act, block) for act, block in zip(act_blocks, blocks_out))
    )
    back_rows = exchange(expert_rows)
    back_pre = [
        gelu_back(pre, prod_cols(grad_rows, block)) for pre, block in zip(pre_blocks, blocks_out)
    ]
    grad_sent = low(
        sum(prod_cols(low(back), block) for back, block in zip(back_pre, blocks_in))
    )
    grad_back = exchange(grad_sent)
    grad_gated = low(grad_rows.astype(jnp.float32) * gate_rows)
    weight_expert_in = reduce_hid(
        [prod_rows(rows, low(back * gate_rows)) for back in back_pre]
    )
    weight_expert_out = reduce_hid([prod_rows(act, grad_gated) for act in act_blocks])

    weight_shared = jnp.stack(
        [prod_rows(tokens_all, grad_pre_shared), prod_rows(grad_tokens, act_shared)], axis=0
    )
    share = model_dim // experts
    weight_shared = reduce_axis(
        jnp.moveaxis(weight_shared.reshape(2, experts, share, weight_shared.shape[2]), 1, 0), "exp"
    )

    picked = mat_prod(picks, back_rows)
    picked_first, picked_second = picked[:tokens], picked[tokens:]
    moe_out = gate_first * picked_first + gate_second * picked_second
    branch_two = (shared_sum + moe_out).reshape(item_count, SEQ, model_dim)
    output = low(residual_one + gate_two * branch_two).reshape(tokens, model_dim)
    grad_gate_two = jnp.sum(branch_two * grad_result, axis=1)
    grad_gap = (
        jnp.sum(grad_branch * (picked_first - picked_second), axis=1)
        * gate_first[:, 0]
        * gate_second[:, 0]
    )
    grad_logits = low(grad_gap[:, None] * (first_hot - second_hot))
    picked_grad = mat_prod(picks, grad_back)
    grad_hidden = (
        prod_cols(grad_logits, router_weight)
        + shared_term
        + gate_first * picked_grad[:tokens]
        + gate_second * picked_grad[tokens:]
    ).reshape(item_count, SEQ, model_dim)
    grad_shift_two = jnp.sum(grad_hidden, axis=1)
    grad_scale_two = jnp.sum(grad_hidden * normed_two, axis=1)
    grad_residual = grad_result + normalize_back(
        normed_two, inverse_two, grad_hidden * (1.0 + scale_two)
    )
    grad_gate_one = jnp.sum(branch_one * grad_residual, axis=1)
    grad_branch_one = low((gate_one * grad_residual).reshape(tokens, model_dim))
    dense_two = sum_all(
        jnp.concatenate(
            [prod_rows(attended_low, grad_branch_one), prod_rows(hidden_two, grad_logits)], axis=1
        ),
        model_dim + experts,
    )
    counts_local = jnp.sum(
        first_hot * kept_first.astype(jnp.float32) + second_hot * kept_second.astype(jnp.float32),
        axis=0,
    )
    counts_rows = jnp.zeros((item_count, experts), jnp.float32).at[0].set(counts_local)
    early = gather_items(
        low(
            jnp.concatenate(
                [grad_gate_one, grad_shift_two, grad_scale_two, grad_gate_two, counts_rows], axis=1
            )
        )
    )

    grad_attended = low(prod_cols(grad_branch_one, proj_weight)).reshape(
        item_count, SEQ, HEADS, HDIM
    )
    grad_values = jnp.einsum(
        "bhqk,bqhd->bkhd", attention_low, grad_attended, preferred_element_type=jnp.float32
    )
    grad_values = low(grad_values).reshape(tokens, model_dim)
    dense_values = sum_all(prod_rows(flat_one, grad_values), model_dim)
    grad_probs = jnp.einsum(
        "bqhd,bkhd->bhqk", grad_attended, value_rows, preferred_element_type=jnp.float32
    )
    grad_scores = attention * (grad_probs - jnp.sum(attention * grad_probs, axis=-1, keepdims=True))
    grad_scores_low = low(grad_scores * score_scale)
    grad_queries = jnp.einsum(
        "bhqk,bkhd->bqhd", grad_scores_low, key_rows, preferred_element_type=jnp.float32
    )
    grad_keys = jnp.einsum(
        "bhqk,bqhd->bkhd", grad_scores_low, queries, preferred_element_type=jnp.float32
    )
    grad_pair = jnp.concatenate(
        [
            low(grad_queries).reshape(tokens, model_dim),
            low(grad_keys).reshape(tokens, model_dim),
        ],
        axis=1,
    )
    dense_pair = sum_all(prod_rows(flat_one, grad_pair), 2 * model_dim)
    grad_hidden_one = (
        prod_cols(grad_pair, qkv_weight[:, : 2 * model_dim])
        + prod_cols(grad_values, qkv_weight[:, 2 * model_dim :])
    ).reshape(item_count, SEQ, model_dim)
    grad_shift_one = jnp.sum(grad_hidden_one, axis=1)
    grad_scale_one = jnp.sum(grad_hidden_one * normed_one, axis=1)
    grad_input = grad_residual + normalize_back(
        normed_one, inverse_one, grad_hidden_one * (1.0 + scale_one)
    )
    grad_patches = low(grad_input.reshape(tokens, model_dim))
    late = gather_items(low(jnp.concatenate([grad_shift_one, grad_scale_one], axis=1)))

    freq_all, label_all, condition_all, silu_all = condition_of(
        numbers[:, 0], numbers[:, 1], time_weight, time_bias, class_table
    )
    early_mod = early[:, : 4 * model_dim]
    expert_counts = jnp.sum(early[:, 4 * model_dim :].astype(jnp.float32), axis=0)
    silu_share = lax.dynamic_slice_in_dim(silu_all, place_exp * share, share, 1)
    weight_ada = jnp.concatenate(
        [prod_rows(silu_share, late), prod_rows(silu_share, early_mod)], axis=1
    )
    bias_ada = jnp.concatenate(
        [
            jnp.sum(late.astype(jnp.float32), axis=0),
            jnp.sum(early_mod.astype(jnp.float32), axis=0),
        ],
        axis=0,
    )
    grad_silu = prod_cols(early_mod, ada_weight[:, 2 * model_dim :]) + prod_cols(
        late, ada_weight[:, : 2 * model_dim]
    )
    grad_condition = jax.vjp(jax.nn.silu, condition_all)[1](grad_silu)[0]
    bias_time = jnp.sum(grad_condition, axis=0)
    grad_condition_low = low(grad_condition)
    table_grad = prod_rows(label_all, grad_condition_low)
    freq_share = time_weight.shape[0] // experts
    weight_time = prod_rows(
        lax.dynamic_slice_in_dim(freq_all, place_exp * freq_share, freq_share, 1),
        grad_condition_low,
    )
    return (
        output,
        grad_patches,
        weight_time,
        bias_time,
        table_grad,
        weight_ada,
        bias_ada,
        jnp.concatenate([dense_pair, dense_values], axis=1),
        dense_two[:, :model_dim],
        dense_two[:, model_dim:],
        weight_shared[0],
        weight_shared[1].T,
        weight_expert_in[None],
        weight_expert_out[None],
        expert_counts,
    )


def solution(mesh):
    placed = (
        P(("exp", "hid"), None),
        P(("exp", "hid"), None),
        P(("exp", "hid")),
        P(("exp", "hid")),
        P(("exp", "hid"), None),
        P(("exp", "hid"), None),
        P(),
        P(),
        P(),
        P(),
        P(),
        P(),
        P(),
        P(),
        P(None, "hid"),
        P("hid", None),
        P("exp", None, "hid"),
        P("exp", "hid", None),
    )
    return jax.shard_map(
        per_device,
        mesh=mesh,
        in_specs=placed,
        out_specs=(
            P(("exp", "hid"), None),
            P(("exp", "hid"), None),
            P("exp", None),
            P(),
            P(),
            P("exp", None),
            P(),
            P("exp", None),
            P("exp", None),
            P("exp", None),
            P("exp", "hid"),
            P("hid", "exp"),
            P("exp", None, "hid"),
            P("exp", "hid", None),
            P(),
        ),
        check_vma=False,
    )
```

time: 1220 us -> 526 us (0.43)
  waiting for transfers between devices: 837 us -> 220 us
  blocking collectives: 108 us -> 0 us
  starting transfers between devices: 13 us -> 115 us
  matrix products: 156 us -> 118 us
  other arithmetic: 49.2 us -> 33.1 us
    reduce_scatter x8 -> x0, waiting for transfers between devices: 642 us -> none  [the longest x1 231 us: per_device(): lax.psum_scatter(weight_ada, 'exp', scatter_dimension=0, tiled=True)]
    ppermute x0 -> x106, waiting for transfers between devices: none -> 220 us  [swap(): return lax.ppermute(values, axis, pairs_of(lax.axis_size(axis), mask))]
    psum x2 -> x0, waiting for transfers between devices: 171 us -> none  [the longest x1 143 us: per_device(): lax.psum((bias_time, bias_ada, table_grad, counts_local), ('exp', 'hid'))]
    ppermute x0 -> x106, starting transfers between devices: none -> 115 us  [swap(): return lax.ppermute(values, axis, pairs_of(lax.axis_size(axis), mask))]
    all_to_all x2 -> x0, blocking collectives: 55.5 us -> none  [the longest x1 30 us: per_device(): lax.all_to_all(send_rows, 'exp', split_axis=0, concat_axis=0, tiled=True)]
    psum x2 -> x0, blocking collectives: 52.9 us -> none  [the longest x1 40.1 us: per_device(): lax.psum((bias_time, bias_ada, table_grad, counts_local), ('exp', 'hid'))]
    dot_general x19 -> x22, matrix products: 54.3 us -> 29.8 us  [mat_prod(): return jnp.dot(left_side, right_side, preferred_element_type=jnp.float32)]
    all_to_all x2 -> x0, waiting for transfers between devices: 19.4 us -> none  [the longest x1 19.4 us: per_device(): lax.all_to_all(routed_out, 'exp', split_axis=0, concat_axis=0, tiled=True)]
  transfers between devices with their start and end apart: 17 -> 106, of which waited for: 12 -> 41; matrix products, arithmetic and copies ran while one was open for 15% -> 32% of each run, Pallas kernels for 0% -> 0%
where the time goes in v1:
time: 526 us; the launch traced here: 521 us
  waiting for transfers between devices  220 us (42%)
  matrix products  118 us (22%)
  starting transfers between devices  115 us (22%)
  other arithmetic  33.1 us (6%)
  local copies, waits for them, and re-layouts  31.1 us (6%)
    ppermute x106, waiting for transfers between devices, swap(): return lax.ppermute(values, axis, pairs_of(lax.axis_size(axis), mask))  220 us
    ppermute x106, starting transfers between devices, swap(): return lax.ppermute(values, axis, pairs_of(lax.axis_size(axis), mask))  115 us
    dot_general x20, matrix products, prod_rows(): lax.dot_general(left_side, right_side, (((0,), (0,)), ((), ())), preferre...  36.7 us
    dot_general x16, matrix products, prod_cols(): lax.dot_general(left_side, right_side, (((1,), (1,)), ((), ())), preferre...  33.7 us
    dot_general x22, matrix products, mat_prod(): return jnp.dot(left_side, right_side, preferred_element_type=jnp.float32)  29.8 us
    unnamed x246, local copies, waits for them, and re-layouts  11.3 us
  transfers between devices with their start and end apart: 106, of which 41 were waited for; matrix products, arithmetic and copies ran while one was open for 32% of the time, Pallas kernels for 0%

profile of v1, /device:TPU:0, one launch (start us, length us, event | category | flops | bytes accessed | tf_op | source)
XLA Modules:
  0.0 520.9 jit_solution(4674964824385682365)
XLA Ops:
  14.3 4.2 convolution_reduce_fusion
  37.9 3.4 collective-permute-start.55
  41.3 2.8 collective-permute-done.55
  44.1 2.5 collective-permute-start.54
  46.6 2.9 collective-permute-done.54
  49.5 5.4 %collective-permute-done.53 = s32[4,2]{0,1:T(2,128)S(1)} collective-permute-done((s32[4,2]{0,1:T(2,128)S(1)}, s32[4,2]{0,1:T(2,128)S(1)}, u32[]{:S(2)}, u32[]{:S(2)}) %collective-permute-start.53) | collective-permute-done | bytes 64 | tf_op jit(solution)/shard_map/ppermute | solution.py:73
  55.0 4.4 collective-permute-done.52
  60.4 3.4 collective-permute-done.51
  64.0 3.4 collective-permute-done.50
  78.4 3.1 collective-permute-start.9
  84.2 3.2 collective-permute-done.9
  94.2 4.8 collective-permute-done.12
  108.3 14.3 %collective-permute-done.15 = bf16[768,768]{1,0:T(8,128)(2,1)S(1)} collective-permute-done((bf16[768,768]{1,0:T(8,128)(2,1)S(1)}, bf16[768,768]{1,0:T(8,128)(2,1)S(1)}, u32[]{:S(2)}, u32[]{:S(2)}) %collective-permute-start.15) | collective-permute-done | bytes 1179680 | tf_op jit(solution)/shard_map/ppermute | solution.py:73
  135.3 4.2 collective-permute-start.25
  139.6 7.6 %collective-permute-done.20 = bf16[72,768]{1,0:T(8,128)(2,1)S(1)} collective-permute-done((bf16[72,768]{1,0:T(8,128)(2,1)S(1)}, bf16[72,768]{1,0:T(8,128)(2,1)S(1)}, u32[]{:S(2)}, u32[]{:S(2)}) %collective-permute-start.20) | collective-permute-done | bytes 110624 | tf_op jit(solution)/shard_map/ppermute | solution.py:73
  148.8 4.1 collective-permute-done.21
  154.8 5.5 %collective-permute-done.22 = bf16[72,768]{1,0:T(8,128)(2,1)S(1)} collective-permute-done((bf16[72,768]{1,0:T(8,128)(2,1)S(1)}, bf16[72,768]{1,0:T(8,128)(2,1)S(1)}, u32[]{:S(2)}, u32[]{:S(2)}) %collective-permute-start.22) | collective-permute-done | bytes 110624 | tf_op jit(solution)/shard_map/ppermute | solution.py:73
  161.2 6.6 %collective-permute-done.23 = bf16[72,768]{1,0:T(8,128)(2,1)S(1)} collective-permute-done((bf16[72,768]{1,0:T(8,128)(2,1)S(1)}, bf16[72,768]{1,0:T(8,128)(2,1)S(1)}, u32[]{:S(2)}, u32[]{:S(2)}) %collective-permute-start.23) | collective-permute-done | bytes 110624 | tf_op jit(solution)/shard_map/ppermute | solution.py:73
  176.8 8.2 %collective-permute-done.33 = bf16[72,768]{1,0:T(8,128)(2,1)S(1)} collective-permute-done((bf16[72,768]{1,0:T(8,128)(2,1)S(1)}, bf16[72,768]{1,0:T(8,128)(2,1)S(1)}, u32[]{:S(2)}, u32[]{:S(2)}) %collective-permute-start.33) | collective-permute-done | bytes 110624 | tf_op jit(solution)/shard_map/ppermute | solution.py:73
  186.1 4.7 collective-permute-done.34
  191.8 6.4 %collective-permute-done.35 = bf16[72,768]{1,0:T(8,128)(2,1)S(1)} collective-permute-done((bf16[72,768]{1,0:T(8,128)(2,1)S(1)}, bf16[72,768]{1,0:T(8,128)(2,1)S(1)}, u32[]{:S(2)}, u32[]{:S(2)}) %collective-permute-start.35) | collective-permute-done | bytes 110624 | tf_op jit(solution)/shard_map/ppermute | solution.py:73
  198.2 7.7 %collective-permute-done.36 = bf16[72,768]{1,0:T(8,128)(2,1)S(1)} collective-permute-done((bf16[72,768]{1,0:T(8,128)(2,1)S(1)}, bf16[72,768]{1,0:T(8,128)(2,1)S(1)}, u32[]{:S(2)}, u32[]{:S(2)}) %collective-permute-start.36) | collective-permute-done | bytes 110624 | tf_op jit(solution)/shard_map/ppermute | solution.py:73
  205.9 2.5 convolution_convert_fusion.4
  211.7 3.0 fusion.218
  216.9 2.9 convolution_convert_fusion.6
  233.2 2.6 fusion.81
  236.9 4.7 collective-permute-done.40
  242.3 4.9 collective-permute-done.41
  247.3 8.3 %collective-permute-done.42 = bf16[72,768]{1,0:T(8,128)(2,1)S(1)} collective-permute-done((bf16[72,768]{1,0:T(8,128)(2,1)S(1)}, bf16[72,768]{1,0:T(8,128)(2,1)S(1)}, u32[]{:S(2)}, u32[]{:S(2)}) %collective-permute-start.42) | collective-permute-done | bytes 110624 | tf_op jit(solution)/shard_map/ppermute | solution.py:73
  256.1 8.2 %collective-permute-done.43 = bf16[72,768]{1,0:T(8,128)(2,1)S(1)} collective-permute-done((bf16[72,768]{1,0:T(8,128)(2,1)S(1)}, bf16[72,768]{1,0:T(8,128)(2,1)S(1)}, u32[]{:S(2)}, u32[]{:S(2)}) %collective-permute-start.43) | collective-permute-done | bytes 110624 | tf_op jit(solution)/shard_map/ppermute | solution.py:73
  266.5 4.3 collective-permute-done.44
  270.9 2.7 collective-permute-start.45
  273.6 4.7 collective-permute-done.45
  279.1 4.5 fusion.9
  293.3 2.9 add_convert_fusion.1
  296.2 2.5 add_convert_fusion
  298.7 4.0 collective-permute-done.31
  310.5 2.8 fusion.150
  315.2 2.5 convolution_convert_fusion.9
  317.7 3.3 fusion.121
  321.0 5.4 %fusion.53 = bf16[12,64,256]{2,1,0:T(8,128)(2,1)} fusion(f32[12,256,256]{1,2,0:T(8,128)} %fusion.121, f32[12,256]{1,0:T(8,128)S(1)} %log_add_fusion, f32[12,256,256]{1,2,0:T(8,128)S(1)} %copy-done.3, bf16[1,256,3,12,64]{1,4,3,2,0:T(8,128)(2,1)} %bitcast.239), kind=kOutput, calls=%fused_computation.96 | convolution fusion | flops 107941120 | bytes 13402112 | tf_op jit(solution)/shard_map/bhqk,bkhd->bqhd/dot_general | solution.py:392
  326.4 5.2 %fusion.56 = bf16[12,64,256]{2,1,0:T(8,128)(2,1)} fusion(f32[12,256,256]{1,2,0:T(8,128)} %fusion.121, f32[12,256]{1,0:T(8,128)S(1)} %log_add_fusion, f32[12,256,256]{1,2,0:T(8,128)S(1)} %copy-done.3, bf16[1,256,3,12,64]{1,4,3,2,0:T(8,128)(2,1)} %bitcast.240), kind=kOutput, calls=%fused_computation.97 | convolution fusion | flops 107941120 | bytes 13402112 | tf_op jit(solution)/shard_map/bhqk,bqhd->bkhd/dot_general | solution.py:395
  334.1 2.6 fusion.50
  352.5 2.7 collective-permute-start.75
  358.3 2.8 collective-permute-start.72
  361.6 2.6 collective-permute-start.70
  365.5 2.7 collective-permute-start.65
  370.4 2.8 collective-permute-start.62
  374.0 2.7 collective-permute-start.60
  382.8 3.3 concatenate.179
  387.1 3.9 fusion.1
  392.3 3.2 fusion.240
  401.3 6.0 %collective-permute-done.97 = bf16[4,2,96,768]{3,2,1,0:T(8,128)(2,1)} collective-permute-done((bf16[4,2,96,768]{3,2,1,0:T(8,128)(2,1)}, bf16[4,2,96,768]{3,2,1,0:T(8,128)(2,1)}, u32[]{:S(2)}, u32[]{:S(2)}) %collective-permute-start.97) | collective-permute-done | bytes 1179680 | tf_op jit(solution)/shard_map/ppermute | solution.py:73
  412.8 31.1 %collective-permute-done.84 = bf16[8,1,24,768]{3,2,1,0:T(8,128)(2,1)S(1)} collective-permute-done((bf16[8,1,24,768]{3,2,1,0:T(8,128)(2,1)S(1)}, bf16[8,1,24,768]{3,2,1,0:T(8,128)(2,1)S(1)}, u32[]{:S(2)}, u32[]{:S(2)}) %collective-permute-start.84) | collective-permute-done | bytes 294944 | tf_op jit(solution)/shard_map/ppermute | solution.py:73
  445.6 7.9 %collective-permute-done.91 = bf16[8,1,24,776]{3,2,1,0:T(8,128)(2,1)S(1)} collective-permute-done((bf16[8,1,24,776]{3,2,1,0:T(8,128)(2,1)S(1)}, bf16[8,1,24,776]{3,2,1,0:T(8,128)(2,1)S(1)}, u32[]{:S(2)}, u32[]{:S(2)}) %collective-permute-start.91) | collective-permute-done | bytes 298016 | tf_op jit(solution)/shard_map/ppermute | solution.py:73
  455.3 3.6 add_bitcast_fusion
  459.4 3.1 add_bitcast_fusion.1
  462.5 6.9 %collective-permute-done.98 = bf16[2,2,96,768]{3,2,1,0:T(8,128)(2,1)S(1)} collective-permute-done((bf16[2,2,96,768]{3,2,1,0:T(8,128)(2,1)S(1)}, bf16[2,2,96,768]{3,2,1,0:T(8,128)(2,1)S(1)}, u32[]{:S(2)}, u32[]{:S(2)}) %collective-permute-start.98) | collective-permute-done | bytes 589856 | tf_op jit(solution)/shard_map/ppermute | solution.py:73
  473.0 6.5 %collective-permute-done.86 = bf16[2,24,768]{2,1,0:T(8,128)(2,1)S(1)} collective-permute-done((bf16[2,24,768]{2,1,0:T(8,128)(2,1)S(1)}, bf16[2,24,768]{2,1,0:T(8,128)(2,1)S(1)}, u32[]{:S(2)}, u32[]{:S(2)}) %collective-permute-start.86) | collective-permute-done | bytes 73760 | tf_op jit(solution)/shard_map/ppermute | solution.py:73
  481.8 2.6 collective-permute-start.87
  487.2 6.2 %collective-permute-done.77 = bf16[8,1,24,1536]{3,2,1,0:T(8,128)(2,1)S(1)} collective-permute-done((bf16[8,1,24,1536]{3,2,1,0:T(8,128)(2,1)S(1)}, bf16[8,1,24,1536]{3,2,1,0:T(8,128)(2,1)S(1)}, u32[]{:S(2)}, u32[]{:S(2)}) %collective-permute-start.77) | collective-permute-done | bytes 589856 | tf_op jit(solution)/shard_map/ppermute | solution.py:73
  496.4 4.0 collective-permute-done.78
  500.4 2.5 collective-permute-start.79
  516.2 3.4 collective-permute-done.82
  (587 shorter events, 208.6 us)
Async XLA Ops:
  2.7 32.3 %collective-permute-start.48 = (s32[1,2]{0,1:T(2,128)}, s32[1,2]{0,1:T(2,128)}, u32[]{:S(2)}, u32[]{:S(2)}) collective-permute-start(s32[1,2]{0,1:T(2,128)} %pad_add_fusion), channel_id=1, source_target_pairs={{0,3},{1,2},{2,1},{3,0},{4,7},{5,6},{6,5},{7,4},{8,11},{9,10},{10,... | collective-permute-start | bytes 32 | tf_op jit(solution)/shard_map/ppermute | solution.py:73
  5.1 30.5 %collective-permute-start.47 = (s32[1,2]{0,1:T(2,128)}, s32[1,2]{0,1:T(2,128)}, u32[]{:S(2)}, u32[]{:S(2)}) collective-permute-start(s32[1,2]{0,1:T(2,128)} %pad_add_fusion), channel_id=1, source_target_pairs={{0,2},{1,3},{2,0},{3,1},{4,6},{5,7},{6,4},{7,5},{8,10},{9,11},{10,... | collective-permute-start | bytes 32 | tf_op jit(solution)/shard_map/ppermute | solution.py:73
  5.6 31.5 %collective-permute-start.46 = (s32[1,2]{0,1:T(2,128)}, s32[1,2]{0,1:T(2,128)}, u32[]{:S(2)}, u32[]{:S(2)}) collective-permute-start(s32[1,2]{0,1:T(2,128)} %pad_add_fusion), channel_id=1, source_target_pairs={{0,1},{1,0},{2,3},{3,2},{4,5},{5,4},{6,7},{7,6},{8,9},{9,8},{10,11... | collective-permute-start | bytes 32 | tf_op jit(solution)/shard_map/ppermute | solution.py:73
  5.7 122.2 %collective-permute-start.14 = (bf16[768,768]{1,0:T(8,128)(2,1)}, bf16[768,768]{1,0:T(8,128)(2,1)}, u32[]{:S(2)}, u32[]{:S(2)}) collective-permute-start(bf16[768,768]{1,0:T(8,128)(2,1)} %bitcast.277), channel_id=1, source_target_pairs={{0,1},{1,0},{2,3},{3,2},{4,5},{5,4},{6,7},{7,6},{8,9},{9,8},{10,11... | collective-permute-start | bytes 3538952 | tf_op jit(solution)/shard_map/ppermute | solution.py:73
  6.1 117.4 %collective-permute-start.16 = (bf16[768,768]{1,0:T(8,128)(2,1)}, bf16[768,768]{1,0:T(8,128)(2,1)}, u32[]{:S(2)}, u32[]{:S(2)}) collective-permute-start(bf16[768,768]{1,0:T(8,128)(2,1)} %bitcast.278), channel_id=1, source_target_pairs={{0,2},{1,3},{2,0},{3,1},{4,6},{5,7},{6,4},{7,5},{8,10},{9,11},{10,... | collective-permute-start | bytes 3538952 | tf_op jit(solution)/shard_map/ppermute | solution.py:73
  35.0 66.4 %collective-permute-start.1 = (bf16[256,768]{1,0:T(8,128)(2,1)S(1)}, bf16[256,768]{1,0:T(8,128)(2,1)}, u32[]{:S(2)}, u32[]{:S(2)}) collective-permute-start(bf16[256,768]{1,0:T(8,128)(2,1)S(1)} %add_convert_fusion.5), channel_id=1, source_target_pairs={{0,2},{1,3},{2,0},{3,1},{4,6},{5,7},{6,4},{7,5},{8,10},{9,11},{10,... | collective-permute-start | bytes 1179656 | tf_op jit(solution)/shard_map/ppermute | solution.py:73
  35.5 42.8 %collective-permute-start.7 = (bf16[72,896]{1,0:T(8,128)(2,1)}, bf16[72,896]{1,0:T(8,128)(2,1)}, u32[]{:S(2)}, u32[]{:S(2)}) collective-permute-start(bf16[72,896]{1,0:T(8,128)(2,1)} %get-tuple-element.140), channel_id=1, source_target_pairs={{0,8},{4,12},{8,0},{12,4},{16,24},{20,28},{24,16},{28,20},{1,9},{5... | collective-permute-start | bytes 387080 | tf_op jit(solution)/shard_map/ppermute | solution.py:73
  78.4 9.0 %collective-permute-start.9 = (bf16[72,896]{1,0:T(8,128)(2,1)S(1)}, bf16[72,896]{1,0:T(8,128)(2,1)S(1)}, u32[]{:S(2)}, u32[]{:S(2)}) collective-permute-start(bf16[72,896]{1,0:T(8,128)(2,1)S(1)} %copy-done.43), channel_id=1, source_target_pairs={{0,16},{4,20},{8,24},{12,28},{16,0},{20,4},{24,8},{28,12},{1,17},{... | collective-permute-start | bytes 387080 | tf_op jit(solution)/shard_map/ppermute | solution.py:73
  83.1 8.1 %collective-permute-start.10 = (bf16[72,896]{1,0:T(8,128)(2,1)S(1)}, bf16[72,896]{1,0:T(8,128)(2,1)S(1)}, u32[]{:S(2)}, u32[]{:S(2)}) collective-permute-start(bf16[72,896]{1,0:T(8,128)(2,1)S(1)} %copy-done.42), channel_id=1, source_target_pairs={{0,20},{4,16},{8,28},{12,24},{16,4},{20,0},{24,12},{28,8},{1,21},{... | collective-permute-start | bytes 387080 | tf_op jit(solution)/shard_map/ppermute | solution.py:73
  94.1 9.1 %collective-permute-start = (bf16[256,768]{1,0:T(8,128)(2,1)S(1)}, bf16[256,768]{1,0:T(8,128)(2,1)S(1)}, u32[]{:S(2)}, u32[]{:S(2)}) collective-permute-start(bf16[256,768]{1,0:T(8,128)(2,1)S(1)} %add_convert_fusion.5), channel_id=1, source_target_pairs={{0,1},{1,0},{2,3},{3,2},{4,5},{5,4},{6,7},{7,6},{8,9},{9,8},{10,11... | collective-permute-start | bytes 1179656 | tf_op jit(solution)/shard_map/ppermute | solution.py:73
  98.9 23.7 %collective-permute-start.15 = (bf16[768,768]{1,0:T(8,128)(2,1)S(1)}, bf16[768,768]{1,0:T(8,128)(2,1)S(1)}, u32[]{:S(2)}, u32[]{:S(2)}) collective-permute-start(bf16[768,768]{1,0:T(8,128)(2,1)S(1)} %bitcast.259), channel_id=1, source_target_pairs={{0,2},{1,3},{2,0},{3,1},{4,6},{5,7},{6,4},{7,5},{8,10},{9,11},{10,... | collective-permute-start | bytes 3538952 | tf_op jit(solution)/shard_map/ppermute | solution.py:73
  103.2 20.9 %collective-permute-start.13 = (bf16[768,768]{1,0:T(8,128)(2,1)S(1)}, bf16[768,768]{1,0:T(8,128)(2,1)S(1)}, u32[]{:S(2)}, u32[]{:S(2)}) collective-permute-start(bf16[768,768]{1,0:T(8,128)(2,1)S(1)} %bitcast.260), channel_id=1, source_target_pairs={{0,1},{1,0},{2,3},{3,2},{4,5},{5,4},{6,7},{7,6},{8,9},{9,8},{10,11... | collective-permute-start | bytes 3538952 | tf_op jit(solution)/shard_map/ppermute | solution.py:73
  108.0 60.7 %collective-permute-start.3 = (bf16[256,768]{1,0:T(8,128)(2,1)S(1)}, bf16[256,768]{1,0:T(8,128)(2,1)S(1)}, u32[]{:S(2)}, u32[]{:S(2)}) collective-permute-start(bf16[256,768]{1,0:T(8,128)(2,1)S(1)} %get-tuple-element.133), channel_id=1, source_target_pairs={{0,1},{1,0},{2,3},{3,2},{4,5},{5,4},{6,7},{7,6},{8,9},{9,8},{10,11... | collective-permute-start | bytes 1179656 | tf_op jit(solution)/shard_map/ppermute | solution.py:73
  122.6 7.8 %collective-permute-start.17 = (bf16[768,768]{1,0:T(8,128)(2,1)S(1)}, bf16[768,768]{1,0:T(8,128)(2,1)S(1)}, u32[]{:S(2)}, u32[]{:S(2)}) collective-permute-start(bf16[768,768]{1,0:T(8,128)(2,1)S(1)} %collective-permute-done.15), channel_id=1, source_target_pairs={{0,1},{1,0},{2,3},{3,2},{4,5},{5,4},{6,7},{7,6},{8,9},{9,8},{10,11... | collective-permute-start | bytes 3538952 | tf_op jit(solution)/shard_map/ppermute | solution.py:73
  123.5 10.2 %collective-permute-start.4 = (bf16[256,768]{1,0:T(8,128)(2,1)S(1)}, bf16[256,768]{1,0:T(8,128)(2,1)S(1)}, u32[]{:S(2)}, u32[]{:S(2)}) collective-permute-start(bf16[256,768]{1,0:T(8,128)(2,1)S(1)} %get-tuple-element.134), channel_id=1, source_target_pairs={{0,1},{1,0},{2,3},{3,2},{4,5},{5,4},{6,7},{7,6},{8,9},{9,8},{10,11... | collective-permute-start | bytes 1179656 | tf_op jit(solution)/shard_map/ppermute | solution.py:73
  133.7 34.9 %collective-permute-start.5 = (bf16[256,768]{1,0:T(8,128)(2,1)S(1)}, bf16[256,768]{1,0:T(8,128)(2,1)S(1)}, u32[]{:S(2)}, u32[]{:S(2)}) collective-permute-start(bf16[256,768]{1,0:T(8,128)(2,1)S(1)} %fusion.109), channel_id=1, source_target_pairs={{0,2},{1,3},{2,0},{3,1},{4,6},{5,7},{6,4},{7,5},{8,10},{9,11},{10,... | collective-permute-start | bytes 1179656 | tf_op jit(solution)/shard_map/ppermute | solution.py:73
  135.3 32.5 %collective-permute-start.25 = (bf16[72,768]{1,0:T(8,128)(2,1)S(1)}, bf16[72,768]{1,0:T(8,128)(2,1)S(1)}, u32[]{:S(2)}, u32[]{:S(2)}) collective-permute-start(bf16[72,768]{1,0:T(8,128)(2,1)S(1)} %get-tuple-element.159), channel_id=1, source_target_pairs={{0,28},{4,24},{8,20},{12,16},{16,12},{20,8},{24,4},{28,0},{1,29},{... | collective-permute-start | bytes 331784 | tf_op jit(solution)/shard_map/ppermute | solution.py:73
  139.5 28.3 %collective-permute-start.24 = (bf16[72,768]{1,0:T(8,128)(2,1)S(1)}, bf16[72,768]{1,0:T(8,128)(2,1)S(1)}, u32[]{:S(2)}, u32[]{:S(2)}) collective-permute-start(bf16[72,768]{1,0:T(8,128)(2,1)S(1)} %get-tuple-element.160), channel_id=1, source_target_pairs={{0,24},{4,28},{8,16},{12,20},{16,8},{20,12},{24,0},{28,4},{1,25},{... | collective-permute-start | bytes 331784 | tf_op jit(solution)/shard_map/ppermute | solution.py:73
  169.4 104.1 %collective-permute-start.27 = (bf16[256,768]{1,0:T(8,128)(2,1)S(1)}, bf16[256,768]{1,0:T(8,128)(2,1)S(1)}, u32[]{:S(2)}, u32[]{:S(2)}) collective-permute-start(bf16[256,768]{1,0:T(8,128)(2,1)S(1)} %get-tuple-element.171), channel_id=1, source_target_pairs={{0,2},{1,3},{2,0},{3,1},{4,6},{5,7},{6,4},{7,5},{8,10},{9,11},{10,... | collective-permute-start | bytes 1179656 | tf_op jit(solution)/shard_map/ppermute | solution.py:73
  169.8 109.3 %collective-permute-start.26 = (bf16[256,768]{1,0:T(8,128)(2,1)S(1)}, bf16[256,768]{1,0:T(8,128)(2,1)S(1)}, u32[]{:S(2)}, u32[]{:S(2)}) collective-permute-start(bf16[256,768]{1,0:T(8,128)(2,1)S(1)} %get-tuple-element.171), channel_id=1, source_target_pairs={{0,1},{1,0},{2,3},{3,2},{4,5},{5,4},{6,7},{7,6},{8,9},{9,8},{10,11... | collective-permute-start | bytes 1179656 | tf_op jit(solution)/shard_map/ppermute | solution.py:73
  173.4 32.5 %collective-permute-start.38 = (bf16[72,768]{1,0:T(8,128)(2,1)S(1)}, bf16[72,768]{1,0:T(8,128)(2,1)S(1)}, u32[]{:S(2)}, u32[]{:S(2)}) collective-permute-start(bf16[72,768]{1,0:T(8,128)(2,1)S(1)} %get-tuple-element.151), channel_id=1, source_target_pairs={{0,28},{4,24},{8,20},{12,16},{16,12},{20,8},{24,4},{28,0},{1,29},{... | collective-permute-start | bytes 331784 | tf_op jit(solution)/shard_map/ppermute | solution.py:73
  175.5 30.4 %collective-permute-start.37 = (bf16[72,768]{1,0:T(8,128)(2,1)S(1)}, bf16[72,768]{1,0:T(8,128)(2,1)S(1)}, u32[]{:S(2)}, u32[]{:S(2)}) collective-permute-start(bf16[72,768]{1,0:T(8,128)(2,1)S(1)} %get-tuple-element.152), channel_id=1, source_target_pairs={{0,24},{4,28},{8,16},{12,20},{16,8},{20,12},{24,0},{28,4},{1,25},{... | collective-permute-start | bytes 331784 | tf_op jit(solution)/shard_map/ppermute | solution.py:73
  176.7 8.2 %collective-permute-start.33 = (bf16[72,768]{1,0:T(8,128)(2,1)S(1)}, bf16[72,768]{1,0:T(8,128)(2,1)S(1)}, u32[]{:S(2)}, u32[]{:S(2)}) collective-permute-start(bf16[72,768]{1,0:T(8,128)(2,1)S(1)} %get-tuple-element.156), channel_id=1, source_target_pairs={{0,8},{4,12},{8,0},{12,4},{16,24},{20,28},{24,16},{28,20},{1,9},{5... | collective-permute-start | bytes 331784 | tf_op jit(solution)/shard_map/ppermute | solution.py:73
  235.8 60.4 %collective-permute-start.104 = (bf16[768,768]{1,0:T(8,128)(2,1)S(1)}, bf16[768,768]{1,0:T(8,128)(2,1)S(1)}, u32[]{:S(2)}, u32[]{:S(2)}) collective-permute-start(bf16[768,768]{1,0:T(8,128)(2,1)S(1)} %convolution_convert_fusion.3), channel_id=1, source_target_pairs={{0,1},{1,0},{2,3},{3,2},{4,5},{5,4},{6,7},{7,6},{8,9},{9,8},{10,11... | collective-permute-start | bytes 3538952 | tf_op jit(solution)/shard_map/ppermute | solution.py:73
  235.8 57.5 %collective-permute-start.101 = (bf16[768,768]{1,0:T(8,128)(2,1)S(1)}, bf16[768,768]{1,0:T(8,128)(2,1)S(1)}, u32[]{:S(2)}, u32[]{:S(2)}) collective-permute-start(bf16[768,768]{1,0:T(8,128)(2,1)S(1)} %convolution_convert_fusion.5), channel_id=1, source_target_pairs={{0,1},{1,0},{2,3},{3,2},{4,5},{5,4},{6,7},{7,6},{8,9},{9,8},{10,11... | collective-permute-start | bytes 3538952 | tf_op jit(solution)/shard_map/ppermute | solution.py:73
  247.2 8.3 %collective-permute-start.42 = (bf16[72,768]{1,0:T(8,128)(2,1)S(1)}, bf16[72,768]{1,0:T(8,128)(2,1)S(1)}, u32[]{:S(2)}, u32[]{:S(2)}) collective-permute-start(bf16[72,768]{1,0:T(8,128)(2,1)S(1)} %get-tuple-element.146), channel_id=1, source_target_pairs={{0,16},{4,20},{8,24},{12,28},{16,0},{20,4},{24,8},{28,12},{1,17},{... | collective-permute-start | bytes 331784 | tf_op jit(solution)/shard_map/ppermute | solution.py:73
  255.6 8.7 %collective-permute-start.43 = (bf16[72,768]{1,0:T(8,128)(2,1)S(1)}, bf16[72,768]{1,0:T(8,128)(2,1)S(1)}, u32[]{:S(2)}, u32[]{:S(2)}) collective-permute-start(bf16[72,768]{1,0:T(8,128)(2,1)S(1)} %get-tuple-element.145), channel_id=1, source_target_pairs={{0,20},{4,16},{8,28},{12,24},{16,4},{20,0},{24,12},{28,8},{1,21},{... | collective-permute-start | bytes 331784 | tf_op jit(solution)/shard_map/ppermute | solution.py:73
  285.1 13.6 %collective-permute-start.29 = (bf16[256,768]{1,0:T(8,128)(2,1)S(1)}, bf16[256,768]{1,0:T(8,128)(2,1)S(1)}, u32[]{:S(2)}, u32[]{:S(2)}) collective-permute-start(bf16[256,768]{1,0:T(8,128)(2,1)S(1)} %get-tuple-element.131), channel_id=1, source_target_pairs={{0,1},{1,0},{2,3},{3,2},{4,5},{5,4},{6,7},{7,6},{8,9},{9,8},{10,11... | collective-permute-start | bytes 1179656 | tf_op jit(solution)/shard_map/ppermute | solution.py:73
  291.6 11.2 %collective-permute-start.31 = (bf16[256,768]{1,0:T(8,128)(2,1)S(1)}, bf16[256,768]{1,0:T(8,128)(2,1)S(1)}, u32[]{:S(2)}, u32[]{:S(2)}) collective-permute-start(bf16[256,768]{1,0:T(8,128)(2,1)S(1)} %fusion.106), channel_id=1, source_target_pairs={{0,2},{1,3},{2,0},{3,1},{4,6},{5,7},{6,4},{7,5},{8,10},{9,11},{10,... | collective-permute-start | bytes 1179656 | tf_op jit(solution)/shard_map/ppermute | solution.py:73
  307.6 50.7 %collective-permute-start.58 = (bf16[1,3080]{1,0:T(2,128)(2,1)}, bf16[1,3080]{1,0:T(2,128)(2,1)}, u32[]{:S(2)}, u32[]{:S(2)}) collective-permute-start(bf16[1,3080]{1,0:T(2,128)(2,1)} %constant_dynamic-update-slice_fusion.28), channel_id=1, source_target_pairs={{0,3},{1,2},{2,1},{3,0},{4,7},{5,6},{6,5},{7,4},{8,11},{9,10},{10,... | collective-permute-start | bytes 18488 | tf_op jit(solution)/shard_map/ppermute | solution.py:73
  308.1 50.3 %collective-permute-start.57 = (bf16[1,3080]{1,0:T(2,128)(2,1)}, bf16[1,3080]{1,0:T(2,128)(2,1)}, u32[]{:S(2)}, u32[]{:S(2)}) collective-permute-start(bf16[1,3080]{1,0:T(2,128)(2,1)} %constant_dynamic-update-slice_fusion.28), channel_id=1, source_target_pairs={{0,2},{1,3},{2,0},{3,1},{4,6},{5,7},{6,4},{7,5},{8,10},{9,11},{10,... | collective-permute-start | bytes 18488 | tf_op jit(solution)/shard_map/ppermute | solution.py:73
  338.1 13.9 %collective-permute-start.68 = (bf16[1,1536]{1,0:T(2,128)(2,1)S(1)}, bf16[1,1536]{1,0:T(2,128)(2,1)S(1)}, u32[]{:S(2)}, u32[]{:S(2)}) collective-permute-start(bf16[1,1536]{1,0:T(2,128)(2,1)S(1)} %constant_dynamic-update-slice_fusion.33), channel_id=1, source_target_pairs={{0,3},{1,2},{2,1},{3,0},{4,7},{5,6},{6,5},{7,4},{8,11},{9,10},{10,... | collective-permute-start | bytes 9224 | tf_op jit(solution)/shard_map/ppermute | solution.py:73
  339.6 12.9 %collective-permute-start.67 = (bf16[1,1536]{1,0:T(2,128)(2,1)S(1)}, bf16[1,1536]{1,0:T(2,128)(2,1)S(1)}, u32[]{:S(2)}, u32[]{:S(2)}) collective-permute-start(bf16[1,1536]{1,0:T(2,128)(2,1)S(1)} %constant_dynamic-update-slice_fusion.33), channel_id=1, source_target_pairs={{0,2},{1,3},{2,0},{3,1},{4,6},{5,7},{6,4},{7,5},{8,10},{9,11},{10,... | collective-permute-start | bytes 9224 | tf_op jit(solution)/shard_map/ppermute | solution.py:73
  340.0 12.5 %collective-permute-start.66 = (bf16[1,1536]{1,0:T(2,128)(2,1)S(1)}, bf16[1,1536]{1,0:T(2,128)(2,1)S(1)}, u32[]{:S(2)}, u32[]{:S(2)}) collective-permute-start(bf16[1,1536]{1,0:T(2,128)(2,1)S(1)} %constant_dynamic-update-slice_fusion.33), channel_id=1, source_target_pairs={{0,1},{1,0},{2,3},{3,2},{4,5},{5,4},{6,7},{7,6},{8,9},{9,8},{10,11... | collective-permute-start | bytes 9224 | tf_op jit(solution)/shard_map/ppermute | solution.py:73
  352.0 9.2 %collective-permute-start.56 = (bf16[1,3080]{1,0:T(2,128)(2,1)}, bf16[1,3080]{1,0:T(2,128)(2,1)S(1)}, u32[]{:S(2)}, u32[]{:S(2)}) collective-permute-start(bf16[1,3080]{1,0:T(2,128)(2,1)} %constant_dynamic-update-slice_fusion.28), channel_id=1, source_target_pairs={{0,1},{1,0},{2,3},{3,2},{4,5},{5,4},{6,7},{7,6},{8,9},{9,8},{10,11... | collective-permute-start | bytes 18488 | tf_op jit(solution)/shard_map/ppermute | solution.py:73
  352.5 9.1 %collective-permute-start.75 = (bf16[4,1536]{1,0:T(4,128)(2,1)S(1)}, bf16[4,1536]{1,0:T(4,128)(2,1)S(1)}, u32[]{:S(2)}, u32[]{:S(2)}) collective-permute-start(bf16[4,1536]{1,0:T(4,128)(2,1)S(1)} %pad_maximum_fusion.22), channel_id=1, source_target_pairs={{0,28},{4,24},{8,20},{12,16},{16,12},{20,8},{24,4},{28,0},{1,29},{... | collective-permute-start | bytes 36872 | tf_op jit(solution)/shard_map/ppermute | solution.py:73
  355.3 8.9 %collective-permute-start.74 = (bf16[4,1536]{1,0:T(4,128)(2,1)S(1)}, bf16[4,1536]{1,0:T(4,128)(2,1)S(1)}, u32[]{:S(2)}, u32[]{:S(2)}) collective-permute-start(bf16[4,1536]{1,0:T(4,128)(2,1)S(1)} %pad_maximum_fusion.22), channel_id=1, source_target_pairs={{0,24},{4,28},{8,16},{12,20},{16,8},{20,12},{24,0},{28,4},{1,25},{... | collective-permute-start | bytes 36872 | tf_op jit(solution)/shard_map/ppermute | solution.py:73
  358.3 9.9 %collective-permute-start.72 = (bf16[4,1536]{1,0:T(4,128)(2,1)S(1)}, bf16[4,1536]{1,0:T(4,128)(2,1)S(1)}, u32[]{:S(2)}, u32[]{:S(2)}) collective-permute-start(bf16[4,1536]{1,0:T(4,128)(2,1)S(1)} %pad_maximum_fusion.22), channel_id=1, source_target_pairs={{0,16},{4,20},{8,24},{12,28},{16,0},{20,4},{24,8},{28,12},{1,17},{... | collective-permute-start | bytes 36872 | tf_op jit(solution)/shard_map/ppermute | solution.py:73
  361.2 9.2 %collective-permute-start.71 = (bf16[4,1536]{1,0:T(4,128)(2,1)S(1)}, bf16[4,1536]{1,0:T(4,128)(2,1)S(1)}, u32[]{:S(2)}, u32[]{:S(2)}) collective-permute-start(bf16[4,1536]{1,0:T(4,128)(2,1)S(1)} %pad_maximum_fusion.22), channel_id=1, source_target_pairs={{0,12},{4,8},{8,4},{12,0},{16,28},{20,24},{24,20},{28,16},{1,13},{... | collective-permute-start | bytes 36872 | tf_op jit(solution)/shard_map/ppermute | solution.py:73
  361.6 8.8 %collective-permute-start.70 = (bf16[4,1536]{1,0:T(4,128)(2,1)S(1)}, bf16[4,1536]{1,0:T(4,128)(2,1)S(1)}, u32[]{:S(2)}, u32[]{:S(2)}) collective-permute-start(bf16[4,1536]{1,0:T(4,128)(2,1)S(1)} %pad_maximum_fusion.22), channel_id=1, source_target_pairs={{0,8},{4,12},{8,0},{12,4},{16,24},{20,28},{24,16},{28,20},{1,9},{5... | collective-permute-start | bytes 36872 | tf_op jit(solution)/shard_map/ppermute | solution.py:73
  364.2 9.0 %collective-permute-start.69 = (bf16[4,1536]{1,0:T(4,128)(2,1)S(1)}, bf16[4,1536]{1,0:T(4,128)(2,1)S(1)}, u32[]{:S(2)}, u32[]{:S(2)}) collective-permute-start(bf16[4,1536]{1,0:T(4,128)(2,1)S(1)} %pad_maximum_fusion.22), channel_id=1, source_target_pairs={{0,4},{4,0},{8,12},{12,8},{16,20},{20,16},{24,28},{28,24},{1,5},{5... | collective-permute-start | bytes 36872 | tf_op jit(solution)/shard_map/ppermute | solution.py:73
  365.5 8.5 %collective-permute-start.65 = (bf16[4,3080]{1,0:T(4,128)(2,1)S(1)}, bf16[4,3080]{1,0:T(4,128)(2,1)S(1)}, u32[]{:S(2)}, u32[]{:S(2)}) collective-permute-start(bf16[4,3080]{1,0:T(4,128)(2,1)S(1)} %pad_maximum_fusion.18), channel_id=1, source_target_pairs={{0,28},{4,24},{8,20},{12,16},{16,12},{20,8},{24,4},{28,0},{1,29},{... | collective-permute-start | bytes 73928 | tf_op jit(solution)/shard_map/ppermute | solution.py:73
  368.2 8.5 %collective-permute-start.64 = (bf16[4,3080]{1,0:T(4,128)(2,1)S(1)}, bf16[4,3080]{1,0:T(4,128)(2,1)S(1)}, u32[]{:S(2)}, u32[]{:S(2)}) collective-permute-start(bf16[4,3080]{1,0:T(4,128)(2,1)S(1)} %pad_maximum_fusion.18), channel_id=1, source_target_pairs={{0,24},{4,28},{8,16},{12,20},{16,8},{20,12},{24,0},{28,4},{1,25},{... | collective-permute-start | bytes 73928 | tf_op jit(solution)/shard_map/ppermute | solution.py:73
  370.4 7.9 %collective-permute-start.63 = (bf16[4,3080]{1,0:T(4,128)(2,1)S(1)}, bf16[4,3080]{1,0:T(4,128)(2,1)S(1)}, u32[]{:S(2)}, u32[]{:S(2)}) collective-permute-start(bf16[4,3080]{1,0:T(4,128)(2,1)S(1)} %pad_maximum_fusion.18), channel_id=1, source_target_pairs={{0,20},{4,16},{8,28},{12,24},{16,4},{20,0},{24,12},{28,8},{1,21},{... | collective-permute-start | bytes 73928 | tf_op jit(solution)/shard_map/ppermute | solution.py:73
  370.4 8.0 %collective-permute-start.62 = (bf16[4,3080]{1,0:T(4,128)(2,1)S(1)}, bf16[4,3080]{1,0:T(4,128)(2,1)S(1)}, u32[]{:S(2)}, u32[]{:S(2)}) collective-permute-start(bf16[4,3080]{1,0:T(4,128)(2,1)S(1)} %pad_maximum_fusion.18), channel_id=1, source_target_pairs={{0,16},{4,20},{8,24},{12,28},{16,0},{20,4},{24,8},{28,12},{1,17},{... | collective-permute-start | bytes 73928 | tf_op jit(solution)/shard_map/ppermute | solution.py:73
  378.4 75.2 %collective-permute-start.103 = (bf16[768,768]{1,0:T(8,128)(2,1)}, bf16[768,768]{1,0:T(8,128)(2,1)}, u32[]{:S(2)}, u32[]{:S(2)}) collective-permute-start(bf16[768,768]{1,0:T(8,128)(2,1)} %convolution_convert_fusion.4), channel_id=1, source_target_pairs={{0,1},{1,0},{2,3},{3,2},{4,5},{5,4},{6,7},{7,6},{8,9},{9,8},{10,11... | collective-permute-start | bytes 3538952 | tf_op jit(solution)/shard_map/ppermute | solution.py:73
  378.5 80.5 %collective-permute-start.100 = (bf16[768,768]{1,0:T(8,128)(2,1)}, bf16[768,768]{1,0:T(8,128)(2,1)}, u32[]{:S(2)}, u32[]{:S(2)}) collective-permute-start(bf16[768,768]{1,0:T(8,128)(2,1)} %convolution_convert_fusion.6), channel_id=1, source_target_pairs={{0,1},{1,0},{2,3},{3,2},{4,5},{5,4},{6,7},{7,6},{8,9},{9,8},{10,11... | collective-permute-start | bytes 3538952 | tf_op jit(solution)/shard_map/ppermute | solution.py:73
  378.9 28.3 %collective-permute-start.97 = (bf16[4,2,96,768]{3,2,1,0:T(8,128)(2,1)}, bf16[4,2,96,768]{3,2,1,0:T(8,128)(2,1)}, u32[]{:S(2)}, u32[]{:S(2)}) collective-permute-start(bf16[4,2,96,768]{3,2,1,0:T(8,128)(2,1)} %fusion.60), channel_id=1, source_target_pairs={{0,4},{4,0},{8,12},{12,8},{16,20},{20,16},{24,28},{28,24},{1,5},{5... | collective-permute-start | bytes 3538952 | tf_op jit(solution)/shard_map/ppermute | solution.py:73
  380.5 73.3 %collective-permute-start.105 = (bf16[768,768]{1,0:T(8,128)(2,1)}, bf16[768,768]{1,0:T(8,128)(2,1)}, u32[]{:S(2)}, u32[]{:S(2)}) collective-permute-start(bf16[768,768]{1,0:T(8,128)(2,1)} %add_convert_fusion), channel_id=1, source_target_pairs={{0,2},{1,3},{2,0},{3,1},{4,6},{5,7},{6,4},{7,5},{8,10},{9,11},{10,... | collective-permute-start | bytes 3538952 | tf_op jit(solution)/shard_map/ppermute | solution.py:73
  382.8 26.3 %collective-permute-start.83 = (bf16[8,2,24,768]{3,2,1,0:T(8,128)(2,1)}, bf16[8,2,24,768]{3,2,1,0:T(8,128)(2,1)}, u32[]{:S(2)}, u32[]{:S(2)}) collective-permute-start(bf16[8,2,24,768]{3,2,1,0:T(8,128)(2,1)} %fusion.119), channel_id=1, source_target_pairs={{0,1},{1,0},{2,3},{3,2},{4,5},{5,4},{6,7},{7,6},{8,9},{9,8},{10,11... | collective-permute-start | bytes 1769480 | tf_op jit(solution)/shard_map/ppermute | solution.py:73
  409.1 50.3 %collective-permute-start.102 = (bf16[768,768]{1,0:T(8,128)(2,1)S(1)}, bf16[768,768]{1,0:T(8,128)(2,1)S(1)}, u32[]{:S(2)}, u32[]{:S(2)}) collective-permute-start(bf16[768,768]{1,0:T(8,128)(2,1)S(1)} %copy-done.103), channel_id=1, source_target_pairs={{0,2},{1,3},{2,0},{3,1},{4,6},{5,7},{6,4},{7,5},{8,10},{9,11},{10,... | collective-permute-start | bytes 3538952 | tf_op jit(solution)/shard_map/ppermute | solution.py:73
  412.1 31.8 %collective-permute-start.84 = (bf16[8,1,24,768]{3,2,1,0:T(8,128)(2,1)S(1)}, bf16[8,1,24,768]{3,2,1,0:T(8,128)(2,1)S(1)}, u32[]{:S(2)}, u32[]{:S(2)}) collective-permute-start(bf16[8,1,24,768]{3,2,1,0:T(8,128)(2,1)S(1)} %dynamic-slice_convert_fusion.8), channel_id=1, source_target_pairs={{0,2},{1,3},{2,0},{3,1},{4,6},{5,7},{6,4},{7,5},{8,10},{9,11},{10,... | collective-permute-start | bytes 884744 | tf_op jit(solution)/shard_map/ppermute | solution.py:73
  443.9 9.6 %collective-permute-start.91 = (bf16[8,1,24,776]{3,2,1,0:T(8,128)(2,1)S(1)}, bf16[8,1,24,776]{3,2,1,0:T(8,128)(2,1)S(1)}, u32[]{:S(2)}, u32[]{:S(2)}) collective-permute-start(bf16[8,1,24,776]{3,2,1,0:T(8,128)(2,1)S(1)} %dynamic-slice_convert_fusion.6), channel_id=1, source_target_pairs={{0,2},{1,3},{2,0},{3,1},{4,6},{5,7},{6,4},{7,5},{8,10},{9,11},{10,... | collective-permute-start | bytes 893960 | tf_op jit(solution)/shard_map/ppermute | solution.py:73
  453.5 26.1 %collective-permute-start.76 = (bf16[8,2,24,1536]{3,2,1,0:T(8,128)(2,1)S(1)}, bf16[8,2,24,1536]{3,2,1,0:T(8,128)(2,1)S(1)}, u32[]{:S(2)}, u32[]{:S(2)}) collective-permute-start(bf16[8,2,24,1536]{3,2,1,0:T(8,128)(2,1)S(1)} %copy-done.31), channel_id=1, source_target_pairs={{0,1},{1,0},{2,3},{3,2},{4,5},{5,4},{6,7},{7,6},{8,9},{9,8},{10,11... | collective-permute-start | bytes 3538952 | tf_op jit(solution)/shard_map/ppermute | solution.py:73
  453.6 15.8 %collective-permute-start.98 = (bf16[2,2,96,768]{3,2,1,0:T(8,128)(2,1)S(1)}, bf16[2,2,96,768]{3,2,1,0:T(8,128)(2,1)S(1)}, u32[]{:S(2)}, u32[]{:S(2)}) collective-permute-start(bf16[2,2,96,768]{3,2,1,0:T(8,128)(2,1)S(1)} %fusion.120), channel_id=1, source_target_pairs={{0,8},{4,12},{8,0},{12,4},{16,24},{20,28},{24,16},{28,20},{1,9},{5... | collective-permute-start | bytes 1769480 | tf_op jit(solution)/shard_map/ppermute | solution.py:73
  453.8 16.9 %collective-permute-start.85 = (bf16[4,24,768]{2,1,0:T(8,128)(2,1)S(1)}, bf16[4,24,768]{2,1,0:T(8,128)(2,1)S(1)}, u32[]{:S(2)}, u32[]{:S(2)}) collective-permute-start(bf16[4,24,768]{2,1,0:T(8,128)(2,1)S(1)} %fusion.152), channel_id=1, source_target_pairs={{0,4},{4,0},{8,12},{12,8},{16,20},{20,16},{24,28},{28,24},{1,5},{5... | collective-permute-start | bytes 442376 | tf_op jit(solution)/shard_map/ppermute | solution.py:73
  458.9 13.6 %collective-permute-start.92 = (bf16[4,24,776]{2,1,0:T(8,128)(2,1)S(1)}, bf16[4,24,776]{2,1,0:T(8,128)(2,1)S(1)}, u32[]{:S(2)}, u32[]{:S(2)}) collective-permute-start(bf16[4,24,776]{2,1,0:T(8,128)(2,1)S(1)} %fusion.133), channel_id=1, source_target_pairs={{0,4},{4,0},{8,12},{12,8},{16,20},{20,16},{24,28},{28,24},{1,5},{5... | collective-permute-start | bytes 446984 | tf_op jit(solution)/shard_map/ppermute | solution.py:73
  469.6 42.8 %collective-permute-start.99 = (bf16[1,2,96,768]{3,2,1,0:T(8,128)(2,1)S(1)}, bf16[1,2,96,768]{3,2,1,0:T(8,128)(2,1)S(1)}, u32[]{:S(2)}, u32[]{:S(2)}) collective-permute-start(bf16[1,2,96,768]{3,2,1,0:T(8,128)(2,1)S(1)} %dynamic-slice_convert_fusion.7), channel_id=1, source_target_pairs={{0,16},{4,20},{8,24},{12,28},{16,0},{20,4},{24,8},{28,12},{1,17},{... | collective-permute-start | bytes 884744 | tf_op jit(solution)/shard_map/ppermute | solution.py:73
  470.7 8.8 %collective-permute-start.86 = (bf16[2,24,768]{2,1,0:T(8,128)(2,1)S(1)}, bf16[2,24,768]{2,1,0:T(8,128)(2,1)S(1)}, u32[]{:S(2)}, u32[]{:S(2)}) collective-permute-start(bf16[2,24,768]{2,1,0:T(8,128)(2,1)S(1)} %fusion.160), channel_id=1, source_target_pairs={{0,8},{4,12},{8,0},{12,4},{16,24},{20,28},{24,16},{28,20},{1,9},{5... | collective-permute-start | bytes 221192 | tf_op jit(solution)/shard_map/ppermute | solution.py:73
  472.6 11.8 %collective-permute-start.93 = (bf16[2,24,776]{2,1,0:T(8,128)(2,1)S(1)}, bf16[2,24,776]{2,1,0:T(8,128)(2,1)S(1)}, u32[]{:S(2)}, u32[]{:S(2)}) collective-permute-start(bf16[2,24,776]{2,1,0:T(8,128)(2,1)S(1)} %fusion.158), channel_id=1, source_target_pairs={{0,8},{4,12},{8,0},{12,4},{16,24},{20,28},{24,16},{28,20},{1,9},{5... | collective-permute-start | bytes 223496 | tf_op jit(solution)/shard_map/ppermute | solution.py:73
  480.1 13.3 %collective-permute-start.77 = (bf16[8,1,24,1536]{3,2,1,0:T(8,128)(2,1)S(1)}, bf16[8,1,24,1536]{3,2,1,0:T(8,128)(2,1)S(1)}, u32[]{:S(2)}, u32[]{:S(2)}) collective-permute-start(bf16[8,1,24,1536]{3,2,1,0:T(8,128)(2,1)S(1)} %dynamic-slice_convert_fusion.5), channel_id=1, source_target_pairs={{0,2},{1,3},{2,0},{3,1},{4,6},{5,7},{6,4},{7,5},{8,10},{9,11},{10,... | collective-permute-start | bytes 1769480 | tf_op jit(solution)/shard_map/ppermute | solution.py:73
  484.4 10.1 %collective-permute-start.94 = (bf16[1,24,776]{2,1,0:T(8,128)(2,1)S(1)}, bf16[1,24,776]{2,1,0:T(8,128)(2,1)S(1)}, u32[]{:S(2)}, u32[]{:S(2)}) collective-permute-start(bf16[1,24,776]{2,1,0:T(8,128)(2,1)S(1)} %dynamic-slice_convert_fusion.12), channel_id=1, source_target_pairs={{0,16},{4,20},{8,24},{12,28},{16,0},{20,4},{24,8},{28,12},{1,17},{... | collective-permute-start | bytes 111752 | tf_op jit(solution)/shard_map/ppermute | solution.py:73
  494.5 8.4 %collective-permute-start.95 = (bf16[24,776]{1,0:T(8,128)(2,1)S(1)}, bf16[24,776]{1,0:T(8,128)(2,1)S(1)}, u32[]{:S(2)}, u32[]{:S(2)}) collective-permute-start(bf16[24,776]{1,0:T(8,128)(2,1)S(1)} %fusion.165), channel_id=1, source_target_pairs={{0,1},{1,0},{2,3},{3,2},{4,5},{5,4},{6,7},{7,6},{8,9},{9,8},{10,11... | collective-permute-start | bytes 111752 | tf_op jit(solution)/shard_map/ppermute | solution.py:73
  494.7 10.1 %collective-permute-start.89 = (bf16[48,768]{1,0:T(8,128)(2,1)S(1)}, bf16[48,768]{1,0:T(8,128)(2,1)S(1)}, u32[]{:S(2)}, u32[]{:S(2)}) collective-permute-start(bf16[48,768]{1,0:T(8,128)(2,1)S(1)} %maximum_select_fusion.5), channel_id=1, source_target_pairs={{0,2},{1,3},{2,0},{3,1},{4,6},{5,7},{6,4},{7,5},{8,10},{9,11},{10,... | collective-permute-start | bytes 221192 | tf_op jit(solution)/shard_map/ppermute | solution.py:73
  (150 other events, 1338.6 us)

commit v2 on v1

--- a/solution.py
+++ b/solution.py
@@ -84,12 +84,28 @@
     return masks
 
 
-def gather_hid(own):
-    blocks = {0: own}
-    for mask in reversed(bits_of("hid")):
+def gather_hid(own, far):
+    masks = bits_of("hid")
+    blocks = {0: own, masks[-1]: far}
+    for mask in reversed(masks[:-1]):
         for index in list(blocks):
             blocks[index ^ mask] = swap(blocks[index], "hid", mask)
     return [blocks[index] for index in range(lax.axis_size("hid"))]
+
+
+def gather_rows(own):
+    rows = own
+    for mask in reversed(bits_of("hid")):
+        rows = jnp.concatenate([rows, swap(rows, "hid", mask)], axis=0)
+    return rows
+
+
+def reduce_rows(rows):
+    for mask in bits_of("hid"):
+        half = rows.shape[0] // 2
+        moved = swap(low(rows[half:]), "hid", mask)
+        rows = rows[:half].astype(jnp.float32) + moved.astype(jnp.float32)
+    return rows
 
 
 def reduce_hid(blocks):
@@ -121,40 +137,31 @@
     return values[0]
 
 
-def small_exp():
-    return lax.axis_size("exp") <= 8
-
-
 def exchange(rows):
-    size = lax.axis_size("exp")
-    if not small_exp():
-        return lax.all_to_all(rows, "exp", split_axis=0, concat_axis=0, tiled=True)
-    per = rows.shape[0] // size
-    chunks = [rows[index * per : (index + 1) * per] for index in range(size)]
-    moved = [chunks[0]] + [swap(chunks[index], "exp", index) for index in range(1, size)]
-    return jnp.concatenate(moved, axis=0)
+    return lax.all_to_all(rows, "exp", split_axis=0, concat_axis=0, tiled=True)
+
+
+def join_hid(own):
+    place = lax.axis_index("hid")
+    for step, mask in reversed(list(enumerate(bits_of("hid")))):
+        other = swap(own, "hid", mask)
+        both = jnp.stack([own, other], axis=0)
+        swapped = jnp.stack([other, own], axis=0)
+        own = jnp.where((place >> step) & 1 == 0, both, swapped)
+    depth = len(bits_of("hid"))
+    own = jnp.transpose(own, tuple(reversed(range(depth))) + tuple(range(depth, own.ndim)))
+    return own.reshape((-1,) + own.shape[depth + 1 :])
 
 
 def gather_items(own):
+    near = join_hid(own)
+    return exchange(jnp.concatenate([near] * lax.axis_size("exp"), axis=0))
+
+
+def sum_all(partial):
     size = lax.axis_size("exp")
     width = lax.axis_size("hid")
-    if not small_exp():
-        return lax.all_gather(own, ("exp", "hid"), axis=0, tiled=True)
-    near = jnp.concatenate([own] + [swap(own, "hid", mask) for mask in range(1, width)], axis=0)
-    rows = jnp.concatenate([near] + [swap(near, "exp", mask) for mask in range(1, size)], axis=0)
-    count = own.shape[0]
-    place = lax.axis_index("exp") * width + lax.axis_index("hid")
-    target = jnp.arange(size * width * count, dtype=jnp.int32)
-    source = (target // count ^ place) * count + target % count
-    hot = source[:, None] == target[None, :]
-    if own.dtype == jnp.bfloat16:
-        return low(mat_prod(low(hot), rows))
-    return jnp.sum(jnp.where(hot[:, :, None], rows[None, :, :], 0), axis=1)
-
-
-def sum_all(partial, columns):
-    size = lax.axis_size("exp")
-    width = lax.axis_size("hid")
+    columns = partial.shape[1]
     share = partial.shape[0] // (size * width)
     values = partial.reshape(size, width, share, columns)
     place = lax.axis_index("hid")
@@ -165,16 +172,9 @@
         sent = lax.dynamic_index_in_dim(halves, 1 - bit, 2, keepdims=False)
         moved = swap(low(sent), "hid", mask)
         values = kept.astype(jnp.float32) + moved.astype(jnp.float32)
-    mine = low(reduce_axis(values.reshape(size, share, columns), "exp"))
-    for step, mask in enumerate(bits_of("hid")):
-        bit = (place >> step) & 1
-        other = swap(mine, "hid", mask)
-        mine = jnp.where(
-            bit == 0,
-            jnp.concatenate([mine, other], axis=0),
-            jnp.concatenate([other, mine], axis=0),
-        )
-    return mine.astype(jnp.float32)
+    parts = exchange(low(values).reshape(size * share, columns)).reshape(size, share, columns)
+    mine = low(jnp.sum(parts.astype(jnp.float32), axis=0))
+    return join_hid(mine).astype(jnp.float32)
 
 
 def condition_of(timesteps, labels, time_weight, time_bias, class_table):
@@ -214,9 +214,11 @@
     slots_all = experts * capacity
     score_scale = 1.0 / math.sqrt(HDIM)
 
-    blocks_in = gather_hid(expert_in[0])
-    blocks_out = gather_hid(expert_out[0])
-    numbers = gather_items(jnp.stack([timesteps, labels], axis=1))
+    own_in, own_out = expert_in[0], expert_out[0]
+    far_mask = bits_of("hid")[-1]
+    far_in = swap(own_in, "hid", far_mask)
+    far_in, later_out = lax.optimization_barrier((far_in, own_out))
+    far_out = swap(later_out, "hid", far_mask)
 
     freq_emb, label_hot, condition, silu_cond = condition_of(
         timesteps, labels, time_weight, time_bias, class_table
@@ -234,19 +236,16 @@
     kept_first = slot_index[:, 0:1] < capacity
     kept_second = slot_index[:, 1:2] < capacity
     slot_ids = jnp.arange(slots_all, dtype=jnp.int32)[None, :]
-    first_chunk, second_chunk = first_route, second_route
-    if small_exp():
-        first_chunk, second_chunk = first_route ^ place_exp, second_route ^ place_exp
     dispatch_first = low(
-        (first_chunk * capacity + slot_index[:, 0:1] == slot_ids) & kept_first
+        (first_route * capacity + slot_index[:, 0:1] == slot_ids) & kept_first
     )
     dispatch_second = low(
-        (second_chunk * capacity + slot_index[:, 1:2] == slot_ids) & kept_second
+        (second_route * capacity + slot_index[:, 1:2] == slot_ids) & kept_second
     )
     dispatch_both = dispatch_first + dispatch_second
     picks = jnp.concatenate([dispatch_first, dispatch_second], axis=0)
     grad_rows = exchange(low(prod_rows(dispatch_both, grad_branch_low)))
-    grad_tokens = jnp.concatenate(gather_hid(grad_branch_low), axis=0)
+    grad_tokens = gather_rows(grad_branch_low)
 
     residual = patches.astype(jnp.float32).reshape(item_count, SEQ, model_dim)
     normed_one, inverse_one = normalize(residual)
@@ -284,8 +283,13 @@
         ],
         axis=1,
     )
-    received = exchange(low(prod_rows(picks, carried)))
-    tokens_all = jnp.concatenate(gather_hid(hidden_two), axis=0)
+    sent_rows, grad_rows, far_in = lax.optimization_barrier(
+        (low(prod_rows(picks, carried)), grad_rows, far_in)
+    )
+    received = exchange(sent_rows)
+    blocks_in = gather_hid(own_in, far_in)
+    blocks_out = gather_hid(own_out, far_out)
+    tokens_all = gather_rows(hidden_two)
     rows = received[:, :model_dim]
     gate_rows = (
         received[:, model_dim : model_dim + 1].astype(jnp.float32)
@@ -296,13 +300,8 @@
     act_shared = low(jax.nn.gelu(pre_shared))
     grad_pre_shared = low(gelu_back(pre_shared, prod_cols(grad_tokens, shared_out)))
 
-    def split(values):
-        return [
-            values[index * tokens : (index + 1) * tokens] for index in range(lax.axis_size("hid"))
-        ]
-
-    shared_term = reduce_hid(split(prod_cols(grad_pre_shared, shared_in)))
-    shared_sum = reduce_hid(split(mat_prod(act_shared, shared_out)))
+    shared_term = reduce_rows(prod_cols(grad_pre_shared, shared_in))
+    shared_sum = reduce_rows(mat_prod(act_shared, shared_out))
 
     pre_blocks = [mat_prod(rows, block) for block in blocks_in]
     act_blocks = [low(jax.nn.gelu(block)) for block in pre_blocks]
@@ -357,25 +356,6 @@
     )
     grad_gate_one = jnp.sum(branch_one * grad_residual, axis=1)
     grad_branch_one = low((gate_one * grad_residual).reshape(tokens, model_dim))
-    dense_two = sum_all(
-        jnp.concatenate(
-            [prod_rows(attended_low, grad_branch_one), prod_rows(hidden_two, grad_logits)], axis=1
-        ),
-        model_dim + experts,
-    )
-    counts_local = jnp.sum(
-        first_hot * kept_first.astype(jnp.float32) + second_hot * kept_second.astype(jnp.float32),
-        axis=0,
-    )
-    counts_rows = jnp.zeros((item_count, experts), jnp.float32).at[0].set(counts_local)
-    early = gather_items(
-        low(
-            jnp.concatenate(
-                [grad_gate_one, grad_shift_two, grad_scale_two, grad_gate_two, counts_rows], axis=1
-            )
-        )
-    )
-
     grad_attended = low(prod_cols(grad_branch_one, proj_weight)).reshape(
         item_count, SEQ, HEADS, HDIM
     )
@@ -383,7 +363,17 @@
         "bhqk,bqhd->bkhd", attention_low, grad_attended, preferred_element_type=jnp.float32
     )
     grad_values = low(grad_values).reshape(tokens, model_dim)
-    dense_values = sum_all(prod_rows(flat_one, grad_values), model_dim)
+    padded = jnp.pad(grad_logits, ((0, 0), (0, -experts % 128)))
+    dense_one = sum_all(
+        jnp.concatenate(
+            [
+                low(prod_rows(attended_low, grad_branch_one)),
+                low(prod_rows(flat_one, grad_values)),
+                low(prod_rows(hidden_two, padded)),
+            ],
+            axis=1,
+        )
+    )
     grad_probs = jnp.einsum(
         "bqhd,bkhd->bhqk", grad_attended, value_rows, preferred_element_type=jnp.float32
     )
@@ -402,7 +392,10 @@
         ],
         axis=1,
     )
-    dense_pair = sum_all(prod_rows(flat_one, grad_pair), 2 * model_dim)
+    pair_rows, weight_expert_in, weight_expert_out, weight_shared = lax.optimization_barrier(
+        (grad_pair, weight_expert_in, weight_expert_out, weight_shared)
+    )
+    dense_pair = sum_all(prod_rows(flat_one, pair_rows))
     grad_hidden_one = (
         prod_cols(grad_pair, qkv_weight[:, : 2 * model_dim])
         + prod_cols(grad_values, qkv_weight[:, 2 * model_dim :])
@@ -413,27 +406,48 @@
         normed_one, inverse_one, grad_hidden_one * (1.0 + scale_one)
     )
     grad_patches = low(grad_input.reshape(tokens, model_dim))
-    late = gather_items(low(jnp.concatenate([grad_shift_one, grad_scale_one], axis=1)))
-
+    counts_local = jnp.sum(
+        first_hot * kept_first.astype(jnp.float32) + second_hot * kept_second.astype(jnp.float32),
+        axis=0,
+    )
+    counts_rows = jnp.where(jnp.arange(item_count)[:, None] == 0, counts_local[None, :], 0.0)
+    digits = jnp.stack(
+        [timesteps // 32, timesteps % 32, labels // 32, labels % 32], axis=1
+    ).astype(jnp.float32)
+    item_rows = gather_items(
+        low(
+            jnp.concatenate(
+                [
+                    grad_shift_one,
+                    grad_scale_one,
+                    grad_gate_one,
+                    grad_shift_two,
+                    grad_scale_two,
+                    grad_gate_two,
+                    digits,
+                    counts_rows,
+                ],
+                axis=1,
+            )
+        )
+    )
+
+    grad_modulate = item_rows[:, : 6 * model_dim]
+    rest = item_rows[:, 6 * model_dim :].astype(jnp.float32)
+    expert_counts = jnp.sum(rest[:, 4:], axis=0)
+    numbers = rest[:, 0:4:2] * 32.0 + rest[:, 1:4:2]
     freq_all, label_all, condition_all, silu_all = condition_of(
-        numbers[:, 0], numbers[:, 1], time_weight, time_bias, class_table
-    )
-    early_mod = early[:, : 4 * model_dim]
-    expert_counts = jnp.sum(early[:, 4 * model_dim :].astype(jnp.float32), axis=0)
-    silu_share = lax.dynamic_slice_in_dim(silu_all, place_exp * share, share, 1)
-    weight_ada = jnp.concatenate(
-        [prod_rows(silu_share, late), prod_rows(silu_share, early_mod)], axis=1
-    )
-    bias_ada = jnp.concatenate(
-        [
-            jnp.sum(late.astype(jnp.float32), axis=0),
-            jnp.sum(early_mod.astype(jnp.float32), axis=0),
-        ],
-        axis=0,
-    )
-    grad_silu = prod_cols(early_mod, ada_weight[:, 2 * model_dim :]) + prod_cols(
-        late, ada_weight[:, : 2 * model_dim]
-    )
+        numbers[:, 0].astype(jnp.int32),
+        numbers[:, 1].astype(jnp.int32),
+        time_weight,
+        time_bias,
+        class_table,
+    )
+    weight_ada = prod_rows(
+        lax.dynamic_slice_in_dim(silu_all, place_exp * share, share, 1), grad_modulate
+    )
+    bias_ada = jnp.sum(grad_modulate.astype(jnp.float32), axis=0)
+    grad_silu = prod_cols(grad_modulate, ada_weight)
     grad_condition = jax.vjp(jax.nn.silu, condition_all)[1](grad_silu)[0]
     bias_time = jnp.sum(grad_condition, axis=0)
     grad_condition_low = low(grad_condition)
@@ -451,9 +465,9 @@
         table_grad,
         weight_ada,
         bias_ada,
-        jnp.concatenate([dense_pair, dense_values], axis=1),
-        dense_two[:, :model_dim],
-        dense_two[:, model_dim:],
+        jnp.concatenate([dense_pair, dense_one[:, model_dim : 2 * model_dim]], axis=1),
+        dense_one[:, :model_dim],
+        dense_one[:, 2 * model_dim : 2 * model_dim + experts],
         weight_shared[0],
         weight_shared[1].T,
         weight_expert_in[None],

time: 526 us -> 425 us (0.81)
  waiting for transfers between devices: 220 us -> 100 us
  starting transfers between devices: 115 us -> 61.3 us
  matrix products: 118 us -> 166 us
  other arithmetic: 33.1 us -> 48.9 us
  local copies, waits for them, and re-layouts: 31.1 us -> 37.6 us
    ppermute x106 -> x33, waiting for transfers between devices: 220 us -> 72.9 us  [swap(): return lax.ppermute(values, axis, pairs_of(lax.axis_size(axis), mask))]
    ppermute x106 -> x33, starting transfers between devices: 115 us -> 26.3 us  [swap(): return lax.ppermute(values, axis, pairs_of(lax.axis_size(axis), mask))]
    all_to_all x0 -> x7, starting transfers between devices: none -> 34.9 us  [exchange(): return lax.all_to_all(rows, 'exp', split_axis=0, concat_axis=0, tiled=True)]
    all_to_all x0 -> x7, waiting for transfers between devices: none -> 27.3 us  [exchange(): return lax.all_to_all(rows, 'exp', split_axis=0, concat_axis=0, tiled=True)]
    dot_general x20 -> x19, matrix products: 36.7 us -> 54.9 us  [prod_rows(): lax.dot_general(left_side, right_side, (((0,), (0,)), ((), ())), preferre...]
    dot_general x22 -> x20, matrix products: 29.8 us -> 43.9 us  [mat_prod(): return jnp.dot(left_side, right_side, preferred_element_type=jnp.float32)]
    dot_general x16 -> x15, matrix products: 33.7 us -> 43.7 us  [prod_cols(): lax.dot_general(left_side, right_side, (((1,), (1,)), ((), ())), preferre...]
    add x1 -> x6, other arithmetic: 0.61 us -> 9.11 us  [the longest x2 7.07 us: reduce_hid(): blocks[index].astype(jnp.float32) + moved[index].astype(jnp.float32)]
  transfers between devices with their start and end apart: 106 -> 40, of which waited for: 41 -> 15; matrix products, arithmetic and copies ran while one was open for 32% -> 58% of each run, Pallas kernels for 0% -> 0%
where the time goes in v2:
time: 425 us; the launch traced here: 418 us
  matrix products  166 us (39%)
  waiting for transfers between devices  100 us (24%)
  starting transfers between devices  61.3 us (14%)
  other arithmetic  48.9 us (12%)
  local copies, waits for them, and re-layouts  37.6 us (9%)
    ppermute x33, waiting for transfers between devices, swap(): return lax.ppermute(values, axis, pairs_of(lax.axis_size(axis), mask))  72.9 us
    dot_general x19, matrix products, prod_rows(): lax.dot_general(left_side, right_side, (((0,), (0,)), ((), ())), preferre...  54.9 us
    dot_general x20, matrix products, mat_prod(): return jnp.dot(left_side, right_side, preferred_element_type=jnp.float32)  43.9 us
    dot_general x15, matrix products, prod_cols(): lax.dot_general(left_side, right_side, (((1,), (1,)), ((), ())), preferre...  43.7 us
    all_to_all x7, starting transfers between devices, exchange(): return lax.all_to_all(rows, 'exp', split_axis=0, concat_axis=0, tiled=True)  34.9 us
    all_to_all x7, waiting for transfers between devices, exchange(): return lax.all_to_all(rows, 'exp', split_axis=0, concat_axis=0, tiled=True)  27.3 us
    ppermute x33, starting transfers between devices, swap(): return lax.ppermute(values, axis, pairs_of(lax.axis_size(axis), mask))  26.3 us
  transfers between devices with their start and end apart: 40, of which 15 were waited for; matrix products, arithmetic and copies ran while one was open for 58% of the time, Pallas kernels for 0%

profile of v2, /device:TPU:0, one launch (start us, length us, event | category | flops | bytes accessed | tf_op | source)
XLA Modules:
  0.0 417.9 jit_solution(8427806705778635747)
XLA Ops:
  1.2 2.6 collective-permute-start.4
  6.8 4.1 convolution_reduce_fusion
  13.1 2.6 convolution_convert_fusion.8
  15.8 6.3 %all-to-all-start = ((bf16[8,72,768]{2,1,0:T(8,128)(2,1)}), bf16[8,72,768]{2,1,0:T(8,128)(2,1)}, u32[]{:S(2)}, u32[]{:S(2)}) async-start(bf16[8,72,768]{2,1,0:T(8,128)(2,1)} %bitcast.236), calls=%async_computation | async-start | bytes 1769472 | tf_op jit(solution)/shard_map/all_to_all | solution.py:141
  22.5 4.2 %convolution_convert_fusion = bf16[256,2304]{1,0:T(8,128)(2,1)} fusion(bf16[768,2304]{1,0:T(8,128)(2,1)} %param.29, bf16[256,768]{1,0:T(8,128)(2,1)S(1)} %copy-done.5, f32[768]{0:T(1024)S(1)} %get-tuple-element.91, f32[768]{0:T(1024)S(1)} %get-tuple-element.92, f32[256]{0:T(256)S(1)} %add_rsqrt_fusion.1, f32[256]{0:T(256)S(1)} %broadcast_multiply_fusion.5), kind=kOutput, calls=%fused_computation.4 | convolution fusion | flops 907739136 | bytes 5120000 | tf_op jit(solution)/shard_map/dot_general | solution.py:18
  26.7 2.5 copy.68
  38.5 8.9 %collective-permute-done = bf16[256,768]{1,0:T(8,128)(2,1)S(1)} collective-permute-done((bf16[256,768]{1,0:T(8,128)(2,1)S(1)}, bf16[256,768]{1,0:T(8,128)(2,1)S(1)}, u32[]{:S(2)}, u32[]{:S(2)}) %collective-permute-start) | collective-permute-done | bytes 393248 | tf_op jit(solution)/shard_map/ppermute | solution.py:73
  54.7 2.9 convolution_convert_fusion.7
  57.6 2.5 fusion.111
  60.2 3.1 fusion.108
  63.3 4.2 %fusion.7 = bf16[1024,768]{1,0:T(8,128)(2,1)S(1)} fusion(f32[1024,768]{1,0:T(8,128)S(1)} %fusion.111, bf16[768,768]{1,0:T(8,128)(2,1)S(1)} %copy-done.83, bf16[512,768]{1,0:T(8,128)(2,1)} %collective-permute-done.11, bf16[256,768]{1,0:T(8,128)(2,1)} %collective-permute-done.10, bf16[256,768]{1,0:T(8,128)(2,1)} %fusion.66), kind=kOutput, calls=%fused_computation.11 | convolution fusion | flops 1228406784 | bytes 7471104 | tf_op jit(solution)/shard_map/dot_general | solution.py:28
  67.5 2.6 fusion.110
  82.1 4.8 %all-to-all-start.1 = ((bf16[8,72,896]{2,1,0:T(8,128)(2,1)}), bf16[8,72,896]{2,1,0:T(8,128)(2,1)}, u32[]{:S(2)}, u32[]{:S(2)}) async-start(bf16[8,72,896]{2,1,0:T(8,128)(2,1)} %bitcast.235), calls=%async_computation.1 | async-start | bytes 2064384 | tf_op jit(solution)/shard_map/all_to_all | solution.py:141
  87.2 3.6 fusion.220
  90.9 18.4 %collective-permute-done.22 = bf16[4,2,96,768]{3,2,1,0:T(8,128)(2,1)} collective-permute-done((bf16[4,2,96,768]{3,2,1,0:T(8,128)(2,1)}, bf16[4,2,96,768]{3,2,1,0:T(8,128)(2,1)}, u32[]{:S(2)}, u32[]{:S(2)}) %collective-permute-start.22) | collective-permute-done | bytes 1179680 | tf_op jit(solution)/shard_map/ppermute | solution.py:73
  109.3 2.4 bitcast_add_fusion.1
  117.6 10.0 %collective-permute-done.23 = bf16[2,2,96,768]{3,2,1,0:T(8,128)(2,1)S(1)} collective-permute-done((bf16[2,2,96,768]{3,2,1,0:T(8,128)(2,1)S(1)}, bf16[2,2,96,768]{3,2,1,0:T(8,128)(2,1)S(1)}, u32[]{:S(2)}, u32[]{:S(2)}) %collective-permute-start.23) | collective-permute-done | bytes 589856 | tf_op jit(solution)/shard_map/ppermute | solution.py:73
  129.6 2.7 collective-permute-start.24
  132.2 3.6 fusion.221
  135.9 9.3 %collective-permute-done.24 = bf16[1,2,96,768]{3,2,1,0:T(8,128)(2,1)S(1)} collective-permute-done((bf16[1,2,96,768]{3,2,1,0:T(8,128)(2,1)S(1)}, bf16[1,2,96,768]{3,2,1,0:T(8,128)(2,1)S(1)}, u32[]{:S(2)}, u32[]{:S(2)}) %collective-permute-start.24) | collective-permute-done | bytes 294944 | tf_op jit(solution)/shard_map/ppermute | solution.py:73
  152.1 4.3 %convolution_convert_fusion.3 = bf16[768,768]{1,0:T(8,128)(2,1)} fusion(f32[576,768]{1,0:T(8,128)S(1)} %fusion.131, bf16[576,768]{1,0:T(8,128)(2,1)} %bitcast.14, f32[576]{0:T(1024)S(1)} %add_reduce_fusion), kind=kOutput, calls=%fused_computation.86 | convolution fusion | flops 685375488 | bytes 3836160 | tf_op jit(solution)/shard_map/dot_general | solution.py:22
  156.9 2.4 fusion.185
  161.7 4.7 %fusion.199 = f32[768,768]{1,0:T(8,128)} fusion(f32[576,768]{1,0:T(8,128)S(1)} %fusion.137, bf16[576,768]{1,0:T(8,128)(2,1)} %bitcast.14, f32[576]{0:T(1024)S(1)} %add_reduce_fusion), kind=kOutput, calls=%fused_computation.350 | convolution fusion | flops 684785664 | bytes 5015808 | tf_op jit(solution)/shard_map/dot_general | solution.py:22
  166.4 3.1 fusion.24
  169.6 3.0 fusion.135
  172.6 4.0 convolution_convert_fusion.4
  176.6 4.3 %fusion.81 = f32[576,768]{1,0:T(8,128)} fusion(bf16[768,768]{1,0:T(8,128)(2,1)} %collective-permute-done.4, f32[576,768]{1,0:T(8,128)S(1)} %fusion.133, f32[576,768]{1,0:T(8,128)S(1)} %copy-done.85), kind=kOutput, calls=%fused_computation.145 | convolution fusion | flops 688324608 | bytes 6488064 | tf_op jit(solution)/shard_map/dot_general | solution.py:28
  180.9 2.5 fusion.202
  183.4 2.5 fusion.200
  185.9 3.9 fusion.74
  189.8 4.3 %fusion.83 = f32[576,768]{1,0:T(8,128)} fusion(bf16[768,768]{1,0:T(8,128)(2,1)} %collective-permute-done.5, f32[576,768]{1,0:T(8,128)S(1)} %fusion.135, f32[576,768]{1,0:T(8,128)S(1)} %copy-done.86), kind=kOutput, calls=%fused_computation.147 | convolution fusion | flops 688324608 | bytes 6488064 | tf_op jit(solution)/shard_map/dot_general | solution.py:28
  194.1 4.0 convolution_convert_fusion.6
  198.1 3.4 add_convert_fusion.3
  201.5 5.7 %all-to-all-start.2 = ((bf16[8,72,768]{2,1,0:T(8,128)(2,1)}), bf16[8,72,768]{2,1,0:T(8,128)(2,1)}, u32[]{:S(2)}, u32[]{:S(2)}) async-start(bf16[8,72,768]{2,1,0:T(8,128)(2,1)} %bitcast.218), calls=%async_computation.2 | async-start | bytes 1769472 | tf_op jit(solution)/shard_map/all_to_all | solution.py:141
  207.3 2.6 fusion.222
  209.9 4.2 %convolution_convert_fusion.5 = bf16[768,768]{1,0:T(8,128)(2,1)} fusion(f32[576]{0:T(1024)S(1)} %add_reduce_fusion, bf16[576,896]{1,0:T(8,128)(2,1)} %bitcast.18, f32[576,768]{1,0:T(8,128)S(1)} %copy-done.35, f32[576,768]{1,0:T(8,128)S(1)} %fusion.222), kind=kOutput, calls=%fused_computation.88 | convolution fusion | flops 689356800 | bytes 5605632 | tf_op jit(solution)/shard_map/dot_general | solution.py:22
  216.1 4.2 %add_convert_fusion.2 = bf16[576,768]{1,0:T(8,128)(2,1)} fusion(f32[576,768]{1,0:T(8,128)S(1)} %copy-done.89, f32[576,768]{1,0:T(8,128)S(1)} %fusion.85, f32[576,768]{1,0:T(8,128)S(1)} %copy-done.90, bf16[768,768]{1,0:T(8,128)(2,1)} %collective-permute-done.8, f32[576,768]{1,0:T(8,128)S(1)} %copy-done.35, f32[576,768]{1,0:T(8,128)S(1)} %fusion.222), kind=kOutput, calls=%fused_computation.70 | convolution fusion | flops 690094080 | bytes 10911744 | tf_op jit(solution)/shard_map/dot_general | solution.py:28
  220.6 4.0 add_convert_fusion
  224.6 5.7 %all-to-all-done.2 = bf16[8,72,768]{2,1,0:T(8,128)(2,1)} async-done(((bf16[8,72,768]{2,1,0:T(8,128)(2,1)}), bf16[8,72,768]{2,1,0:T(8,128)(2,1)}, u32[]{:S(2)}, u32[]{:S(2)}) %all-to-all-start.2) | async-done | bytes 884768 | tf_op jit(solution)/shard_map/all_to_all | solution.py:141
  230.3 4.6 %all-to-all-start.3 = ((bf16[8,72,768]{2,1,0:T(8,128)(2,1)}), bf16[8,72,768]{2,1,0:T(8,128)(2,1)}, u32[]{:S(2)}, u32[]{:S(2)}) async-start(bf16[8,72,768]{2,1,0:T(8,128)(2,1)} %bitcast.237), calls=%async_computation.3 | async-start | bytes 1769472 | tf_op jit(solution)/shard_map/all_to_all | solution.py:141
  235.6 5.5 %add_convert_fusion.1 = bf16[768,768]{1,0:T(8,128)(2,1)} fusion(bf16[768,768]{1,0:T(8,128)(2,1)} %collective-permute-done.17, f32[576]{0:T(1024)S(1)} %add_reduce_fusion, bf16[576,896]{1,0:T(8,128)(2,1)} %bitcast.18, f32[576,768]{1,0:T(8,128)} %copy-done.87, f32[576,768]{1,0:T(8,128)} %fusion.221), kind=kOutput, calls=%fused_computation.36 | convolution fusion | flops 690536448 | bytes 6785280 | tf_op jit(solution)/shard_map/dot_general | solution.py:22
  244.7 2.9 fusion.97
  248.3 8.8 %all-to-all-done.3 = bf16[8,72,768]{2,1,0:T(8,128)(2,1)} async-done(((bf16[8,72,768]{2,1,0:T(8,128)(2,1)}), bf16[8,72,768]{2,1,0:T(8,128)(2,1)}, u32[]{:S(2)}, u32[]{:S(2)}) %all-to-all-start.3) | async-done | bytes 884768 | tf_op jit(solution)/shard_map/all_to_all | solution.py:141
  259.4 2.5 multiply_reduce_fusion.2
  266.4 2.6 convolution_convert_fusion.9
  269.0 2.7 fusion.57
  273.3 3.2 fusion.115
  276.6 7.1 %fusion.49 = bf16[12,64,256]{2,1,0:T(8,128)(2,1)} fusion(f32[12,256,256]{1,2,0:T(8,128)} %fusion.115, f32[12,256]{1,0:T(8,128)S(1)} %log_add_fusion, f32[12,256,256]{1,2,0:T(8,128)} %copy-done.1, bf16[1,256,3,12,64]{1,4,3,2,0:T(8,128)(2,1)} %bitcast.216), kind=kOutput, calls=%fused_computation.97 | convolution fusion | flops 107941120 | bytes 13402112 | tf_op jit(solution)/shard_map/bhqk,bkhd->bqhd/dot_general | solution.py:382
  283.7 7.1 %fusion.52 = bf16[12,64,256]{2,1,0:T(8,128)(2,1)} fusion(f32[12,256,256]{1,2,0:T(8,128)} %fusion.115, f32[12,256]{1,0:T(8,128)S(1)} %log_add_fusion, f32[12,256,256]{1,2,0:T(8,128)} %copy-done.1, bf16[1,256,3,12,64]{1,4,3,2,0:T(8,128)(2,1)} %bitcast.217), kind=kOutput, calls=%fused_computation.98 | convolution fusion | flops 107941120 | bytes 13402112 | tf_op jit(solution)/shard_map/bhqk,bqhd->bkhd/dot_general | solution.py:385
  292.3 3.3 pad_maximum_fusion.1
  295.5 4.7 %copy.82 = bf16[768,1664]{1,0:T(8,128)(2,1)} copy(bf16[768,1664]{0,1:T(8,128)(2,1)} %pad_maximum_fusion.1) | data formatting | bytes 5111808 | tf_op jit(solution)/shard_map/concatenate | solution.py:368
  302.1 2.9 fusion.46
  308.3 2.4 dynamic-slice_bitcast_fusion
  314.8 2.7 concatenate.220
  319.3 4.1 all-to-all-start.4
  328.4 5.5 %all-to-all-done.4 = bf16[8,4,4620]{2,1,0:T(4,128)(2,1)} async-done(((bf16[8,4,4620]{2,1,0:T(4,128)(2,1)}), bf16[8,4,4620]{2,1,0:T(4,128)(2,1)}, u32[]{:S(2)}, u32[]{:S(2)}) %all-to-all-start.4) | async-done | bytes 295712 | tf_op jit(solution)/shard_map/all_to_all | solution.py:141
  337.6 3.6 convert_add_fusion.1
  341.1 3.5 convert_add_fusion.2
  352.8 2.7 fusion.218
  356.4 11.2 %collective-permute-done.30 = bf16[8,1,24,1664]{3,2,1,0:T(8,128)(2,1)S(1)} collective-permute-done((bf16[8,1,24,1664]{3,2,1,0:T(8,128)(2,1)S(1)}, bf16[8,1,24,1664]{3,2,1,0:T(8,128)(2,1)S(1)}, u32[]{:S(2)}, u32[]{:S(2)}) %collective-permute-start.30) | collective-permute-done | bytes 639008 | tf_op jit(solution)/shard_map/ppermute | solution.py:73
  368.5 3.7 all-to-all-start.6
  381.0 8.0 %collective-permute-done.26 = bf16[8,1,24,1536]{3,2,1,0:T(8,128)(2,1)S(1)} collective-permute-done((bf16[8,1,24,1536]{3,2,1,0:T(8,128)(2,1)S(1)}, bf16[8,1,24,1536]{3,2,1,0:T(8,128)(2,1)S(1)}, u32[]{:S(2)}, u32[]{:S(2)}) %collective-permute-start.26) | collective-permute-done | bytes 589856 | tf_op jit(solution)/shard_map/ppermute | solution.py:73
  390.0 5.7 %all-to-all-start.5 = ((bf16[8,24,1536]{2,1,0:T(8,128)(2,1)}), bf16[8,24,1536]{2,1,0:T(8,128)(2,1)}, u32[]{:S(2)}, u32[]{:S(2)}) async-start(bf16[8,24,1536]{2,1,0:T(8,128)(2,1)} %fusion.114), calls=%async_computation.5 | async-start | bytes 1179648 | tf_op jit(solution)/shard_map/all_to_all | solution.py:141
  402.4 7.2 %all-to-all-done.5 = bf16[8,24,1536]{2,1,0:T(8,128)(2,1)} async-done(((bf16[8,24,1536]{2,1,0:T(8,128)(2,1)}), bf16[8,24,1536]{2,1,0:T(8,128)(2,1)}, u32[]{:S(2)}, u32[]{:S(2)}) %all-to-all-start.5) | async-done | bytes 589856 | tf_op jit(solution)/shard_map/all_to_all | solution.py:141
  (379 shorter events, 121.7 us)
Async XLA Ops:
  0.7 168.9 %collective-permute-start.5 = (bf16[768,768]{1,0:T(8,128)(2,1)}, bf16[768,768]{1,0:T(8,128)(2,1)}, u32[]{:S(2)}, u32[]{:S(2)}) collective-permute-start(bf16[768,768]{1,0:T(8,128)(2,1)} %bitcast.233), channel_id=1, source_target_pairs={{0,1},{1,0},{2,3},{3,2},{4,5},{5,4},{6,7},{7,6},{8,9},{9,8},{10,11... | collective-permute-start | bytes 3538952 | tf_op jit(solution)/shard_map/ppermute | solution.py:73
  1.2 78.2 %collective-permute-start.4 = (bf16[768,768]{1,0:T(8,128)(2,1)}, bf16[768,768]{1,0:T(8,128)(2,1)}, u32[]{:S(2)}, u32[]{:S(2)}) collective-permute-start(bf16[768,768]{1,0:T(8,128)(2,1)} %bitcast.234), channel_id=1, source_target_pairs={{0,2},{1,3},{2,0},{3,1},{4,6},{5,7},{6,4},{7,5},{8,10},{9,11},{10,... | collective-permute-start | bytes 3538952 | tf_op jit(solution)/shard_map/ppermute | solution.py:73
  11.6 10.9 %copy-start.54 = (f32[768]{0:T(1024)}, f32[768]{0:T(1024)S(1)}, u32[]{:S(2)}) copy-start(f32[768]{0:T(1024)S(1)} %get-tuple-element.91) | copy-start | bytes 9220
  11.6 293.5 %copy-start.44 = (f32[768]{0:T(1024)}, f32[768]{0:T(1024)S(1)}, u32[]{:S(2)}) copy-start(f32[768]{0:T(1024)S(1)} %get-tuple-element.92) | copy-start | bytes 9220
  12.4 38.1 %collective-permute-start.10 = (bf16[256,768]{1,0:T(8,128)(2,1)}, bf16[256,768]{1,0:T(8,128)(2,1)}, u32[]{:S(2)}, u32[]{:S(2)}) collective-permute-start(bf16[256,768]{1,0:T(8,128)(2,1)} %fusion.66), channel_id=1, source_target_pairs={{0,2},{1,3},{2,0},{3,1},{4,6},{5,7},{6,4},{7,5},{8,10},{9,11},{10,... | collective-permute-start | bytes 1179656 | tf_op jit(solution)/shard_map/ppermute | solution.py:73
  13.1 8.9 %copy-start.5 = (bf16[256,768]{1,0:T(8,128)(2,1)S(1)}, bf16[256,768]{1,0:T(8,128)(2,1)}, u32[]{:S(2)}) copy-start(bf16[256,768]{1,0:T(8,128)(2,1)} %param.18) | copy-start | bytes 1179652
  15.8 66.3 %all-to-all-start = ((bf16[8,72,768]{2,1,0:T(8,128)(2,1)}), bf16[8,72,768]{2,1,0:T(8,128)(2,1)}, u32[]{:S(2)}, u32[]{:S(2)}) async-start(bf16[8,72,768]{2,1,0:T(8,128)(2,1)} %bitcast.236), calls=%async_computation | async-start | bytes 1769472 | tf_op jit(solution)/shard_map/all_to_all | solution.py:141
  22.1 64.9 %collective-permute-start.6 = (bf16[768,768]{1,0:T(8,128)(2,1)}, bf16[768,768]{1,0:T(8,128)(2,1)}, u32[]{:S(2)}, u32[]{:S(2)}) collective-permute-start(bf16[768,768]{1,0:T(8,128)(2,1)} %bitcast.16), channel_id=1, source_target_pairs={{0,1},{1,0},{2,3},{3,2},{4,5},{5,4},{6,7},{7,6},{8,9},{9,8},{10,11... | collective-permute-start | bytes 3538952 | tf_op jit(solution)/shard_map/ppermute | solution.py:73
  22.2 282.8 %copy-start.47 = (f32[256]{0:T(256)}, f32[256]{0:T(256)S(1)}, u32[]{:S(2)}) copy-start(f32[256]{0:T(256)S(1)} %broadcast_multiply_fusion.5) | copy-start | bytes 3076
  35.6 31.9 %copy-start.9 = (bf16[256,768]{1,0:T(8,128)(2,1)}, bf16[256,768]{1,0:T(8,128)(2,1)S(1)}, u32[]{:S(2)}) copy-start(bf16[256,768]{1,0:T(8,128)(2,1)S(1)} %add_convert_fusion.7) | copy-start | bytes 1179652
  35.6 11.8 %collective-permute-start = (bf16[256,768]{1,0:T(8,128)(2,1)S(1)}, bf16[256,768]{1,0:T(8,128)(2,1)S(1)}, u32[]{:S(2)}, u32[]{:S(2)}) collective-permute-start(bf16[256,768]{1,0:T(8,128)(2,1)S(1)} %add_convert_fusion.7), channel_id=1, source_target_pairs={{0,2},{1,3},{2,0},{3,1},{4,6},{5,7},{6,4},{7,5},{8,10},{9,11},{10,... | collective-permute-start | bytes 1179656 | tf_op jit(solution)/shard_map/ppermute | solution.py:73
  49.1 8.5 %collective-permute-start.1 = (bf16[512,768]{1,0:T(8,128)(2,1)}, bf16[512,768]{1,0:T(8,128)(2,1)}, u32[]{:S(2)}, u32[]{:S(2)}) collective-permute-start(bf16[512,768]{1,0:T(8,128)(2,1)} %pad_maximum_fusion.5), channel_id=1, source_target_pairs={{0,1},{1,0},{2,3},{3,2},{4,5},{5,4},{6,7},{7,6},{8,9},{9,8},{10,11... | collective-permute-start | bytes 2359304 | tf_op jit(solution)/shard_map/ppermute | solution.py:73
  52.5 7.7 %collective-permute-start.11 = (bf16[512,768]{1,0:T(8,128)(2,1)}, bf16[512,768]{1,0:T(8,128)(2,1)}, u32[]{:S(2)}, u32[]{:S(2)}) collective-permute-start(bf16[512,768]{1,0:T(8,128)(2,1)} %pad_maximum_fusion.6), channel_id=1, source_target_pairs={{0,1},{1,0},{2,3},{3,2},{4,5},{5,4},{6,7},{7,6},{8,9},{9,8},{10,11... | collective-permute-start | bytes 2359304 | tf_op jit(solution)/shard_map/ppermute | solution.py:73
  71.8 37.5 %collective-permute-start.22 = (bf16[4,2,96,768]{3,2,1,0:T(8,128)(2,1)}, bf16[4,2,96,768]{3,2,1,0:T(8,128)(2,1)}, u32[]{:S(2)}, u32[]{:S(2)}) collective-permute-start(bf16[4,2,96,768]{3,2,1,0:T(8,128)(2,1)} %fusion.55), channel_id=1, source_target_pairs={{0,4},{4,0},{8,12},{12,8},{16,20},{20,16},{24,28},{28,24},{1,5},{5... | collective-permute-start | bytes 3538952 | tf_op jit(solution)/shard_map/ppermute | solution.py:73
  78.0 33.8 %collective-permute-start.2 = (bf16[512,768]{1,0:T(8,128)(2,1)}, bf16[512,768]{1,0:T(8,128)(2,1)}, u32[]{:S(2)}, u32[]{:S(2)}) collective-permute-start(bf16[512,768]{1,0:T(8,128)(2,1)} %slice.301), channel_id=1, source_target_pairs={{0,1},{1,0},{2,3},{3,2},{4,5},{5,4},{6,7},{7,6},{8,9},{9,8},{10,11... | collective-permute-start | bytes 2359304 | tf_op jit(solution)/shard_map/ppermute | solution.py:73
  79.4 50.1 %collective-permute-start.7 = (bf16[768,768]{1,0:T(8,128)(2,1)}, bf16[768,768]{1,0:T(8,128)(2,1)}, u32[]{:S(2)}, u32[]{:S(2)}) collective-permute-start(bf16[768,768]{1,0:T(8,128)(2,1)} %bitcast.16), channel_id=1, source_target_pairs={{0,2},{1,3},{2,0},{3,1},{4,6},{5,7},{6,4},{7,5},{8,10},{9,11},{10,... | collective-permute-start | bytes 3538952 | tf_op jit(solution)/shard_map/ppermute | solution.py:73
  82.1 63.9 %all-to-all-start.1 = ((bf16[8,72,896]{2,1,0:T(8,128)(2,1)}), bf16[8,72,896]{2,1,0:T(8,128)(2,1)}, u32[]{:S(2)}, u32[]{:S(2)}) async-start(bf16[8,72,896]{2,1,0:T(8,128)(2,1)} %bitcast.235), calls=%async_computation.1 | async-start | bytes 2064384 | tf_op jit(solution)/shard_map/all_to_all | solution.py:141
  86.9 27.9 %collective-permute-start.12 = (bf16[512,768]{1,0:T(8,128)(2,1)}, bf16[512,768]{1,0:T(8,128)(2,1)S(1)}, u32[]{:S(2)}, u32[]{:S(2)}) collective-permute-start(bf16[512,768]{1,0:T(8,128)(2,1)} %slice.300), channel_id=1, source_target_pairs={{0,1},{1,0},{2,3},{3,2},{4,5},{5,4},{6,7},{7,6},{8,9},{9,8},{10,11... | collective-permute-start | bytes 2359304 | tf_op jit(solution)/shard_map/ppermute | solution.py:73
  109.3 40.4 %collective-permute-start.8 = (bf16[768,768]{1,0:T(8,128)(2,1)}, bf16[768,768]{1,0:T(8,128)(2,1)}, u32[]{:S(2)}, u32[]{:S(2)}) collective-permute-start(bf16[768,768]{1,0:T(8,128)(2,1)} %collective-permute-done.4), channel_id=1, source_target_pairs={{0,1},{1,0},{2,3},{3,2},{4,5},{5,4},{6,7},{7,6},{8,9},{9,8},{10,11... | collective-permute-start | bytes 3538952 | tf_op jit(solution)/shard_map/ppermute | solution.py:73
  111.8 15.8 %collective-permute-start.23 = (bf16[2,2,96,768]{3,2,1,0:T(8,128)(2,1)S(1)}, bf16[2,2,96,768]{3,2,1,0:T(8,128)(2,1)S(1)}, u32[]{:S(2)}, u32[]{:S(2)}) collective-permute-start(bf16[2,2,96,768]{3,2,1,0:T(8,128)(2,1)S(1)} %fusion.113), channel_id=1, source_target_pairs={{0,8},{4,12},{8,0},{12,4},{16,24},{20,28},{24,16},{28,20},{1,9},{5... | collective-permute-start | bytes 1769480 | tf_op jit(solution)/shard_map/ppermute | solution.py:73
  114.9 128.3 %collective-permute-start.3 = (bf16[256,768]{1,0:T(8,128)(2,1)}, bf16[256,768]{1,0:T(8,128)(2,1)}, u32[]{:S(2)}, u32[]{:S(2)}) collective-permute-start(bf16[256,768]{1,0:T(8,128)(2,1)} %slice.303), channel_id=1, source_target_pairs={{0,2},{1,3},{2,0},{3,1},{4,6},{5,7},{6,4},{7,5},{8,10},{9,11},{10,... | collective-permute-start | bytes 1179656 | tf_op jit(solution)/shard_map/ppermute | solution.py:73
  116.7 12.8 %copy-start.26 = (f32[512,768]{1,0:T(8,128)}, f32[512,768]{1,0:T(8,128)S(1)}, u32[]{:S(2)}) copy-start(f32[512,768]{1,0:T(8,128)S(1)} %slice_add_fusion) | copy-start | bytes 4718596
  127.6 131.7 %collective-permute-start.13 = (bf16[256,768]{1,0:T(8,128)(2,1)}, bf16[256,768]{1,0:T(8,128)(2,1)}, u32[]{:S(2)}, u32[]{:S(2)}) collective-permute-start(bf16[256,768]{1,0:T(8,128)(2,1)} %slice.302), channel_id=1, source_target_pairs={{0,2},{1,3},{2,0},{3,1},{4,6},{5,7},{6,4},{7,5},{8,10},{9,11},{10,... | collective-permute-start | bytes 1179656 | tf_op jit(solution)/shard_map/ppermute | solution.py:73
  129.6 15.6 %collective-permute-start.24 = (bf16[1,2,96,768]{3,2,1,0:T(8,128)(2,1)S(1)}, bf16[1,2,96,768]{3,2,1,0:T(8,128)(2,1)S(1)}, u32[]{:S(2)}, u32[]{:S(2)}) collective-permute-start(bf16[1,2,96,768]{3,2,1,0:T(8,128)(2,1)S(1)} %dynamic-slice_convert_fusion.5), channel_id=1, source_target_pairs={{0,16},{4,20},{8,24},{12,28},{16,0},{20,4},{24,8},{28,12},{1,17},{... | collective-permute-start | bytes 884744 | tf_op jit(solution)/shard_map/ppermute | solution.py:73
  145.1 53.0 %collective-permute-start.9 = (bf16[768,768]{1,0:T(8,128)(2,1)}, bf16[768,768]{1,0:T(8,128)(2,1)}, u32[]{:S(2)}, u32[]{:S(2)}) collective-permute-start(bf16[768,768]{1,0:T(8,128)(2,1)} %collective-permute-done.7), channel_id=1, source_target_pairs={{0,1},{1,0},{2,3},{3,2},{4,5},{5,4},{6,7},{7,6},{8,9},{9,8},{10,11... | collective-permute-start | bytes 3538952 | tf_op jit(solution)/shard_map/ppermute | solution.py:73
  152.0 46.1 %copy-start.34 = (f32[576,768]{1,0:T(8,128)}, f32[576,768]{1,0:T(8,128)S(1)}, u32[]{:S(2)}) copy-start(f32[576,768]{1,0:T(8,128)S(1)} %fusion.131) | copy-start | bytes 5308420
  156.4 64.0 %collective-permute-start.20 = (bf16[768,768]{1,0:T(8,128)(2,1)}, bf16[768,768]{1,0:T(8,128)(2,1)}, u32[]{:S(2)}, u32[]{:S(2)}) collective-permute-start(bf16[768,768]{1,0:T(8,128)(2,1)} %convolution_convert_fusion.3), channel_id=1, source_target_pairs={{0,1},{1,0},{2,3},{3,2},{4,5},{5,4},{6,7},{7,6},{8,9},{9,8},{10,11... | collective-permute-start | bytes 3538952 | tf_op jit(solution)/shard_map/ppermute | solution.py:73
  161.7 19.2 %copy-start.87 = (f32[576,768]{1,0:T(8,128)}, f32[576,768]{1,0:T(8,128)S(1)}, u32[]{:S(2)}) copy-start(f32[576,768]{1,0:T(8,128)S(1)} %fusion.133) | copy-start | bytes 5308420
  169.5 16.3 %copy-start.7 = (f32[576,768]{1,0:T(8,128)}, f32[576,768]{1,0:T(8,128)S(1)}, u32[]{:S(2)}) copy-start(f32[576,768]{1,0:T(8,128)S(1)} %fusion.24) | copy-start | bytes 5308420
  176.6 160.9 %collective-permute-start.19 = (bf16[768,768]{1,0:T(8,128)(2,1)}, bf16[768,768]{1,0:T(8,128)(2,1)}, u32[]{:S(2)}, u32[]{:S(2)}) collective-permute-start(bf16[768,768]{1,0:T(8,128)(2,1)} %convolution_convert_fusion.4), channel_id=1, source_target_pairs={{0,1},{1,0},{2,3},{3,2},{4,5},{5,4},{6,7},{7,6},{8,9},{9,8},{10,11... | collective-permute-start | bytes 3538952 | tf_op jit(solution)/shard_map/ppermute | solution.py:73
  201.5 28.7 %all-to-all-start.2 = ((bf16[8,72,768]{2,1,0:T(8,128)(2,1)}), bf16[8,72,768]{2,1,0:T(8,128)(2,1)}, u32[]{:S(2)}, u32[]{:S(2)}) async-start(bf16[8,72,768]{2,1,0:T(8,128)(2,1)} %bitcast.218), calls=%async_computation.2 | async-start | bytes 1769472 | tf_op jit(solution)/shard_map/all_to_all | solution.py:141
  214.1 20.9 %collective-permute-start.17 = (bf16[768,768]{1,0:T(8,128)(2,1)}, bf16[768,768]{1,0:T(8,128)(2,1)}, u32[]{:S(2)}, u32[]{:S(2)}) collective-permute-start(bf16[768,768]{1,0:T(8,128)(2,1)} %convolution_convert_fusion.5), channel_id=1, source_target_pairs={{0,1},{1,0},{2,3},{3,2},{4,5},{5,4},{6,7},{7,6},{8,9},{9,8},{10,11... | collective-permute-start | bytes 3538952 | tf_op jit(solution)/shard_map/ppermute | solution.py:73
  220.4 120.8 %collective-permute-start.16 = (bf16[768,768]{1,0:T(8,128)(2,1)}, bf16[768,768]{1,0:T(8,128)(2,1)}, u32[]{:S(2)}, u32[]{:S(2)}) collective-permute-start(bf16[768,768]{1,0:T(8,128)(2,1)} %convolution_convert_fusion.6), channel_id=1, source_target_pairs={{0,1},{1,0},{2,3},{3,2},{4,5},{5,4},{6,7},{7,6},{8,9},{9,8},{10,11... | collective-permute-start | bytes 3538952 | tf_op jit(solution)/shard_map/ppermute | solution.py:73
  230.3 26.8 %all-to-all-start.3 = ((bf16[8,72,768]{2,1,0:T(8,128)(2,1)}), bf16[8,72,768]{2,1,0:T(8,128)(2,1)}, u32[]{:S(2)}, u32[]{:S(2)}) async-start(bf16[8,72,768]{2,1,0:T(8,128)(2,1)} %bitcast.237), calls=%async_computation.3 | async-start | bytes 1769472 | tf_op jit(solution)/shard_map/all_to_all | solution.py:141
  234.9 6.1 %copy-start.23 = (bf16[256,576]{1,0:T(8,128)(2,1)S(1)}, bf16[256,576]{1,0:T(8,128)(2,1)}, u32[]{:S(2)}) copy-start(bf16[256,576]{1,0:T(8,128)(2,1)} %copy-done.22) | copy-start | bytes 884740
  235.0 102.6 %collective-permute-start.21 = (bf16[768,768]{1,0:T(8,128)(2,1)}, bf16[768,768]{1,0:T(8,128)(2,1)}, u32[]{:S(2)}, u32[]{:S(2)}) collective-permute-start(bf16[768,768]{1,0:T(8,128)(2,1)} %add_convert_fusion), channel_id=1, source_target_pairs={{0,2},{1,3},{2,0},{3,1},{4,6},{5,7},{6,4},{7,5},{8,10},{9,11},{10,... | collective-permute-start | bytes 3538952 | tf_op jit(solution)/shard_map/ppermute | solution.py:73
  243.1 98.0 %collective-permute-start.18 = (bf16[768,768]{1,0:T(8,128)(2,1)}, bf16[768,768]{1,0:T(8,128)(2,1)}, u32[]{:S(2)}, u32[]{:S(2)}) collective-permute-start(bf16[768,768]{1,0:T(8,128)(2,1)} %add_convert_fusion.1), channel_id=1, source_target_pairs={{0,2},{1,3},{2,0},{3,1},{4,6},{5,7},{6,4},{7,5},{8,10},{9,11},{10,... | collective-permute-start | bytes 3538952 | tf_op jit(solution)/shard_map/ppermute | solution.py:73
  247.7 11.7 %copy-start.49 = (f32[256]{0:T(256)S(1)}, f32[256]{0:T(256)}, u32[]{:S(2)}) copy-start(f32[256]{0:T(256)} %copy-done.48) | copy-start | bytes 3076
  247.7 11.7 %copy-start.58 = (bf16[768,8]{0,1:T(8,128)(2,1)S(1)}, bf16[768,8]{0,1:T(8,128)(2,1)}, u32[]{:S(2)}) copy-start(bf16[768,8]{0,1:T(8,128)(2,1)} %param.31) | copy-start | bytes 36868
  247.7 11.7 %copy-start.63 = (f32[256]{0:T(256)S(1)}, f32[256]{0:T(256)}, u32[]{:S(2)}) copy-start(f32[256]{0:T(256)} %copy-done.62) | copy-start | bytes 3076
  283.6 7.2 %copy-start.70 = (bf16[768]{0:T(1024)(128)(2,1)S(1)}, bf16[768]{0:T(1024)(128)(2,1)}, u32[]{:S(2)}) copy-start(bf16[768]{0:T(1024)(128)(2,1)} %get-tuple-element.86) | copy-start | bytes 4612
  283.7 7.2 %copy-start.10 = (bf16[256,768]{1,0:T(8,128)(2,1)S(1)}, bf16[256,768]{1,0:T(8,128)(2,1)}, u32[]{:S(2)}) copy-start(bf16[256,768]{1,0:T(8,128)(2,1)} %copy-done.9) | copy-start | bytes 1179652
  283.7 7.2 %copy-start.53 = (bf16[256,8]{0,1:T(8,128)(2,1)S(1)}, bf16[256,8]{0,1:T(8,128)(2,1)}, u32[]{:S(2)}) copy-start(bf16[256,8]{0,1:T(8,128)(2,1)} %multiply_convert_fusion.20) | copy-start | bytes 12292
  283.7 7.4 %copy-start.80 = (bf16[768]{0:T(1024)(128)(2,1)S(1)}, bf16[768]{0:T(1024)(128)(2,1)}, u32[]{:S(2)}) copy-start(bf16[768]{0:T(1024)(128)(2,1)} %get-tuple-element.78) | copy-start | bytes 4612
  283.7 7.4 %copy-start.69 = (bf16[768]{0:T(1024)(128)(2,1)S(1)}, bf16[768]{0:T(1024)(128)(2,1)}, u32[]{:S(2)}) copy-start(bf16[768]{0:T(1024)(128)(2,1)} %get-tuple-element.99) | copy-start | bytes 4612
  283.7 8.0 %copy-start.79 = (bf16[768]{0:T(1024)(128)(2,1)S(1)}, bf16[768]{0:T(1024)(128)(2,1)}, u32[]{:S(2)}) copy-start(bf16[768]{0:T(1024)(128)(2,1)} %get-tuple-element.84) | copy-start | bytes 4612
  307.7 4.0 collective-permute-start.14
  311.7 1.3 collective-permute-start.15
  313.0 36.0 %collective-permute-start.29 = (bf16[8,2,24,1664]{3,2,1,0:T(8,128)(2,1)}, bf16[8,2,24,1664]{3,2,1,0:T(8,128)(2,1)}, u32[]{:S(2)}, u32[]{:S(2)}) collective-permute-start(bf16[8,2,24,1664]{3,2,1,0:T(8,128)(2,1)} %dynamic-slice_bitcast_fusion), channel_id=1, source_target_pairs={{0,1},{1,0},{2,3},{3,2},{4,5},{5,4},{6,7},{7,6},{8,9},{9,8},{10,11... | collective-permute-start | bytes 3833864 | tf_op jit(solution)/shard_map/ppermute | solution.py:73
  317.5 9.2 %copy-start.45 = (f32[768]{0:T(1024)S(1)}, f32[768]{0:T(1024)}, u32[]{:S(2)}) copy-start(f32[768]{0:T(1024)} %copy-done.44) | copy-start | bytes 9220
  319.3 14.6 %all-to-all-start.4 = ((bf16[8,4,4620]{2,1,0:T(4,128)(2,1)}), bf16[8,4,4620]{2,1,0:T(4,128)(2,1)}, u32[]{:S(2)}, u32[]{:S(2)}) async-start(bf16[8,4,4620]{2,1,0:T(4,128)(2,1)} %all_to_all.64), calls=%async_computation.4 | async-start | bytes 606208 | tf_op jit(solution)/shard_map/all_to_all | solution.py:141
  326.0 9.5 %copy-start.82 = (f32[128]{0:T(128)S(1)}, f32[128]{0:T(128)}, u32[]{:S(2)}) copy-start(f32[128]{0:T(128)} %multiply_exponential_fusion) | copy-start | bytes 1540
  326.0 9.7 %copy-start.52 = (f32[768]{0:T(1024)S(1)}, f32[768]{0:T(1024)}, u32[]{:S(2)}) copy-start(f32[768]{0:T(1024)} %param.25) | copy-start | bytes 9220
  344.7 8.1 %slice-start = ((s8[7077888]{0:T(1024)(128)(4,1)}), s8[4194304]{0:T(1024)(128)(4,1)S(1)}, s32[]{:S(2)}) async-start(s8[7077888]{0:T(1024)(128)(4,1)} %bitcast.205), calls=%async_computation.7 | async-start | bytes 8388608
  349.0 23.2 %collective-permute-start.25 = (bf16[8,2,24,1536]{3,2,1,0:T(8,128)(2,1)}, bf16[8,2,24,1536]{3,2,1,0:T(8,128)(2,1)}, u32[]{:S(2)}, u32[]{:S(2)}) collective-permute-start(bf16[8,2,24,1536]{3,2,1,0:T(8,128)(2,1)} %fusion.56), channel_id=1, source_target_pairs={{0,1},{1,0},{2,3},{3,2},{4,5},{5,4},{6,7},{7,6},{8,9},{9,8},{10,11... | collective-permute-start | bytes 3538952 | tf_op jit(solution)/shard_map/ppermute | solution.py:73
  351.2 16.4 %collective-permute-start.30 = (bf16[8,1,24,1664]{3,2,1,0:T(8,128)(2,1)S(1)}, bf16[8,1,24,1664]{3,2,1,0:T(8,128)(2,1)S(1)}, u32[]{:S(2)}, u32[]{:S(2)}) collective-permute-start(bf16[8,1,24,1664]{3,2,1,0:T(8,128)(2,1)S(1)} %dynamic-slice_convert_fusion.2), channel_id=1, source_target_pairs={{0,2},{1,3},{2,0},{3,1},{4,6},{5,7},{6,4},{7,5},{8,10},{9,11},{10,... | collective-permute-start | bytes 1916936 | tf_op jit(solution)/shard_map/ppermute | solution.py:73
  368.5 21.4 %all-to-all-start.6 = ((bf16[8,24,1664]{2,1,0:T(8,128)(2,1)}), bf16[8,24,1664]{2,1,0:T(8,128)(2,1)S(1)}, u32[]{:S(2)}, u32[]{:S(2)}) async-start(bf16[8,24,1664]{2,1,0:T(8,128)(2,1)} %fusion.112), calls=%async_computation.6 | async-start | bytes 1277952 | tf_op jit(solution)/shard_map/all_to_all | solution.py:141
  374.7 14.3 %collective-permute-start.26 = (bf16[8,1,24,1536]{3,2,1,0:T(8,128)(2,1)S(1)}, bf16[8,1,24,1536]{3,2,1,0:T(8,128)(2,1)S(1)}, u32[]{:S(2)}, u32[]{:S(2)}) collective-permute-start(bf16[8,1,24,1536]{3,2,1,0:T(8,128)(2,1)S(1)} %dynamic-slice_convert_fusion.3), channel_id=1, source_target_pairs={{0,2},{1,3},{2,0},{3,1},{4,6},{5,7},{6,4},{7,5},{8,10},{9,11},{10,... | collective-permute-start | bytes 1769480 | tf_op jit(solution)/shard_map/ppermute | solution.py:73
  381.0 16.9 %copy-start.29 = (f32[2,96,768]{2,1,0:T(8,128)S(1)}, f32[2,96,768]{2,1,0:T(8,128)}, u32[]{:S(2)}) copy-start(f32[2,96,768]{2,1,0:T(8,128)} %add_bitcast_fusion) | copy-start | bytes 1769476
  390.0 19.7 %all-to-all-start.5 = ((bf16[8,24,1536]{2,1,0:T(8,128)(2,1)}), bf16[8,24,1536]{2,1,0:T(8,128)(2,1)}, u32[]{:S(2)}, u32[]{:S(2)}) async-start(bf16[8,24,1536]{2,1,0:T(8,128)(2,1)} %fusion.114), calls=%async_computation.5 | async-start | bytes 1179648 | tf_op jit(solution)/shard_map/all_to_all | solution.py:141
  396.3 4.5 %collective-permute-start.31 = (bf16[24,1664]{1,0:T(8,128)(2,1)S(1)}, bf16[24,1664]{1,0:T(8,128)(2,1)S(1)}, u32[]{:S(2)}, u32[]{:S(2)}) collective-permute-start(bf16[24,1664]{1,0:T(8,128)(2,1)S(1)} %reduce_sum.254), channel_id=1, source_target_pairs={{0,2},{1,3},{2,0},{3,1},{4,6},{5,7},{6,4},{7,5},{8,10},{9,11},{10,... | collective-permute-start | bytes 239624 | tf_op jit(solution)/shard_map/ppermute | solution.py:73
  400.8 1.5 collective-permute-start.32
  410.8 4.4 %collective-permute-start.27 = (bf16[24,1536]{1,0:T(8,128)(2,1)S(1)}, bf16[24,1536]{1,0:T(8,128)(2,1)S(1)}, u32[]{:S(2)}, u32[]{:S(2)}) collective-permute-start(bf16[24,1536]{1,0:T(8,128)(2,1)S(1)} %reduce_sum.253), channel_id=1, source_target_pairs={{0,2},{1,3},{2,0},{3,1},{4,6},{5,7},{6,4},{7,5},{8,10},{9,11},{10,... | collective-permute-start | bytes 221192 | tf_op jit(solution)/shard_map/ppermute | solution.py:73
  415.2 1.4 collective-permute-start.28
  (69 other events, 221.2 us)

commit v3 on v2

v3 whole, which is shorter than its diff:
```python
import functools
import math

import jax
import jax.numpy as jnp
from jax import lax
from jax.experimental import pallas as pl
from jax.experimental.pallas import tpu as pltpu
from jax.sharding import PartitionSpec as P

HEADS = 12
HDIM = 64
SEQ = 256


eps_norm = 1e-06
highest = lax.Precision.HIGHEST


def mat_prod(left_side, right_side):
    return jnp.dot(left_side, right_side, preferred_element_type=jnp.float32)


def prod_rows(left_side, right_side):
    return lax.dot_general(
        left_side, right_side, (((0,), (0,)), ((), ())), preferred_element_type=jnp.float32
    )


def prod_cols(left_side, right_side):
    return lax.dot_general(
        left_side, right_side, (((1,), (1,)), ((), ())), preferred_element_type=jnp.float32
    )


def sinus_table(timesteps, columns):
    half_cols = columns // 2
    freqs = jnp.exp(-math.log(10000.0) * jnp.arange(half_cols, dtype=jnp.float32) / half_cols)
    angles = timesteps.astype(jnp.float32)[:, None] * freqs[None, :]
    return jnp.concatenate([jnp.cos(angles), jnp.sin(angles)], axis=1)


def normalize(inputs):
    center = inputs - jnp.mean(inputs, axis=-1, keepdims=True)
    inverse = lax.rsqrt(jnp.mean(center * center, axis=-1, keepdims=True) + eps_norm)
    return (center * inverse, inverse)


def normalize_back(normed, inverse, grad_normed):
    return inverse * (
        grad_normed
        - jnp.mean(grad_normed, axis=-1, keepdims=True)
        - normed * jnp.mean(grad_normed * normed, axis=-1, keepdims=True)
    )


def pairs_of(size, mask):
    return [(index, index ^ mask) for index in range(size)]


def swap(values, axis, mask):
    return lax.ppermute(values, axis, pairs_of(lax.axis_size(axis), mask))


def low(values):
    return values.astype(jnp.bfloat16)


def bits_of(axis):
    masks = [1]
    while masks[-1] * 2 < lax.axis_size(axis):
        masks.append(masks[-1] * 2)
    return masks


def gather_hid(own, far):
    masks = bits_of("hid")
    blocks = {0: own, masks[-1]: far}
    for mask in reversed(masks[:-1]):
        for index in list(blocks):
            blocks[index ^ mask] = swap(blocks[index], "hid", mask)
    return [blocks[index] for index in range(lax.axis_size("hid"))]


def gather_rows(own):
    masks = bits_of("hid")
    rows, first = own, own
    for mask in reversed(masks[1:]):
        moved = swap(rows, "hid", mask)
        first = moved if rows is own else first
        rows = jnp.concatenate([rows, moved], axis=0)
    return (rows, swap(rows, "hid", masks[0])), first


def after(values, other):
    seen = other.reshape(-1)[0].astype(jnp.float32)
    return jnp.where(seen == seen, values, jnp.zeros_like(values))


def reduce_rows(halves):
    first = swap(halves[1], "hid", bits_of("hid")[0])
    return halves[0].astype(jnp.float32) + first.astype(jnp.float32), first


def reduce_more(rows):
    for mask in bits_of("hid")[1:]:
        half = rows.shape[0] // 2
        moved = swap(low(rows[half:]), "hid", mask)
        rows = rows[:half] + moved.astype(jnp.float32)
    return rows


def reduce_step(values, axis, step):
    bit = (lax.axis_index(axis) >> step) & 1
    halves = values.reshape((values.shape[0], values.shape[1] // 2, 2) + values.shape[2:])
    kept = lax.dynamic_index_in_dim(halves, bit, 2, keepdims=False)
    sent = lax.dynamic_index_in_dim(halves, 1 - bit, 2, keepdims=False)
    return kept.astype(jnp.float32) + swap(low(sent), axis, 1 << step).astype(jnp.float32)


def spread_rest(values):
    left = values.shape[1]
    if left > 4:
        for step in range(1, len(bits_of("exp"))):
            values = reduce_step(values, "exp", step)
        return [values[:, 0]]
    place = lax.axis_index("exp") >> 1
    parts = [lax.dynamic_index_in_dim(values, place ^ mask, 1, keepdims=False) for mask in range(left)]
    return parts[:1] + [swap(low(parts[mask]), "exp", 2 * mask) for mask in range(1, left)]


def exchange(rows):
    return lax.all_to_all(rows, "exp", split_axis=0, concat_axis=0, tiled=True)


def join_hid(own):
    place = lax.axis_index("hid")
    for step, mask in reversed(list(enumerate(bits_of("hid")))):
        other = swap(own, "hid", mask)
        both = jnp.stack([own, other], axis=0)
        swapped = jnp.stack([other, own], axis=0)
        own = jnp.where((place >> step) & 1 == 0, both, swapped)
    depth = len(bits_of("hid"))
    own = jnp.transpose(own, tuple(reversed(range(depth))) + tuple(range(depth, own.ndim)))
    return own.reshape((-1,) + own.shape[depth + 1 :])


def gather_items(own, gate):
    count = own.shape[0]
    width = lax.axis_size("hid")
    rows, offsets = own, [0]
    for axis, weight in (("exp", width), ("hid", 1)):
        for mask in bits_of(axis):
            rows = jnp.concatenate([rows, swap(rows, axis, mask)], axis=0)
            offsets = offsets + [offset ^ (mask * weight) for offset in offsets]
        if axis == "exp":
            rows, gate = lax.optimization_barrier((rows, gate))
    place = lax.axis_index("exp") * width + lax.axis_index("hid")
    part = jnp.arange(len(offsets) * count, dtype=jnp.int32)
    source = (jnp.repeat(jnp.array(offsets, jnp.int32), count) ^ place) * count + part % count
    return low(mat_prod(low(source[None, :] == part[:, None]), rows)), gate


def sum_hid(partial, gates):
    size = lax.axis_size("exp")
    width = lax.axis_size("hid")
    columns = partial.shape[1]
    share = partial.shape[0] // (size * width)
    values = partial.reshape(size, width, share, columns)
    place = lax.axis_index("hid")
    masks = bits_of("hid")
    for step, mask in enumerate(masks):
        bit = (place >> step) & 1
        halves = values.reshape(size, values.shape[1] // 2, 2, share, columns)
        kept = lax.dynamic_index_in_dim(halves, bit, 2, keepdims=False)
        sent = low(lax.dynamic_index_in_dim(halves, 1 - bit, 2, keepdims=False))
        if mask == masks[-1]:
            sent, gates = lax.optimization_barrier((sent, gates))
        values = kept.astype(jnp.float32) + swap(sent, "hid", mask).astype(jnp.float32)
    return low(values).reshape(size * share, columns), gates


def sum_parts(values):
    size = lax.axis_size("exp")
    parts = values.reshape(size, values.shape[0] // size, values.shape[1])
    return join_hid(low(jnp.sum(parts.astype(jnp.float32), axis=0))).astype(jnp.float32)


SMALL_COST = pl.CostEstimate(flops=1000, bytes_accessed=1000, transcendentals=0)


def gelu_pair(pre):
    square = pre * pre
    scale = math.sqrt(2.0 / math.pi)
    bent = jnp.tanh(pre * (scale + (scale * 0.044715) * square))
    half = 0.5 + 0.5 * bent
    slope = half + (0.5 * pre) * (1.0 - bent * bent) * (scale + (3.0 * scale * 0.044715) * square)
    return pre * half, slope


def expert_body(block_count, width, gated, *refs):
    rows_ref, grads_ref = refs[0], refs[1]
    in_refs = refs[2 : 2 + block_count]
    out_refs = refs[2 + block_count : 2 + 2 * block_count]
    rest = refs[2 + 2 * block_count :]
    if gated:
        back_ref, sum_ref, scaled_ref = rest[:3]
        rest = rest[3:]
    else:
        back_ref, sum_ref = rest[:2]
        rest = rest[2:]
    act_refs, slope_refs = rest[:block_count], rest[block_count : 2 * block_count]
    pre_ref, hidden_ref, low_ref, sum_acc, back_acc = rest[2 * block_count :]
    count = rows_ref.shape[0]
    step = 32
    for index in range(block_count):
        pre_ref[...] = mat_prod(rows_ref[:, :width], in_refs[index][...])
        hidden_ref[...] = prod_cols(grads_ref[...], out_refs[index][...])

        def bend(place, carry, index=index):
            span = pl.ds(pl.multiple_of(place * step, step), step)
            act, slope = gelu_pair(pre_ref[span, :])
            back = hidden_ref[span, :] * slope
            act_refs[index][span, :] = low(act)
            if gated:
                low_ref[span, :] = low(back)
                gate = rows_ref[span, width : width + 128].astype(jnp.float32)
                slope_refs[index][span, :] = low(back * (gate[:, 0:1] + gate[:, 1:2]))
            else:
                slope_refs[index][span, :] = low(back)
            return carry

        lax.fori_loop(0, count // step, bend, 0)
        part_sum = mat_prod(act_refs[index][...], out_refs[index][...])
        sent = low_ref if gated else slope_refs[index]
        part_back = prod_cols(sent[...], in_refs[index][...])
        if index == 0:
            sum_acc[...] = part_sum
            back_acc[...] = part_back
        else:
            sum_acc[...] += part_sum
            back_acc[...] += part_back

    def finish(place, carry):
        span = pl.ds(pl.multiple_of(place * step, step), step)
        total = sum_acc[span, :]
        sum_ref[span, :] = low(total)
        back_ref[span, :width] = low(back_acc[span, :])
        if gated:
            grads = grads_ref[span, :].astype(jnp.float32)
            gate = rows_ref[span, width : width + 128].astype(jnp.float32)
            scaled_ref[span, :] = low(grads * (gate[:, 0:1] + gate[:, 1:2]))
            dots = jnp.sum(total * grads, axis=1, keepdims=True)
            high = low(dots).astype(jnp.float32)
            lane = lax.broadcasted_iota(jnp.int32, (step, 128), 1)
            back_ref[span, width : width + 128] = low(
                jnp.where(lane == 0, high, jnp.where(lane == 1, dots - high, 0.0))
            )
        return carry

    lax.fori_loop(0, count // step, finish, 0)


def expert_pass(rows, grads, blocks_in, blocks_out, gated):
    count, width = grads.shape
    hidden = blocks_in[0].shape[1]
    blocks = len(blocks_in)

    def shape(columns):
        return jax.ShapeDtypeStruct((count, columns), jnp.bfloat16)

    outs = [shape(rows.shape[1]), shape(width)] + ([shape(width)] if gated else [])
    outs += [shape(hidden)] * (2 * blocks)
    scratch = [
        pltpu.VMEM((count, hidden), jnp.float32),
        pltpu.VMEM((count, hidden), jnp.float32),
        pltpu.VMEM((count, hidden), jnp.bfloat16),
        pltpu.VMEM((count, width), jnp.float32),
        pltpu.VMEM((count, width), jnp.float32),
    ]
    return pl.pallas_call(
        functools.partial(expert_body, blocks, width, gated),
        out_shape=outs,
        scratch_shapes=scratch,
        cost_estimate=SMALL_COST,
        compiler_params=pltpu.CompilerParams(vmem_limit_bytes=56 * 1024 * 1024),
    )(rows, grads, *blocks_in, *blocks_out)


def outer_body(block_count, width, added, *refs):
    rows_ref, grads_ref = refs[0], refs[1]
    parts = [
        refs[2 + kind * block_count : 2 + (kind + 1) * block_count] for kind in range(6 if added else 4)
    ]
    act_refs, back_refs = parts[:2]
    in_refs, out_refs = parts[-2:]
    for index in range(block_count):
        first = prod_rows(rows_ref[:, :width], back_refs[index][...])
        second = prod_rows(act_refs[index][...], grads_ref[...])
        if added:
            first += parts[2][index][...].astype(jnp.float32)
            second += parts[3][index][...].astype(jnp.float32)
        in_refs[index][...] = low(first)
        out_refs[index][...] = low(second)


def outer_pass(rows, grads, acts, backs, added=()):
    width, hidden, blocks = grads.shape[1], acts[0].shape[1], len(acts)
    outs = [jax.ShapeDtypeStruct((width, hidden), jnp.bfloat16)] * blocks
    outs += [jax.ShapeDtypeStruct((hidden, width), jnp.bfloat16)] * blocks
    made = pl.pallas_call(
        functools.partial(outer_body, blocks, width, bool(added)),
        out_shape=outs,
        cost_estimate=SMALL_COST,
        compiler_params=pltpu.CompilerParams(vmem_limit_bytes=56 * 1024 * 1024),
    )(rows, grads, *acts, *backs, *added)
    return made[:blocks], made[blocks:]


def shared_body(rows_a, rows_b, grads_a, grads_b, act_a, act_b, back_a, back_b, out_ref):
    out_ref[0] = low(prod_rows(rows_a[...], back_a[...]) + prod_rows(rows_b[...], back_b[...]))
    out_ref[1] = low(prod_rows(grads_a[...], act_a[...]) + prod_rows(grads_b[...], act_b[...]))


def shared_outer(*arrays):
    return pl.pallas_call(
        shared_body,
        out_shape=jax.ShapeDtypeStruct((2, arrays[0].shape[1], arrays[4].shape[1]), jnp.bfloat16),
        cost_estimate=SMALL_COST,
        compiler_params=pltpu.CompilerParams(vmem_limit_bytes=56 * 1024 * 1024),
    )(*arrays)


def head_weights(queries, key_rows, score_scale):
    scores = prod_cols(queries, key_rows) * score_scale
    raised = jnp.exp(scores - jnp.max(scores, axis=1, keepdims=True))
    return raised / jnp.sum(raised, axis=1, keepdims=True)


def pair_spans(pair, width):
    return [pl.ds(pl.multiple_of(part * width + pair * 128, 128), 128) for part in range(3)]


def attend_body(score_scale, rows_ref, out_ref):
    width = out_ref.shape[1]
    lane = lax.broadcasted_iota(jnp.int32, (out_ref.shape[0], 128), 1)

    def step(pair, carry):
        at_q, at_k, at_v = pair_spans(pair, width)
        queries, keys, values = rows_ref[:, at_q], rows_ref[:, at_k], rows_ref[:, at_v]
        sides = []
        for side in range(2):
            mine = (lane >= side * HDIM) & (lane < (side + 1) * HDIM)
            weights = head_weights(jnp.where(mine, queries, 0), keys, score_scale)
            sides.append(mat_prod(low(weights), values))
        out_ref[:, at_q] = low(jnp.where(lane < HDIM, sides[0], sides[1]))
        return carry

    lax.fori_loop(0, width // 128, step, 0)


def attend_back_body(score_scale, rows_ref, grad_ref, out_ref):
    width = grad_ref.shape[1]
    lane = lax.broadcasted_iota(jnp.int32, (grad_ref.shape[0], 128), 1)

    def step(pair, carry):
        at_q, at_k, at_v = pair_spans(pair, width)
        queries, keys, values = rows_ref[:, at_q], rows_ref[:, at_k], rows_ref[:, at_v]
        grads = grad_ref[:, at_q]
        to_q, to_k, to_v = [], [], []
        for side in range(2):
            mine = (lane >= side * HDIM) & (lane < (side + 1) * HDIM)
            head_queries, head_grads = jnp.where(mine, queries, 0), jnp.where(mine, grads, 0)
            weights = head_weights(head_queries, keys, score_scale)
            to_v.append(prod_rows(low(weights), head_grads))
            probs = prod_cols(head_grads, values)
            inner = jnp.sum(weights * probs, axis=1, keepdims=True)
            scores = low(weights * (probs - inner) * score_scale)
            to_q.append(mat_prod(scores, keys))
            to_k.append(prod_rows(scores, head_queries))
        out_ref[:, at_q] = low(jnp.where(lane < HDIM, to_q[0], to_q[1]))
        out_ref[:, at_k] = low(to_k[0] + to_k[1])
        out_ref[:, at_v] = low(to_v[0] + to_v[1])
        return carry

    lax.fori_loop(0, width // 128, step, 0)


def attend(body, arrays, columns, score_scale):
    rows = arrays[0].shape[0]
    return pl.pallas_call(
        functools.partial(body, score_scale),
        grid=(rows // SEQ,),
        in_specs=[pl.BlockSpec((SEQ, array.shape[1]), lambda item: (item, 0)) for array in arrays],
        out_specs=pl.BlockSpec((SEQ, columns), lambda item: (item, 0)),
        out_shape=jax.ShapeDtypeStruct((rows, columns), jnp.bfloat16),
        cost_estimate=SMALL_COST,
    )(*arrays)


def condition_of(timesteps, labels, time_weight, time_bias, class_table):
    freq_emb = low(sinus_table(timesteps, time_weight.shape[0]))
    label_hot = low(
        labels[:, None] == jnp.arange(class_table.shape[0], dtype=jnp.int32)[None, :]
    )
    condition = mat_prod(freq_emb, time_weight) + time_bias + mat_prod(label_hot, class_table)
    return freq_emb, label_hot, condition, low(jax.nn.silu(condition))


def per_device(
    patches,
    cotangent,
    timesteps,
    labels,
    routes,
    slot_index,
    time_weight,
    time_bias,
    class_table,
    ada_weight,
    ada_bias,
    qkv_weight,
    proj_weight,
    router_weight,
    shared_in,
    shared_out,
    expert_in,
    expert_out,
):
    tokens, model_dim = patches.shape
    item_count = timesteps.shape[0]
    experts = lax.axis_size("exp")
    place_exp = lax.axis_index("exp")
    capacity = 9 * tokens // (4 * experts)
    slots_all = experts * capacity
    score_scale = 1.0 / math.sqrt(HDIM)

    own_in, own_out = expert_in[0], expert_out[0]
    far_mask = bits_of("hid")[-1]
    far_in = swap(own_in, "hid", far_mask)

    freq_emb, label_hot, condition, silu_cond = condition_of(
        timesteps, labels, time_weight, time_bias, class_table
    )
    modulate = mat_prod(silu_cond, ada_weight) + ada_bias
    shift_one, scale_one, gate_one, shift_two, scale_two, gate_two = [
        modulate[:, None, block_index * model_dim : (block_index + 1) * model_dim]
        for block_index in range(6)
    ]
    grad_result = cotangent.astype(jnp.float32).reshape(item_count, SEQ, model_dim)
    grad_branch = (gate_two * grad_result).reshape(tokens, model_dim)
    grad_branch_low = low(grad_branch)

    first_route, second_route = routes[:, 0:1], routes[:, 1:2]
    kept_first = slot_index[:, 0:1] < capacity
    kept_second = slot_index[:, 1:2] < capacity
    slot_ids = jnp.arange(slots_all, dtype=jnp.int32)[None, :]
    dispatch_first = low(
        (first_route * capacity + slot_index[:, 0:1] == slot_ids) & kept_first
    )
    dispatch_second = low(
        (second_route * capacity + slot_index[:, 1:2] == slot_ids) & kept_second
    )
    dispatch_both = dispatch_first + dispatch_second
    picks = jnp.concatenate([dispatch_first, dispatch_second], axis=0)
    grad_rows = exchange(low(prod_rows(dispatch_both, grad_branch_low)))
    grad_tokens, _ = gather_rows(grad_branch_low)

    residual = patches.astype(jnp.float32).reshape(item_count, SEQ, model_dim)
    normed_one, inverse_one = normalize(residual)
    flat_one = low(normed_one * (1.0 + scale_one) + shift_one).reshape(tokens, model_dim)
    qkv_rows = low(mat_prod(flat_one, qkv_weight))
    qkv_rows, far_in = lax.optimization_barrier((qkv_rows, far_in))
    attended_low = attend(attend_body, [qkv_rows], model_dim, score_scale)
    branch_one = mat_prod(attended_low, proj_weight).reshape(item_count, SEQ, model_dim)
    residual_one = residual + gate_one * branch_one
    normed_two, inverse_two = normalize(residual_one)
    hidden_two = low(normed_two * (1.0 + scale_two) + shift_two).reshape(tokens, model_dim)
    logits = mat_prod(hidden_two, router_weight)
    expert_ids = jnp.arange(experts, dtype=jnp.int32)[None, :]
    first_hot = (first_route == expert_ids).astype(jnp.float32)
    second_hot = (second_route == expert_ids).astype(jnp.float32)
    logit_gap = jnp.sum(logits * first_hot, axis=1) - jnp.sum(logits * second_hot, axis=1)
    gate_first = jax.nn.sigmoid(logit_gap)[:, None]
    gate_second = 1.0 - gate_first

    lane = jnp.arange(128, dtype=jnp.int32)[None, :]

    def gate_lanes(gate):
        high = low(gate).astype(jnp.float32)
        return low(jnp.where(lane == 0, high, jnp.where(lane == 1, gate - high, 0.0)))

    carried = jnp.concatenate(
        [
            jnp.concatenate([hidden_two, hidden_two], axis=0),
            jnp.concatenate([gate_lanes(gate_first), gate_lanes(gate_second)], axis=0),
        ],
        axis=1,
    )
    sent_rows, grad_rows = lax.optimization_barrier((low(prod_rows(picks, carried)), grad_rows))
    received = exchange(sent_rows)
    blocks_in = gather_hid(own_in, far_in)
    tokens_all, first_tokens = gather_rows(hidden_two)
    far_out = swap(after(own_out, first_tokens[:1, :128]), "hid", far_mask)
    blocks_out = gather_hid(own_out, far_out)

    halves = [
        expert_pass(rows, grads, [shared_in], [shared_out], False)
        for rows, grads in zip(tokens_all, grad_tokens)
    ]
    term_part, sum_part, act_shared, back_shared = zip(*halves)
    shared_term = reduce_more(reduce_rows(term_part)[0])
    weight_shared = shared_outer(*tokens_all, *grad_tokens, *act_shared, *back_shared)

    received, weight_shared = lax.optimization_barrier((received, weight_shared))
    share = model_dim // experts
    weight_shared = weight_shared.reshape(2, experts, share, weight_shared.shape[2])
    weight_shared = reduce_step(weight_shared, "exp", 0)
    grad_sent, expert_rows, grad_gated, *kept = expert_pass(
        received, grad_rows, blocks_in, blocks_out, True
    )
    grad_sent, sum_part, weight_shared = lax.optimization_barrier(
        (grad_sent, sum_part, weight_shared)
    )
    shared_sum, first_sum = reduce_rows(sum_part)
    grad_back = exchange(grad_sent)
    grad_gated, first_sum = lax.optimization_barrier((grad_gated, first_sum))
    blocks = list(range(len(blocks_in)))
    shares = {}
    for mask in bits_of("hid")[:-1]:
        here, there = [r for r in blocks if not r & mask], [r for r in blocks if r & mask]
        made = outer_pass(
            received,
            grad_gated,
            [kept[r] for r in there],
            [kept[len(blocks_in) + r] for r in there],
            added=[part for kind in range(2) for part in (shares[kind, r] for r in there)]
            if shares
            else (),
        )
        shares = {
            (kind, r): swap(made[kind][there.index(r | mask)], "hid", mask)
            for kind in range(2)
            for r in here
        }
        blocks = here
    made_in, made_out = outer_pass(
        received,
        grad_gated,
        [kept[r] for r in blocks],
        [kept[len(blocks_in) + r] for r in blocks],
        added=[shares[kind, r] for kind in range(2) for r in blocks],
    )
    (kept_in, sent_in), (kept_out, sent_out) = made_in, made_out
    grad_back, expert_rows, sent_in, sent_out, weight_shared, shared_sum = (
        lax.optimization_barrier(
            (grad_back, expert_rows, sent_in, sent_out, weight_shared, shared_sum)
        )
    )
    shared_sum = reduce_more(shared_sum)
    weight_shared = spread_rest(weight_shared)
    moved_in, moved_out = swap(sent_in, "hid", far_mask), swap(sent_out, "hid", far_mask)
    back_rows = exchange(expert_rows)

    picked_grad = mat_prod(picks, grad_back)
    dots = jnp.sum(picked_grad[:, model_dim:], axis=1)
    picked_grad = picked_grad[:, :model_dim]
    grad_gap = (dots[:tokens] - dots[tokens:])[:, None] * gate_first * gate_second
    grad_logits = low(grad_gap * (first_hot - second_hot))
    grad_hidden = (
        prod_cols(grad_logits, router_weight)
        + shared_term
        + gate_first * picked_grad[:tokens]
        + gate_second * picked_grad[tokens:]
    ).reshape(item_count, SEQ, model_dim)
    grad_shift_two = jnp.sum(grad_hidden, axis=1)
    grad_scale_two = jnp.sum(grad_hidden * normed_two, axis=1)
    grad_residual = grad_result + normalize_back(
        normed_two, inverse_two, grad_hidden * (1.0 + scale_two)
    )
    grad_gate_one = jnp.sum(branch_one * grad_residual, axis=1)
    grad_branch_one = low((gate_one * grad_residual).reshape(tokens, model_dim))
    grad_attended = low(prod_cols(grad_branch_one, proj_weight))
    moved_in, moved_out, grad_attended = lax.optimization_barrier(
        (moved_in, moved_out, grad_attended)
    )
    grad_qkv = attend(attend_back_body, [qkv_rows, grad_attended], 3 * model_dim, score_scale)
    back_rows, shared_sum, weight_shared, grad_qkv = lax.optimization_barrier(
        (back_rows, shared_sum, weight_shared, grad_qkv)
    )
    padded = jnp.pad(grad_logits, ((0, 0), (0, -experts % 128)))
    dense, (grad_qkv,) = sum_hid(
        jnp.concatenate(
            [
                low(prod_rows(flat_one, grad_qkv)),
                low(prod_rows(attended_low, grad_branch_one)),
                low(prod_rows(hidden_two, padded)),
            ],
            axis=1,
        ),
        (grad_qkv,),
    )
    tail = dense[:1, :128]
    weight_expert_in = kept_in.astype(jnp.float32) + after(moved_in, tail).astype(jnp.float32)
    weight_expert_out = kept_out.astype(jnp.float32) + after(moved_out, tail).astype(jnp.float32)
    weight_shared = sum(part.astype(jnp.float32) for part in weight_shared)
    grad_hidden_one = prod_cols(grad_qkv, qkv_weight).reshape(item_count, SEQ, model_dim)
    grad_shift_one = jnp.sum(grad_hidden_one, axis=1)
    grad_scale_one = jnp.sum(grad_hidden_one * normed_one, axis=1)
    grad_input = grad_residual + normalize_back(
        normed_one, inverse_one, grad_hidden_one * (1.0 + scale_one)
    )
    grad_patches = low(grad_input.reshape(tokens, model_dim))
    picked = mat_prod(picks, back_rows)
    picked_first, picked_second = picked[:tokens], picked[tokens:]
    moe_out = gate_first * picked_first + gate_second * picked_second
    branch_two = (shared_sum + moe_out).reshape(item_count, SEQ, model_dim)
    output = low(residual_one + gate_two * branch_two).reshape(tokens, model_dim)
    grad_gate_two = jnp.sum(branch_two * grad_result, axis=1)
    counts_local = jnp.sum(
        first_hot * kept_first.astype(jnp.float32) + second_hot * kept_second.astype(jnp.float32),
        axis=0,
    )
    counts_rows = jnp.where(jnp.arange(item_count)[:, None] == 0, counts_local[None, :], 0.0)
    digits = jnp.stack(
        [timesteps >> 5, timesteps & 31, labels >> 5, labels & 31], axis=1
    ).astype(jnp.float32)
    item_rows = low(
        jnp.concatenate(
            [
                grad_shift_one,
                grad_scale_one,
                grad_gate_one,
                grad_shift_two,
                grad_scale_two,
                grad_gate_two,
                digits,
                counts_rows,
                jnp.zeros((item_count, -(experts + 4) % 128), jnp.float32),
            ],
            axis=1,
        )
    )
    item_rows, dense = gather_items(item_rows, dense)
    dense = sum_parts(exchange(dense))

    grad_modulate = item_rows[:, : 6 * model_dim]
    rest = item_rows[:, 6 * model_dim :].astype(jnp.float32)
    expert_counts = jnp.sum(rest[:, 4 : 4 + experts], axis=0)
    numbers = rest[:, 0:4:2] * 32.0 + rest[:, 1:4:2]
    freq_all, label_all, condition_all, silu_all = condition_of(
        numbers[:, 0].astype(jnp.int32),
        numbers[:, 1].astype(jnp.int32),
        time_weight,
        time_bias,
        class_table,
    )
    weight_ada = prod_rows(
        lax.dynamic_slice_in_dim(silu_all, place_exp * share, share, 1), grad_modulate
    )
    bias_ada = jnp.sum(grad_modulate.astype(jnp.float32), axis=0)
    grad_silu = prod_cols(grad_modulate, ada_weight)
    grad_condition = jax.vjp(jax.nn.silu, condition_all)[1](grad_silu)[0]
    bias_time = jnp.sum(grad_condition, axis=0)
    grad_condition_low = low(grad_condition)
    table_grad = prod_rows(label_all, grad_condition_low)
    freq_share = time_weight.shape[0] // experts
    weight_time = prod_rows(
        lax.dynamic_slice_in_dim(freq_all, place_exp * freq_share, freq_share, 1),
        grad_condition_low,
    )
    return (
        output,
        grad_patches,
        weight_time,
        bias_time,
        table_grad,
        weight_ada,
        bias_ada,
        dense[:, : 3 * model_dim],
        dense[:, 3 * model_dim : 4 * model_dim],
        dense[:, 4 * model_dim : 4 * model_dim + experts],
        weight_shared[0],
        weight_shared[1].T,
        weight_expert_in[None],
        weight_expert_out[None],
        expert_counts,
    )


def solution(mesh):
    placed = (
        P(("exp", "hid"), None),
        P(("exp", "hid"), None),
        P(("exp", "hid")),
        P(("exp", "hid")),
        P(("exp", "hid"), None),
        P(("exp", "hid"), None),
        P(),
        P(),
        P(),
        P(),
        P(),
        P(),
        P(),
        P(),
        P(None, "hid"),
        P("hid", None),
        P("exp", None, "hid"),
        P("exp", "hid", None),
    )
    return jax.shard_map(
        per_device,
        mesh=mesh,
        in_specs=placed,
        out_specs=(
            P(("exp", "hid"), None),
            P(("exp", "hid"), None),
            P("exp", None),
            P(),
            P(),
            P("exp", None),
            P(),
            P("exp", None),
            P("exp", None),
            P("exp", None),
            P("exp", "hid"),
            P("hid", "exp"),
            P("exp", None, "hid"),
            P("exp", "hid", None),
            P(),
        ),
        check_vma=False,
    )
```

time: 425 us -> 367 us (0.86)
  matrix products: 166 us -> 48.1 us
  Pallas kernels: 0 us -> 87.8 us
  waiting for transfers between devices: 100 us -> 68.8 us
  other arithmetic: 48.9 us -> 58.3 us
  local copies, waits for them, and re-layouts: 37.6 us -> 32.8 us
    pallas_call x0 -> x8, Pallas kernels: none -> 87.8 us  [the longest x3 48.9 us: expert_pass(): pl.pallas_call(functools.partial(expert_body, blocks, width, gated), out_...]
    dot_general x19 -> x8, matrix products: 54.9 us -> 15.7 us  [prod_rows(): lax.dot_general(left_side, right_side, (((0,), (0,)), ((), ())), preferre...]
    dot_general x15 -> x4, matrix products: 43.7 us -> 9.98 us  [prod_cols(): lax.dot_general(left_side, right_side, (((1,), (1,)), ((), ())), preferre...]
    all_to_all x7 -> x5, waiting for transfers between devices: 27.3 us -> 0.78 us  [exchange(): return lax.all_to_all(rows, 'exp', split_axis=0, concat_axis=0, tiled=True)]
    dot_general x6 -> x0, matrix products: 23.8 us -> none  [the longest x1 7.14 us: per_device(): jnp.einsum('bhqk,bqhd->bkhd', grad_scores_low, queries, preferred_element...]
    dot_general x20 -> x11, matrix products: 43.9 us -> 22.5 us  [mat_prod(): return jnp.dot(left_side, right_side, preferred_element_type=jnp.float32)]
    concatenate x2 -> x0, local copies, waits for them, and re-layouts: 7.48 us -> none  [the longest x1 4.73 us: per_device(): jnp.concatenate([low(prod_rows(attended_low, grad_branch_one)), low(prod_...]
    all_to_all x7 -> x5, starting transfers between devices: 34.9 us -> 27.7 us  [exchange(): return lax.all_to_all(rows, 'exp', split_axis=0, concat_axis=0, tiled=True)]
  transfers between devices with their start and end apart: 40 -> 38, of which waited for: 15 -> 10; matrix products, arithmetic and copies ran while one was open for 58% -> 30% of each run, Pallas kernels for 0% -> 24%
where the time goes in v3:
time: 367 us; the launch traced here: 360 us
  Pallas kernels  87.8 us (24%)
  waiting for transfers between devices  68.8 us (19%)
  starting transfers between devices  58.7 us (16%)
  other arithmetic  58.3 us (16%)
  matrix products  48.1 us (13%)
  local copies, waits for them, and re-layouts  32.8 us (9%)
  between operations  5.74 us (2%)
    ppermute x33, waiting for transfers between devices, swap(): return lax.ppermute(values, axis, pairs_of(lax.axis_size(axis), mask))  68 us
    pallas_call x3, Pallas kernels, expert_pass(): pl.pallas_call(functools.partial(expert_body, blocks, width, gated), out_...  48.9 us
    ppermute x33, starting transfers between devices, swap(): return lax.ppermute(values, axis, pairs_of(lax.axis_size(axis), mask))  30.9 us
    all_to_all x5, starting transfers between devices, exchange(): return lax.all_to_all(rows, 'exp', split_axis=0, concat_axis=0, tiled=True)  27.7 us
    dot_general x11, matrix products, mat_prod(): return jnp.dot(left_side, right_side, preferred_element_type=jnp.float32)  22.5 us
    pallas_call x2, Pallas kernels, outer_pass(): pl.pallas_call(functools.partial(outer_body, blocks, width, bool(added)),...  16.7 us
    dot_general x8, matrix products, prod_rows(): lax.dot_general(left_side, right_side, (((0,), (0,)), ((), ())), preferre...  15.7 us
    pallas_call x2, Pallas kernels, attend(): pl.pallas_call(functools.partial(body, score_scale), grid=(rows // SEQ,),...  15.4 us
  transfers between devices with their start and end apart: 38, of which 10 were waited for; matrix products, arithmetic and copies ran while one was open for 30% of the time, Pallas kernels for 24%

profile of v3, /device:TPU:0, one launch (start us, length us, event | category | flops | bytes accessed | tf_op | source)
XLA Modules:
  0.0 360.2 jit_solution(16322376914895990406)
XLA Ops:
  0.7 3.0 collective-permute-start
  5.1 1.7 convolution_reduce_fusion.2
  7.1 4.1 %convolution_reduce_fusion = f32[4608]{0:T(1024)S(1)} fusion(bf16[768,1]{0,1:T(2,128)(2,1)S(1)} %reshape.620, bf16[768,4608]{1,0:T(8,128)(2,1)} %param.28), kind=kOutput, calls=%fused_computation.30 | convolution fusion | flops 7077888 | bytes 7097856 | tf_op jit(solution)/shard_map/dot_general | solution.py:21
  14.9 5.8 %all-to-all-start = ((bf16[8,72,768]{2,1,0:T(8,128)(2,1)}), bf16[8,72,768]{2,1,0:T(8,128)(2,1)}, u32[]{:S(2)}, u32[]{:S(2)}) async-start(bf16[8,72,768]{2,1,0:T(8,128)(2,1)} %bitcast.108), calls=%async_computation | async-start | bytes 1769472 | tf_op jit(solution)/shard_map/all_to_all | solution.py:133
  26.2 1.9 fusion.30
  28.0 3.2 convolution_convert_fusion.2.rows_ref
  31.2 7.6 %shard_map.298 = bf16[256,768]{1,0:T(8,128)(2,1)} custom-call(bf16[256,2304]{1,0:T(8,128)(2,1)} %convolution_convert_fusion.2.rows_ref), custom_call_target="tpu_custom_call" | custom-call | flops 1000 | bytes 1000 | tf_op jit(solution)/shard_map/pallas_call | solution.py:391
  38.8 2.9 fusion.91
  44.1 1.9 select_reduce_fusion
  47.5 2.9 convolution_convert_fusion.4
  50.4 6.2 %all-to-all-start.1 = ((bf16[8,72,896]{2,1,0:T(8,128)(2,1)}), bf16[8,72,896]{2,1,0:T(8,128)(2,1)}, u32[]{:S(2)}, u32[]{:S(2)}) async-start(bf16[8,72,896]{2,1,0:T(8,128)(2,1)} %bitcast.106), calls=%async_computation.1 | async-start | bytes 2064384 | tf_op jit(solution)/shard_map/all_to_all | solution.py:133
  60.6 2.4 broadcast_select_fusion
  63.6 5.3 %collective-permute-done.3 = bf16[256,768]{1,0:T(8,128)(2,1)S(1)} collective-permute-done((bf16[256,768]{1,0:T(8,128)(2,1)}, bf16[256,768]{1,0:T(8,128)(2,1)S(1)}, u32[]{:S(2)}, u32[]{:S(2)}) %collective-permute-start.3) | collective-permute-done | bytes 393248 | tf_op jit(solution)/shard_map/ppermute | solution.py:62
  69.8 2.0 pad_maximum_fusion.1.refs_0_.rows_a
  72.9 7.9 %shard_map.299 = (bf16[512,768]{1,0:T(8,128)(2,1)}, bf16[512,768]{1,0:T(8,128)(2,1)}, bf16[512,768]{1,0:T(8,128)(2,1)}, bf16[512,768]{1,0:T(8,128)(2,1)}) custom-call(bf16[512,768]{1,0:T(8,128)(2,1)} %pad_maximum_fusion.1.refs_0_.rows_a, bf16[512,768]{1,0:T(8,128)(2,1)} %pad_maximum_fusion.2.refs_1_.grads_a, bf16[768,768]{1,0:T(8,128)(2,1)} %refs_2_.3, ...), custom_call_target="tpu_custom_call" | custom-call | flops 1000 | bytes 1000 | tf_op jit(solution)/shard_map/pallas_call | solution.py:281
  80.8 7.9 %shard_map.300 = (bf16[512,768]{1,0:T(8,128)(2,1)}, bf16[512,768]{1,0:T(8,128)(2,1)}, bf16[512,768]{1,0:T(8,128)(2,1)}, bf16[512,768]{1,0:T(8,128)(2,1)}) custom-call(bf16[512,768]{1,0:T(8,128)(2,1)} %collective-permute-done.2.refs_0_.rows_b, bf16[512,768]{1,0:T(8,128)(2,1)} %collective-permute-done.4.refs_1_.grads_b, bf16[768,768]{1,0:T(8,128)(2,1)} %refs_2_.3, ...), custom_call_target="tpu_custom_call" | custom-call | flops 1000 | bytes 1000 | tf_op jit(solution)/shard_map/pallas_call | solution.py:281
  88.7 6.8 %shard_map.301 = bf16[2,768,768]{2,1,0:T(8,128)(2,1)} custom-call(bf16[512,768]{1,0:T(8,128)(2,1)} %pad_maximum_fusion.1.refs_0_.rows_a, bf16[512,768]{1,0:T(8,128)(2,1)} %collective-permute-done.2.refs_0_.rows_b, bf16[512,768]{1,0:T(8,128)(2,1)} %pad_maximum_fusion.2.refs_1_.grads_a, bf16[512,768]{1,0:T(8,128)(2,1)} %collective-permute-done.4.refs_1_.grads_b, ...), custom_call_target="tpu_custom_call" | custom-call | flops 1000 | bytes 1000 | tf_op jit(solution)/shard_map/pallas_call | solution.py:326
  96.0 1.8 constant_dynamic-slice_fusion.1
  97.9 2.0 collective-permute-start.10
  99.9 33.2 %shard_map.302 = (bf16[576,896]{1,0:T(8,128)(2,1)}, bf16[576,768]{1,0:T(8,128)(2,1)}, bf16[576,768]{1,0:T(8,128)(2,1)}, bf16[576,768]{1,0:T(8,128)(2,1)}, bf16[5...) custom-call(bf16[576,896]{1,0:T(8,128)(2,1)} %bitcast.10.refs_0_, ...), custom_call_target="tpu_custom_call" | custom-call | flops 1000 | bytes 1000 | tf_op jit(solution)/shard_map/pallas_call | solution.py:281
  133.0 1.7 convert_add_fusion.1
  134.7 5.2 %all-to-all-start.2 = ((bf16[8,72,896]{2,1,0:T(8,128)(2,1)}), bf16[8,72,896]{2,1,0:T(8,128)(2,1)}, u32[]{:S(2)}, u32[]{:S(2)}) async-start(bf16[8,72,896]{2,1,0:T(8,128)(2,1)} %bitcast.105), calls=%async_computation.2 | async-start | bytes 2064384 | tf_op jit(solution)/shard_map/all_to_all | solution.py:133
  139.9 7.6 %shard_map.303 = (bf16[768,768]{1,0:T(8,128)(2,1)}, bf16[768,768]{1,0:T(8,128)(2,1)}, bf16[768,768]{1,0:T(8,128)(2,1)}, bf16[768,768]{1,0:T(8,128)(2,1)}) custom-call(bf16[576,896]{1,0:T(8,128)(2,1)} %bitcast.10.refs_0_, bf16[576,768]{1,0:T(8,128)(2,1)} %get-tuple-element.90.refs_1_, bf16[576,768]{1,0:T(8,128)(2,1)} %get-tuple-element.95.refs_2_, ...), custom_call_target="tpu_custom_call" | custom-call | flops 1000 | bytes 1000 | tf_op jit(solution)/shard_map/pallas_call | solution.py:311
  148.5 1.6 convert_add_fusion.2
  151.0 1.6 collective-permute-start.23
  152.6 2.4 convert_add_fusion.3
  155.9 9.1 %shard_map.304 = (bf16[768,768]{1,0:T(8,128)(2,1)}, bf16[768,768]{1,0:T(8,128)(2,1)}, bf16[768,768]{1,0:T(8,128)(2,1)}, bf16[768,768]{1,0:T(8,128)(2,1)}) custom-call(bf16[576,896]{1,0:T(8,128)(2,1)} %bitcast.10.refs_0_, bf16[576,768]{1,0:T(8,128)(2,1)} %get-tuple-element.90.refs_1_, bf16[576,768]{1,0:T(8,128)(2,1)} %get-tuple-element.91.refs_2_, ...), custom_call_target="tpu_custom_call" | custom-call | flops 1000 | bytes 1000 | tf_op jit(solution)/shard_map/pallas_call | solution.py:311
  165.7 5.7 %all-to-all-start.3 = ((bf16[8,72,768]{2,1,0:T(8,128)(2,1)}), bf16[8,72,768]{2,1,0:T(8,128)(2,1)}, u32[]{:S(2)}, u32[]{:S(2)}) async-start(bf16[8,72,768]{2,1,0:T(8,128)(2,1)} %bitcast.107), calls=%async_computation.3 | async-start | bytes 1769472 | tf_op jit(solution)/shard_map/all_to_all | solution.py:133
  172.7 1.6 collective-permute-start.16
  174.4 2.4 fusion.41
  176.7 2.0 collective-permute-start.17
  178.8 2.4 collective-permute-start.18
  181.7 2.1 fusion.47
  184.4 1.6 collective-permute-start.21
  186.1 2.3 multiply_reduce_fusion
  191.0 2.0 convolution_convert_fusion.7
  194.6 2.0 dynamic-slice_bitcast_fusion.1
  197.6 12.6 %collective-permute-done.20 = bf16[768,768]{1,0:T(8,128)(2,1)} collective-permute-done((bf16[768,768]{1,0:T(8,128)(2,1)S(1)}, bf16[768,768]{1,0:T(8,128)(2,1)}, u32[]{:S(2)}, u32[]{:S(2)}) %collective-permute-start.20) | collective-permute-done | bytes 1179680 | tf_op jit(solution)/shard_map/ppermute | solution.py:62
  210.2 24.4 %collective-permute-done.21 = bf16[768,768]{1,0:T(8,128)(2,1)} collective-permute-done((bf16[768,768]{1,0:T(8,128)(2,1)S(1)}, bf16[768,768]{1,0:T(8,128)(2,1)}, u32[]{:S(2)}, u32[]{:S(2)}) %collective-permute-start.21) | collective-permute-done | bytes 1179680 | tf_op jit(solution)/shard_map/ppermute | solution.py:62
  234.6 7.8 %shard_map.305 = bf16[256,2304]{1,0:T(8,128)(2,1)} custom-call(bf16[256,2304]{1,0:T(8,128)(2,1)} %convolution_convert_fusion.2.rows_ref, bf16[256,768]{1,0:T(8,128)(2,1)} %convolution_convert_fusion.6.grad_ref), custom_call_target="tpu_custom_call" | custom-call | flops 1000 | bytes 1000 | tf_op jit(solution)/shard_map/pallas_call | solution.py:391
  242.5 2.8 convolution_convert_fusion.1
  245.7 1.8 dynamic-slice_bitcast_fusion
  254.7 2.2 fusion.46
  261.7 2.2 convert_add_fusion
  266.5 2.6 fusion.20
  272.2 1.7 collective-permute-start.25
  277.0 1.8 collective-permute-start.26
  279.5 1.6 collective-permute-start.28
  281.8 2.5 collective-permute-start.27
  284.3 2.5 fusion.19
  287.6 20.2 %collective-permute-done.28 = bf16[8,1,24,3200]{3,2,1,0:T(8,128)(2,1)S(1)} collective-permute-done((bf16[8,1,24,3200]{3,2,1,0:T(8,128)(2,1)}, bf16[8,1,24,3200]{3,2,1,0:T(8,128)(2,1)S(1)}, u32[]{:S(2)}, u32[]{:S(2)}) %collective-permute-start.28) | collective-permute-done | bytes 1228832 | tf_op jit(solution)/shard_map/ppermute | solution.py:62
  307.8 1.9 add_convert_fusion
  310.8 4.8 %all-to-all-start.4 = ((bf16[8,24,3200]{2,1,0:T(8,128)(2,1)}), bf16[8,24,3200]{2,1,0:T(8,128)(2,1)}, u32[]{:S(2)}, u32[]{:S(2)}) async-start(bf16[8,24,3200]{2,1,0:T(8,128)(2,1)} %bitcast.98), calls=%async_computation.4 | async-start | bytes 2457600 | tf_op jit(solution)/shard_map/all_to_all | solution.py:133
  316.8 3.4 add_bitcast_fusion.1
  321.2 1.6 collective-permute-start.30
  322.9 3.0 add_bitcast_fusion
  333.2 1.8 add_divide_fusion
  335.0 5.7 %fusion.93 = (f32[768]{0:T(1024)}, bf16[32,768]{1,0:T(8,128)(2,1)S(1)}) fusion(f32[32,768]{1,0:T(8,128)S(1)} %get-tuple-element.213, bf16[768,4608]{1,0:T(8,128)(2,1)} %param.28, bf16[32,4736]{1,0:T(8,128)(2,1)S(1)} %copy-done.27), kind=kOutput, calls=%fused_computation.214 | convolution fusion | flops 226761984 | bytes 7523328 | tf_op jit(solution)/shard_map/dot_general | solution.py:31
  341.6 1.7 fusion.42
  343.3 2.3 fusion.48
  345.7 2.2 reduce_sum.221
  347.8 1.6 collective-permute-start.31
  350.0 1.6 convert_reduce_fusion.1
  351.7 1.6 collective-permute-done.31
  (287 shorter events, 70.5 us)
Async XLA Ops:
  0.6 27.4 %copy-start = (bf16[768,2304]{1,0:T(8,128)(2,1)S(1)}, bf16[768,2304]{1,0:T(8,128)(2,1)}, u32[]{:S(2)}) copy-start(bf16[768,2304]{1,0:T(8,128)(2,1)} %param.30) | copy-start | bytes 10616836
  0.7 6.2 %copy-start.29 = (bf16[256,768]{1,0:T(8,128)(2,1)S(1)}, bf16[256,768]{1,0:T(8,128)(2,1)}, u32[]{:S(2)}) copy-start(bf16[256,768]{1,0:T(8,128)(2,1)} %param.25) | copy-start | bytes 1179652
  0.7 6.4 %copy-start.50 = (f32[768]{0:T(1024)S(1)}, f32[768]{0:T(1024)}, u32[]{:S(2)}) copy-start(f32[768]{0:T(1024)} %param.26) | copy-start | bytes 9220
  0.7 30.6 %collective-permute-start = (bf16[768,768]{1,0:T(8,128)(2,1)}, bf16[768,768]{1,0:T(8,128)(2,1)}, u32[]{:S(2)}, u32[]{:S(2)}) collective-permute-start(bf16[768,768]{1,0:T(8,128)(2,1)} %bitcast.2.refs_2_), channel_id=1, source_target_pairs={{0,2},{1,3},{2,0},{3,1},{4,6},{5,7},{6,4},{7,5},{8,10},{9,11},{10,... | collective-permute-start | bytes 3538952 | tf_op jit(solution)/shard_map/ppermute | solution.py:62
  14.9 35.4 %all-to-all-start = ((bf16[8,72,768]{2,1,0:T(8,128)(2,1)}), bf16[8,72,768]{2,1,0:T(8,128)(2,1)}, u32[]{:S(2)}, u32[]{:S(2)}) async-start(bf16[8,72,768]{2,1,0:T(8,128)(2,1)} %bitcast.108), calls=%async_computation | async-start | bytes 1769472 | tf_op jit(solution)/shard_map/all_to_all | solution.py:133
  24.9 6.3 %copy-start.43 = (f32[256]{0:T(256)}, f32[256]{0:T(256)S(1)}, u32[]{:S(2)}) copy-start(f32[256]{0:T(256)S(1)} %broadcast_multiply_fusion.5) | copy-start | bytes 3076
  41.7 5.5 %copy-start.68 = (pred[128]{0:T(512)(128)(4,1)S(1)}, pred[128]{0:T(512)(128)(4,1)}, u32[]{:S(2)}) copy-start(pred[128]{0:T(512)(128)(4,1)} %get-tuple-element.218) | copy-start | bytes 388
  41.7 5.5 %copy-start.69 = (pred[128]{0:T(512)(128)(4,1)S(1)}, pred[128]{0:T(512)(128)(4,1)}, u32[]{:S(2)}) copy-start(pred[128]{0:T(512)(128)(4,1)} %get-tuple-element.219) | copy-start | bytes 388
  41.7 5.7 %copy-start.22 = (bf16[256,576]{1,0:T(8,128)(2,1)S(1)}, bf16[256,576]{1,0:T(8,128)(2,1)}, u32[]{:S(2)}) copy-start(bf16[256,576]{1,0:T(8,128)(2,1)} %get-tuple-element.216) | copy-start | bytes 884740
  41.8 5.7 %copy-start.24 = (bf16[256,576]{1,0:T(8,128)(2,1)S(1)}, bf16[256,576]{1,0:T(8,128)(2,1)}, u32[]{:S(2)}) copy-start(bf16[256,576]{1,0:T(8,128)(2,1)} %get-tuple-element.217) | copy-start | bytes 884740
  41.8 5.5 %copy-start.45 = (f32[256]{0:T(256)}, f32[256]{0:T(256)S(1)}, u32[]{:S(2)}) copy-start(f32[256]{0:T(256)S(1)} %broadcast_multiply_fusion.4) | copy-start | bytes 3076
  43.5 14.6 %collective-permute-start.1 = (bf16[256,768]{1,0:T(8,128)(2,1)}, bf16[256,768]{1,0:T(8,128)(2,1)}, u32[]{:S(2)}, u32[]{:S(2)}) collective-permute-start(bf16[256,768]{1,0:T(8,128)(2,1)} %add_convert_fusion.2), channel_id=1, source_target_pairs={{0,2},{1,3},{2,0},{3,1},{4,6},{5,7},{6,4},{7,5},{8,10},{9,11},{10,... | collective-permute-start | bytes 1179656 | tf_op jit(solution)/shard_map/ppermute | solution.py:62
  50.4 45.6 %all-to-all-start.1 = ((bf16[8,72,896]{2,1,0:T(8,128)(2,1)}), bf16[8,72,896]{2,1,0:T(8,128)(2,1)}, u32[]{:S(2)}, u32[]{:S(2)}) async-start(bf16[8,72,896]{2,1,0:T(8,128)(2,1)} %bitcast.106), calls=%async_computation.1 | async-start | bytes 2064384 | tf_op jit(solution)/shard_map/all_to_all | solution.py:133
  56.6 12.3 %copy-start.31 = (bf16[256,768]{1,0:T(8,128)(2,1)S(1)}, bf16[256,768]{1,0:T(8,128)(2,1)}, u32[]{:S(2)}) copy-start(bf16[256,768]{1,0:T(8,128)(2,1)} %copy-done.30) | copy-start | bytes 1179652
  56.6 12.3 %collective-permute-start.3 = (bf16[256,768]{1,0:T(8,128)(2,1)}, bf16[256,768]{1,0:T(8,128)(2,1)S(1)}, u32[]{:S(2)}, u32[]{:S(2)}) collective-permute-start(bf16[256,768]{1,0:T(8,128)(2,1)} %copy-done.30), channel_id=1, source_target_pairs={{0,2},{1,3},{2,0},{3,1},{4,6},{5,7},{6,4},{7,5},{8,10},{9,11},{10,... | collective-permute-start | bytes 1179656 | tf_op jit(solution)/shard_map/ppermute | solution.py:62
  63.0 32.5 %collective-permute-start.8 = (bf16[768,768]{1,0:T(8,128)(2,1)}, bf16[768,768]{1,0:T(8,128)(2,1)}, u32[]{:S(2)}, u32[]{:S(2)}) collective-permute-start(bf16[768,768]{1,0:T(8,128)(2,1)} %broadcast_select_fusion), channel_id=1, source_target_pairs={{0,2},{1,3},{2,0},{3,1},{4,6},{5,7},{6,4},{7,5},{8,10},{9,11},{10,... | collective-permute-start | bytes 3538952 | tf_op jit(solution)/shard_map/ppermute | solution.py:62
  69.8 10.9 %collective-permute-start.4 = (bf16[512,768]{1,0:T(8,128)(2,1)}, bf16[512,768]{1,0:T(8,128)(2,1)}, u32[]{:S(2)}, u32[]{:S(2)}) collective-permute-start(bf16[512,768]{1,0:T(8,128)(2,1)} %pad_maximum_fusion.2.refs_1_.grads_a), channel_id=1, source_target_pairs={{0,1},{1,0},{2,3},{3,2},{4,5},{5,4},{6,7},{7,6},{8,9},{9,8},{10,11... | collective-permute-start | bytes 2359304 | tf_op jit(solution)/shard_map/ppermute | solution.py:62
  71.9 8.9 %collective-permute-start.2 = (bf16[512,768]{1,0:T(8,128)(2,1)}, bf16[512,768]{1,0:T(8,128)(2,1)}, u32[]{:S(2)}, u32[]{:S(2)}) collective-permute-start(bf16[512,768]{1,0:T(8,128)(2,1)} %pad_maximum_fusion.1.refs_0_.rows_a), channel_id=1, source_target_pairs={{0,1},{1,0},{2,3},{3,2},{4,5},{5,4},{6,7},{7,6},{8,9},{9,8},{10,11... | collective-permute-start | bytes 2359304 | tf_op jit(solution)/shard_map/ppermute | solution.py:62
  72.4 27.5 %collective-permute-start.5 = (bf16[768,768]{1,0:T(8,128)(2,1)}, bf16[768,768]{1,0:T(8,128)(2,1)}, u32[]{:S(2)}, u32[]{:S(2)}) collective-permute-start(bf16[768,768]{1,0:T(8,128)(2,1)} %bitcast.2.refs_2_), channel_id=1, source_target_pairs={{0,1},{1,0},{2,3},{3,2},{4,5},{5,4},{6,7},{7,6},{8,9},{9,8},{10,11... | collective-permute-start | bytes 3538952 | tf_op jit(solution)/shard_map/ppermute | solution.py:62
  72.4 27.5 %collective-permute-start.7 = (bf16[768,768]{1,0:T(8,128)(2,1)}, bf16[768,768]{1,0:T(8,128)(2,1)}, u32[]{:S(2)}, u32[]{:S(2)}) collective-permute-start(bf16[768,768]{1,0:T(8,128)(2,1)} %bitcast.11.refs_6_), channel_id=1, source_target_pairs={{0,1},{1,0},{2,3},{3,2},{4,5},{5,4},{6,7},{7,6},{8,9},{9,8},{10,11... | collective-permute-start | bytes 3538952 | tf_op jit(solution)/shard_map/ppermute | solution.py:62
  80.8 19.1 %collective-permute-start.6 = (bf16[768,768]{1,0:T(8,128)(2,1)}, bf16[768,768]{1,0:T(8,128)(2,1)}, u32[]{:S(2)}, u32[]{:S(2)}) collective-permute-start(bf16[768,768]{1,0:T(8,128)(2,1)} %collective-permute-done.refs_4_), channel_id=1, source_target_pairs={{0,1},{1,0},{2,3},{3,2},{4,5},{5,4},{6,7},{7,6},{8,9},{9,8},{10,11... | collective-permute-start | bytes 3538952 | tf_op jit(solution)/shard_map/ppermute | solution.py:62
  95.5 4.4 %collective-permute-start.9 = (bf16[768,768]{1,0:T(8,128)(2,1)}, bf16[768,768]{1,0:T(8,128)(2,1)}, u32[]{:S(2)}, u32[]{:S(2)}) collective-permute-start(bf16[768,768]{1,0:T(8,128)(2,1)} %collective-permute-done.8.refs_8_), channel_id=1, source_target_pairs={{0,1},{1,0},{2,3},{3,2},{4,5},{5,4},{6,7},{7,6},{8,9},{9,8},{10,11... | collective-permute-start | bytes 3538952 | tf_op jit(solution)/shard_map/ppermute | solution.py:62
  97.9 35.2 %collective-permute-start.10 = (bf16[2,4,96,768]{3,2,0,1:T(8,128)(2,1)S(1)}, bf16[2,4,96,768]{3,2,0,1:T(8,128)(2,1)S(1)}, u32[]{:S(2)}, u32[]{:S(2)}) collective-permute-start(bf16[2,4,96,768]{3,2,0,1:T(8,128)(2,1)S(1)} %bitcast.104), channel_id=1, source_target_pairs={{0,4},{4,0},{8,12},{12,8},{16,20},{20,16},{24,28},{28,24},{1,5},{5... | collective-permute-start | bytes 3538952 | tf_op jit(solution)/shard_map/ppermute | solution.py:62
  134.7 5.2 %collective-permute-start.11 = (bf16[512,768]{1,0:T(8,128)(2,1)}, bf16[512,768]{1,0:T(8,128)(2,1)}, u32[]{:S(2)}, u32[]{:S(2)}) collective-permute-start(bf16[512,768]{1,0:T(8,128)(2,1)} %get-tuple-element.89), channel_id=1, source_target_pairs={{0,1},{1,0},{2,3},{3,2},{4,5},{5,4},{6,7},{7,6},{8,9},{9,8},{10,11... | collective-permute-start | bytes 2359304 | tf_op jit(solution)/shard_map/ppermute | solution.py:62
  134.7 31.0 %all-to-all-start.2 = ((bf16[8,72,896]{2,1,0:T(8,128)(2,1)}), bf16[8,72,896]{2,1,0:T(8,128)(2,1)}, u32[]{:S(2)}, u32[]{:S(2)}) async-start(bf16[8,72,896]{2,1,0:T(8,128)(2,1)} %bitcast.105), calls=%async_computation.2 | async-start | bytes 2064384 | tf_op jit(solution)/shard_map/all_to_all | solution.py:133
  139.9 8.7 %collective-permute-start.22 = (bf16[512,768]{1,0:T(8,128)(2,1)}, bf16[512,768]{1,0:T(8,128)(2,1)}, u32[]{:S(2)}, u32[]{:S(2)}) collective-permute-start(bf16[512,768]{1,0:T(8,128)(2,1)} %get-tuple-element.114), channel_id=1, source_target_pairs={{0,1},{1,0},{2,3},{3,2},{4,5},{5,4},{6,7},{7,6},{8,9},{9,8},{10,11... | collective-permute-start | bytes 2359304 | tf_op jit(solution)/shard_map/ppermute | solution.py:62
  147.5 7.5 %collective-permute-start.12 = (bf16[768,768]{1,0:T(8,128)(2,1)}, bf16[768,768]{1,0:T(8,128)(2,1)}, u32[]{:S(2)}, u32[]{:S(2)}) collective-permute-start(bf16[768,768]{1,0:T(8,128)(2,1)} %get-tuple-element.99), channel_id=1, source_target_pairs={{0,1},{1,0},{2,3},{3,2},{4,5},{5,4},{6,7},{7,6},{8,9},{9,8},{10,11... | collective-permute-start | bytes 3538952 | tf_op jit(solution)/shard_map/ppermute | solution.py:62
  148.0 7.1 %collective-permute-start.13 = (bf16[768,768]{1,0:T(8,128)(2,1)}, bf16[768,768]{1,0:T(8,128)(2,1)}, u32[]{:S(2)}, u32[]{:S(2)}) collective-permute-start(bf16[768,768]{1,0:T(8,128)(2,1)} %get-tuple-element.100), channel_id=1, source_target_pairs={{0,1},{1,0},{2,3},{3,2},{4,5},{5,4},{6,7},{7,6},{8,9},{9,8},{10,11... | collective-permute-start | bytes 3538952 | tf_op jit(solution)/shard_map/ppermute | solution.py:62
  148.0 7.0 %collective-permute-start.14 = (bf16[768,768]{1,0:T(8,128)(2,1)}, bf16[768,768]{1,0:T(8,128)(2,1)}, u32[]{:S(2)}, u32[]{:S(2)}) collective-permute-start(bf16[768,768]{1,0:T(8,128)(2,1)} %get-tuple-element.101), channel_id=1, source_target_pairs={{0,1},{1,0},{2,3},{3,2},{4,5},{5,4},{6,7},{7,6},{8,9},{9,8},{10,11... | collective-permute-start | bytes 3538952 | tf_op jit(solution)/shard_map/ppermute | solution.py:62
  148.5 7.4 %collective-permute-start.15 = (bf16[768,768]{1,0:T(8,128)(2,1)}, bf16[768,768]{1,0:T(8,128)(2,1)}, u32[]{:S(2)}, u32[]{:S(2)}) collective-permute-start(bf16[768,768]{1,0:T(8,128)(2,1)} %get-tuple-element.102), channel_id=1, source_target_pairs={{0,1},{1,0},{2,3},{3,2},{4,5},{5,4},{6,7},{7,6},{8,9},{9,8},{10,11... | collective-permute-start | bytes 3538952 | tf_op jit(solution)/shard_map/ppermute | solution.py:62
  151.0 33.4 %collective-permute-start.23 = (bf16[256,768]{1,0:T(8,128)(2,1)}, bf16[256,768]{1,0:T(8,128)(2,1)}, u32[]{:S(2)}, u32[]{:S(2)}) collective-permute-start(bf16[256,768]{1,0:T(8,128)(2,1)} %slice.242), channel_id=1, source_target_pairs={{0,2},{1,3},{2,0},{3,1},{4,6},{5,7},{6,4},{7,5},{8,10},{9,11},{10,... | collective-permute-start | bytes 1179656 | tf_op jit(solution)/shard_map/ppermute | solution.py:62
  165.7 76.7 %all-to-all-start.3 = ((bf16[8,72,768]{2,1,0:T(8,128)(2,1)}), bf16[8,72,768]{2,1,0:T(8,128)(2,1)}, u32[]{:S(2)}, u32[]{:S(2)}) async-start(bf16[8,72,768]{2,1,0:T(8,128)(2,1)} %bitcast.107), calls=%async_computation.3 | async-start | bytes 1769472 | tf_op jit(solution)/shard_map/all_to_all | solution.py:133
  171.4 9.9 %copy-start.71 = (bf16[768,768]{1,0:T(8,128)(2,1)S(1)}, bf16[768,768]{1,0:T(8,128)(2,1)}, u32[]{:S(2)}) copy-start(bf16[768,768]{1,0:T(8,128)(2,1)} %get-tuple-element.110) | copy-start | bytes 3538948
  171.4 10.3 %copy-start.23 = (bf16[256,576]{1,0:T(8,128)(2,1)S(1)}, bf16[256,576]{1,0:T(8,128)(2,1)}, u32[]{:S(2)}) copy-start(bf16[256,576]{1,0:T(8,128)(2,1)} %get-tuple-element.216) | copy-start | bytes 884740
  171.4 10.3 %copy-start.25 = (bf16[256,576]{1,0:T(8,128)(2,1)S(1)}, bf16[256,576]{1,0:T(8,128)(2,1)}, u32[]{:S(2)}) copy-start(bf16[256,576]{1,0:T(8,128)(2,1)} %get-tuple-element.217) | copy-start | bytes 884740
  172.7 21.8 %collective-permute-start.16 = (bf16[256,768]{1,0:T(8,128)(2,1)S(1)}, bf16[256,768]{1,0:T(8,128)(2,1)S(1)}, u32[]{:S(2)}, u32[]{:S(2)}) collective-permute-start(bf16[256,768]{1,0:T(8,128)(2,1)S(1)} %slice.243), channel_id=1, source_target_pairs={{0,2},{1,3},{2,0},{3,1},{4,6},{5,7},{6,4},{7,5},{8,10},{9,11},{10,... | collective-permute-start | bytes 1179656 | tf_op jit(solution)/shard_map/ppermute | solution.py:62
  176.7 65.7 %collective-permute-start.17 = (bf16[2,96,768]{2,1,0:T(8,128)(2,1)}, bf16[2,96,768]{2,1,0:T(8,128)(2,1)}, u32[]{:S(2)}, u32[]{:S(2)}) collective-permute-start(bf16[2,96,768]{2,1,0:T(8,128)(2,1)} %get-tuple-element.191), channel_id=1, source_target_pairs={{0,8},{4,12},{8,0},{12,4},{16,24},{20,28},{24,16},{28,20},{1,9},{5... | collective-permute-start | bytes 884744 | tf_op jit(solution)/shard_map/ppermute | solution.py:62
  178.8 5.6 %copy-start.70 = (bf16[768,768]{1,0:T(8,128)(2,1)S(1)}, bf16[768,768]{1,0:T(8,128)(2,1)}, u32[]{:S(2)}) copy-start(bf16[768,768]{1,0:T(8,128)(2,1)} %get-tuple-element.111) | copy-start | bytes 3538948
  178.8 7.3 %copy-start.2 = (f32[256,768]{1,0:T(8,128)S(1)}, f32[256,768]{1,0:T(8,128)}, u32[]{:S(2)}) copy-start(f32[256,768]{1,0:T(8,128)} %copy-done.1) | copy-start | bytes 2359300
  178.8 7.3 %copy-start.12 = (f32[512,768]{1,0:T(8,128)S(1)}, f32[512,768]{1,0:T(8,128)}, u32[]{:S(2)}) copy-start(f32[512,768]{1,0:T(8,128)} %copy-done.11) | copy-start | bytes 4718596
  178.8 7.3 %copy-start.46 = (f32[256]{0:T(256)S(1)}, f32[256]{0:T(256)}, u32[]{:S(2)}) copy-start(f32[256]{0:T(256)} %copy-done.45) | copy-start | bytes 3076
  178.8 7.3 %copy-start.57 = (f32[256]{0:T(256)S(1)}, f32[256]{0:T(256)}, u32[]{:S(2)}) copy-start(f32[256]{0:T(256)} %copy-done.56) | copy-start | bytes 3076
  178.8 7.2 %copy-start.59 = (f32[256]{0:T(256)S(1)}, f32[256]{0:T(256)}, u32[]{:S(2)}) copy-start(f32[256]{0:T(256)} %get-tuple-element.185) | copy-start | bytes 3076
  178.8 63.6 %collective-permute-start.18 = (bf16[2,96,768]{2,1,0:T(8,128)(2,1)}, bf16[2,96,768]{2,1,0:T(8,128)(2,1)}, u32[]{:S(2)}, u32[]{:S(2)}) collective-permute-start(bf16[2,96,768]{2,1,0:T(8,128)(2,1)} %get-tuple-element.190), channel_id=1, source_target_pairs={{0,16},{4,20},{8,24},{12,28},{16,0},{20,4},{24,8},{28,12},{1,17},{... | collective-permute-start | bytes 884744 | tf_op jit(solution)/shard_map/ppermute | solution.py:62
  181.3 28.9 %collective-permute-start.20 = (bf16[768,768]{1,0:T(8,128)(2,1)S(1)}, bf16[768,768]{1,0:T(8,128)(2,1)}, u32[]{:S(2)}, u32[]{:S(2)}) collective-permute-start(bf16[768,768]{1,0:T(8,128)(2,1)S(1)} %copy-done.71), channel_id=1, source_target_pairs={{0,2},{1,3},{2,0},{3,1},{4,6},{5,7},{6,4},{7,5},{8,10},{9,11},{10,... | collective-permute-start | bytes 3538952 | tf_op jit(solution)/shard_map/ppermute | solution.py:62
  184.4 50.2 %collective-permute-start.21 = (bf16[768,768]{1,0:T(8,128)(2,1)S(1)}, bf16[768,768]{1,0:T(8,128)(2,1)}, u32[]{:S(2)}, u32[]{:S(2)}) collective-permute-start(bf16[768,768]{1,0:T(8,128)(2,1)S(1)} %copy-done.70), channel_id=1, source_target_pairs={{0,2},{1,3},{2,0},{3,1},{4,6},{5,7},{6,4},{7,5},{8,10},{9,11},{10,... | collective-permute-start | bytes 3538952 | tf_op jit(solution)/shard_map/ppermute | solution.py:62
  194.5 47.9 %collective-permute-start.19 = (bf16[2,96,768]{2,1,0:T(8,128)(2,1)}, bf16[2,96,768]{2,1,0:T(8,128)(2,1)}, u32[]{:S(2)}, u32[]{:S(2)}) collective-permute-start(bf16[2,96,768]{2,1,0:T(8,128)(2,1)} %get-tuple-element.189), channel_id=1, source_target_pairs={{0,24},{4,28},{8,16},{12,20},{16,8},{20,12},{24,0},{28,4},{1,25},{... | collective-permute-start | bytes 884744 | tf_op jit(solution)/shard_map/ppermute | solution.py:62
  197.6 44.9 %copy-start.44 = (f32[256]{0:T(256)S(1)}, f32[256]{0:T(256)}, u32[]{:S(2)}) copy-start(f32[256]{0:T(256)} %copy-done.43) | copy-start | bytes 3076
  197.6 44.9 %copy-start.49 = (f32[256]{0:T(256)S(1)}, f32[256]{0:T(256)}, u32[]{:S(2)}) copy-start(f32[256]{0:T(256)} %copy-done.48) | copy-start | bytes 3076
  248.7 13.0 %collective-permute-start.24 = (bf16[8,2,24,3200]{3,2,1,0:T(8,128)(2,1)}, bf16[8,2,24,3200]{3,2,1,0:T(8,128)(2,1)}, u32[]{:S(2)}, u32[]{:S(2)}) collective-permute-start(bf16[8,2,24,3200]{3,2,1,0:T(8,128)(2,1)} %dynamic-slice_bitcast_fusion), channel_id=1, source_target_pairs={{0,1},{1,0},{2,3},{3,2},{4,5},{5,4},{6,7},{7,6},{8,9},{9,8},{10,11... | collective-permute-start | bytes 7372808 | tf_op jit(solution)/shard_map/ppermute | solution.py:62
  248.7 8.2 %copy-start.42 = (f32[256]{0:T(256)S(1)}, f32[256]{0:T(256)}, u32[]{:S(2)}) copy-start(f32[256]{0:T(256)} %copy-done.40) | copy-start | bytes 3076
  248.7 8.2 %copy-start.19 = (bf16[256,768]{1,0:T(8,128)(2,1)S(1)}, bf16[256,768]{1,0:T(8,128)(2,1)}, u32[]{:S(2)}) copy-start(bf16[256,768]{1,0:T(8,128)(2,1)} %param.20) | copy-start | bytes 1179652
  248.7 8.2 %copy-start.21 = (f32[256,768]{1,0:T(8,128)S(1)}, f32[256,768]{1,0:T(8,128)}, u32[]{:S(2)}) copy-start(f32[256,768]{1,0:T(8,128)} %convert_add_fusion.6) | copy-start | bytes 2359300
  272.2 14.6 %copy-start.35 = (bf16[1,4736]{1,0:T(2,128)(2,1)S(1)}, bf16[1,4736]{1,0:T(2,128)(2,1)}, u32[]{:S(2)}) copy-start(bf16[1,4736]{1,0:T(2,128)(2,1)} %concatenate.117) | copy-start | bytes 28420
  272.2 4.0 %collective-permute-start.25 = (bf16[1,4736]{1,0:T(2,128)(2,1)}, bf16[1,4736]{1,0:T(2,128)(2,1)S(1)}, u32[]{:S(2)}, u32[]{:S(2)}) collective-permute-start(bf16[1,4736]{1,0:T(2,128)(2,1)} %concatenate.117), channel_id=1, source_target_pairs={{0,4},{4,0},{8,12},{12,8},{16,20},{20,16},{24,28},{28,24},{1,5},{5... | collective-permute-start | bytes 28424 | tf_op jit(solution)/shard_map/ppermute | solution.py:62
  277.0 4.1 %collective-permute-start.26 = (bf16[2,4736]{1,0:T(2,128)(2,1)S(1)}, bf16[2,4736]{1,0:T(2,128)(2,1)S(1)}, u32[]{:S(2)}, u32[]{:S(2)}) collective-permute-start(bf16[2,4736]{1,0:T(2,128)(2,1)S(1)} %pad_maximum_fusion.10), channel_id=1, source_target_pairs={{0,8},{4,12},{8,0},{12,4},{16,24},{20,28},{24,16},{28,20},{1,9},{5... | collective-permute-start | bytes 56840 | tf_op jit(solution)/shard_map/ppermute | solution.py:62
  279.5 28.3 %collective-permute-start.28 = (bf16[8,1,24,3200]{3,2,1,0:T(8,128)(2,1)}, bf16[8,1,24,3200]{3,2,1,0:T(8,128)(2,1)S(1)}, u32[]{:S(2)}, u32[]{:S(2)}) collective-permute-start(bf16[8,1,24,3200]{3,2,1,0:T(8,128)(2,1)} %dynamic-slice_convert_fusion), channel_id=1, source_target_pairs={{0,2},{1,3},{2,0},{3,1},{4,6},{5,7},{6,4},{7,5},{8,10},{9,11},{10,... | collective-permute-start | bytes 3686408 | tf_op jit(solution)/shard_map/ppermute | solution.py:62
  281.8 5.0 %collective-permute-start.27 = (bf16[4,4736]{1,0:T(4,128)(2,1)S(1)}, bf16[4,4736]{1,0:T(4,128)(2,1)S(1)}, u32[]{:S(2)}, u32[]{:S(2)}) collective-permute-start(bf16[4,4736]{1,0:T(4,128)(2,1)S(1)} %pad_maximum_fusion.9), channel_id=1, source_target_pairs={{0,16},{4,20},{8,24},{12,28},{16,0},{20,4},{24,8},{28,12},{1,17},{... | collective-permute-start | bytes 113672 | tf_op jit(solution)/shard_map/ppermute | solution.py:62
  310.3 10.0 %collective-permute-start.29 = (bf16[8,4736]{1,0:T(8,128)(2,1)}, bf16[8,4736]{1,0:T(8,128)(2,1)}, u32[]{:S(2)}, u32[]{:S(2)}) collective-permute-start(bf16[8,4736]{1,0:T(8,128)(2,1)} %pad_maximum_fusion.8), channel_id=1, source_target_pairs={{0,1},{1,0},{2,3},{3,2},{4,5},{5,4},{6,7},{7,6},{8,9},{9,8},{10,11... | collective-permute-start | bytes 227336 | tf_op jit(solution)/shard_map/ppermute | solution.py:62
  310.8 34.9 %all-to-all-start.4 = ((bf16[8,24,3200]{2,1,0:T(8,128)(2,1)}), bf16[8,24,3200]{2,1,0:T(8,128)(2,1)}, u32[]{:S(2)}, u32[]{:S(2)}) async-start(bf16[8,24,3200]{2,1,0:T(8,128)(2,1)} %bitcast.98), calls=%async_computation.4 | async-start | bytes 2457600 | tf_op jit(solution)/shard_map/all_to_all | solution.py:133
  316.8 6.0 %copy-start.32 = (bf16[768,768]{1,0:T(8,128)(2,1)S(1)}, bf16[768,768]{1,0:T(8,128)(2,1)}, u32[]{:S(2)}) copy-start(bf16[768,768]{1,0:T(8,128)(2,1)} %get-tuple-element.129) | copy-start | bytes 3538948
  321.2 5.6 %collective-permute-start.30 = (bf16[16,4736]{1,0:T(8,128)(2,1)S(1)}, bf16[16,4736]{1,0:T(8,128)(2,1)S(1)}, u32[]{:S(2)}, u32[]{:S(2)}) collective-permute-start(bf16[16,4736]{1,0:T(8,128)(2,1)S(1)} %pad_maximum_fusion.7), channel_id=1, source_target_pairs={{0,2},{1,3},{2,0},{3,1},{4,6},{5,7},{6,4},{7,5},{8,10},{9,11},{10,... | collective-permute-start | bytes 454664 | tf_op jit(solution)/shard_map/ppermute | solution.py:62
  347.8 5.4 %collective-permute-start.31 = (bf16[24,3200]{1,0:T(8,128)(2,1)}, bf16[24,3200]{1,0:T(8,128)(2,1)S(1)}, u32[]{:S(2)}, u32[]{:S(2)}) collective-permute-start(bf16[24,3200]{1,0:T(8,128)(2,1)} %reduce_sum.221), channel_id=1, source_target_pairs={{0,2},{1,3},{2,0},{3,1},{4,6},{5,7},{6,4},{7,5},{8,10},{9,11},{10,... | collective-permute-start | bytes 460808 | tf_op jit(solution)/shard_map/ppermute | solution.py:62
  354.3 1.7 collective-permute-start.32
  (47 other events, 153.2 us)

commit v4 on v3

--- a/solution.py
+++ b/solution.py
@@ -11,6 +11,7 @@
 HEADS = 12
 HDIM = 64
 SEQ = 256
+PIECES = 4
 
 
 eps_norm = 1e-06
@@ -103,11 +104,11 @@
 
 
 def reduce_more(rows):
-    for mask in bits_of("hid")[1:]:
+    for mask in bits_of("hid")[1:-1]:
         half = rows.shape[0] // 2
-        moved = swap(low(rows[half:]), "hid", mask)
-        rows = rows[:half] + moved.astype(jnp.float32)
-    return rows
+        rows = rows[:half] + swap(low(rows[half:]), "hid", mask).astype(jnp.float32)
+    half = rows.shape[0] // 2
+    return rows[:half], swap(low(rows[half:]), "hid", bits_of("hid")[-1])
 
 
 def reduce_step(values, axis, step):
@@ -509,7 +510,8 @@
         for rows, grads in zip(tokens_all, grad_tokens)
     ]
     term_part, sum_part, act_shared, back_shared = zip(*halves)
-    shared_term = reduce_more(reduce_rows(term_part)[0])
+    near_term, far_term = reduce_more(reduce_rows(term_part)[0])
+    shared_term = near_term + far_term.astype(jnp.float32)
     weight_shared = shared_outer(*tokens_all, *grad_tokens, *act_shared, *back_shared)
 
     received, weight_shared = lax.optimization_barrier((received, weight_shared))
@@ -552,14 +554,23 @@
         added=[shares[kind, r] for kind in range(2) for r in blocks],
     )
     (kept_in, sent_in), (kept_out, sent_out) = made_in, made_out
-    grad_back, expert_rows, sent_in, sent_out, weight_shared, shared_sum = (
-        lax.optimization_barrier(
-            (grad_back, expert_rows, sent_in, sent_out, weight_shared, shared_sum)
-        )
-    )
-    shared_sum = reduce_more(shared_sum)
+    near_sum, far_sum = reduce_more(shared_sum)
+    grad_back, expert_rows, sent_in, sent_out, weight_shared, far_sum = lax.optimization_barrier(
+        (grad_back, expert_rows, sent_in, sent_out, weight_shared, far_sum)
+    )
+    shared_sum = near_sum + far_sum.astype(jnp.float32)
+    moved_in = swap(sent_in, "hid", far_mask)
+    cut = sent_out.shape[0] // PIECES
+    moved_out, last = [], moved_in
+    for piece in range(PIECES):
+        last, part = lax.optimization_barrier((last, sent_out[piece * cut : (piece + 1) * cut]))
+        if piece == 0:
+            moved_in = last
+        else:
+            moved_out[-1] = last
+        last = swap(part, "hid", far_mask)
+        moved_out.append(last)
     weight_shared = spread_rest(weight_shared)
-    moved_in, moved_out = swap(sent_in, "hid", far_mask), swap(sent_out, "hid", far_mask)
     back_rows = exchange(expert_rows)
 
     picked_grad = mat_prod(picks, grad_back)
@@ -581,15 +592,13 @@
     grad_gate_one = jnp.sum(branch_one * grad_residual, axis=1)
     grad_branch_one = low((gate_one * grad_residual).reshape(tokens, model_dim))
     grad_attended = low(prod_cols(grad_branch_one, proj_weight))
-    moved_in, moved_out, grad_attended = lax.optimization_barrier(
-        (moved_in, moved_out, grad_attended)
-    )
+    moved_in, grad_attended = lax.optimization_barrier((moved_in, grad_attended))
     grad_qkv = attend(attend_back_body, [qkv_rows, grad_attended], 3 * model_dim, score_scale)
     back_rows, shared_sum, weight_shared, grad_qkv = lax.optimization_barrier(
         (back_rows, shared_sum, weight_shared, grad_qkv)
     )
     padded = jnp.pad(grad_logits, ((0, 0), (0, -experts % 128)))
-    dense, (grad_qkv,) = sum_hid(
+    dense, (moved_out,) = sum_hid(
         jnp.concatenate(
             [
                 low(prod_rows(flat_one, grad_qkv)),
@@ -598,9 +607,10 @@
             ],
             axis=1,
         ),
-        (grad_qkv,),
+        (moved_out,),
     )
     tail = dense[:1, :128]
+    moved_out = jnp.concatenate(moved_out, axis=0)
     weight_expert_in = kept_in.astype(jnp.float32) + after(moved_in, tail).astype(jnp.float32)
     weight_expert_out = kept_out.astype(jnp.float32) + after(moved_out, tail).astype(jnp.float32)
     weight_shared = sum(part.astype(jnp.float32) for part in weight_shared)

time: 367 us -> 348 us (0.948)
  waiting for transfers between devices: 68.8 us -> 55.8 us
  other arithmetic: 58.3 us -> 54.6 us
    ppermute x33 -> x36, waiting for transfers between devices: 68 us -> 55.7 us  [swap(): return lax.ppermute(values, axis, pairs_of(lax.axis_size(axis), mask))]
    ppermute x33 -> x36, starting transfers between devices: 30.9 us -> 31.6 us  [swap(): return lax.ppermute(values, axis, pairs_of(lax.axis_size(axis), mask))]
    unnamed x147 -> x163, local copies, waits for them, and re-layouts: 7.64 us -> 7.64 us
  transfers between devices with their start and end apart: 38 -> 41, of which waited for: 10 -> 9; matrix products, arithmetic and copies ran while one was open for 30% -> 34% of each run, Pallas kernels for 24% -> 26%
where the time goes in v4:
time: 348 us; the launch traced here: 341 us
  Pallas kernels  87.6 us (25%)
  starting transfers between devices  60 us (17%)
  waiting for transfers between devices  55.8 us (16%)
  other arithmetic  54.6 us (16%)
  matrix products  48 us (14%)
  local copies, waits for them, and re-layouts  29.5 us (8%)
  between operations  5.86 us (2%)
    ppermute x36, waiting for transfers between devices, swap(): return lax.ppermute(values, axis, pairs_of(lax.axis_size(axis), mask))  55.7 us
    pallas_call x3, Pallas kernels, expert_pass(): pl.pallas_call(functools.partial(expert_body, blocks, width, gated), out_...  48.8 us
    ppermute x36, starting transfers between devices, swap(): return lax.ppermute(values, axis, pairs_of(lax.axis_size(axis), mask))  31.6 us
    all_to_all x5, starting transfers between devices, exchange(): return lax.all_to_all(rows, 'exp', split_axis=0, concat_axis=0, tiled=True)  28.5 us
    dot_general x11, matrix products, mat_prod(): return jnp.dot(left_side, right_side, preferred_element_type=jnp.float32)  22.2 us
    pallas_call x2, Pallas kernels, outer_pass(): pl.pallas_call(functools.partial(outer_body, blocks, width, bool(added)),...  16.6 us
    dot_general x8, matrix products, prod_rows(): lax.dot_general(left_side, right_side, (((0,), (0,)), ((), ())), preferre...  15.8 us
    pallas_call x2, Pallas kernels, attend(): pl.pallas_call(functools.partial(body, score_scale), grid=(rows // SEQ,),...  15.4 us
  transfers between devices with their start and end apart: 41, of which 9 were waited for; matrix products, arithmetic and copies ran while one was open for 34% of the time, Pallas kernels for 26%

profile of v4, /device:TPU:0, one launch (start us, length us, event | category | flops | bytes accessed | tf_op | source)
XLA Modules:
  0.0 341.4 jit_solution(360519867978837431)
XLA Ops:
  0.7 3.0 collective-permute-start
  5.1 1.7 convolution_reduce_fusion.2
  7.1 4.1 %convolution_reduce_fusion = f32[4608]{0:T(1024)S(1)} fusion(bf16[768,1]{0,1:T(2,128)(2,1)S(1)} %reshape.620, bf16[768,4608]{1,0:T(8,128)(2,1)} %param.28), kind=kOutput, calls=%fused_computation.31 | convolution fusion | flops 7077888 | bytes 7097856 | tf_op jit(solution)/shard_map/dot_general | solution.py:22
  13.4 1.6 convolution_convert_fusion.5
  14.9 5.8 %all-to-all-start = ((bf16[8,72,768]{2,1,0:T(8,128)(2,1)}), bf16[8,72,768]{2,1,0:T(8,128)(2,1)}, u32[]{:S(2)}, u32[]{:S(2)}) async-start(bf16[8,72,768]{2,1,0:T(8,128)(2,1)} %bitcast.108), calls=%async_computation | async-start | bytes 1769472 | tf_op jit(solution)/shard_map/all_to_all | solution.py:134
  26.2 1.8 fusion.30
  28.1 3.2 convolution_convert_fusion.2.rows_ref
  31.3 7.6 %shard_map.298 = bf16[256,768]{1,0:T(8,128)(2,1)} custom-call(bf16[256,2304]{1,0:T(8,128)(2,1)} %convolution_convert_fusion.2.rows_ref), custom_call_target="tpu_custom_call" | custom-call | flops 1000 | bytes 1000 | tf_op jit(solution)/shard_map/pallas_call | solution.py:392
  38.9 2.9 fusion.91
  44.1 1.9 select_reduce_fusion
  47.4 2.9 convolution_convert_fusion.4
  50.3 6.2 %all-to-all-start.1 = ((bf16[8,72,896]{2,1,0:T(8,128)(2,1)}), bf16[8,72,896]{2,1,0:T(8,128)(2,1)}, u32[]{:S(2)}, u32[]{:S(2)}) async-start(bf16[8,72,896]{2,1,0:T(8,128)(2,1)} %bitcast.106), calls=%async_computation.1 | async-start | bytes 2064384 | tf_op jit(solution)/shard_map/all_to_all | solution.py:134
  56.6 1.5 collective-permute-start.3
  60.6 2.4 broadcast_select_fusion
  63.5 5.3 %collective-permute-done.3 = bf16[256,768]{1,0:T(8,128)(2,1)S(1)} collective-permute-done((bf16[256,768]{1,0:T(8,128)(2,1)}, bf16[256,768]{1,0:T(8,128)(2,1)S(1)}, u32[]{:S(2)}, u32[]{:S(2)}) %collective-permute-start.3) | collective-permute-done | bytes 393248 | tf_op jit(solution)/shard_map/ppermute | solution.py:63
  69.8 2.0 pad_maximum_fusion.1.refs_0_.rows_a
  72.8 7.8 %shard_map.299 = (bf16[512,768]{1,0:T(8,128)(2,1)}, bf16[512,768]{1,0:T(8,128)(2,1)}, bf16[512,768]{1,0:T(8,128)(2,1)}, bf16[512,768]{1,0:T(8,128)(2,1)}) custom-call(bf16[512,768]{1,0:T(8,128)(2,1)} %pad_maximum_fusion.1.refs_0_.rows_a, bf16[512,768]{1,0:T(8,128)(2,1)} %pad_maximum_fusion.2.refs_1_.grads_a, bf16[768,768]{1,0:T(8,128)(2,1)} %refs_2_.3, ...), custom_call_target="tpu_custom_call" | custom-call | flops 1000 | bytes 1000 | tf_op jit(solution)/shard_map/pallas_call | solution.py:282
  80.6 7.8 %shard_map.300 = (bf16[512,768]{1,0:T(8,128)(2,1)}, bf16[512,768]{1,0:T(8,128)(2,1)}, bf16[512,768]{1,0:T(8,128)(2,1)}, bf16[512,768]{1,0:T(8,128)(2,1)}) custom-call(bf16[512,768]{1,0:T(8,128)(2,1)} %collective-permute-done.2.refs_0_.rows_b, bf16[512,768]{1,0:T(8,128)(2,1)} %collective-permute-done.4.refs_1_.grads_b, bf16[768,768]{1,0:T(8,128)(2,1)} %refs_2_.3, ...), custom_call_target="tpu_custom_call" | custom-call | flops 1000 | bytes 1000 | tf_op jit(solution)/shard_map/pallas_call | solution.py:282
  88.5 6.8 %shard_map.301 = bf16[2,768,768]{2,1,0:T(8,128)(2,1)} custom-call(bf16[512,768]{1,0:T(8,128)(2,1)} %pad_maximum_fusion.1.refs_0_.rows_a, bf16[512,768]{1,0:T(8,128)(2,1)} %collective-permute-done.2.refs_0_.rows_b, bf16[512,768]{1,0:T(8,128)(2,1)} %pad_maximum_fusion.2.refs_1_.grads_a, bf16[512,768]{1,0:T(8,128)(2,1)} %collective-permute-done.4.refs_1_.grads_b, ...), custom_call_target="tpu_custom_call" | custom-call | flops 1000 | bytes 1000 | tf_op jit(solution)/shard_map/pallas_call | solution.py:327
  95.8 1.8 constant_dynamic-slice_fusion.1
  97.7 2.0 collective-permute-start.10
  99.7 33.2 %shard_map.302 = (bf16[576,896]{1,0:T(8,128)(2,1)}, bf16[576,768]{1,0:T(8,128)(2,1)}, bf16[576,768]{1,0:T(8,128)(2,1)}, bf16[576,768]{1,0:T(8,128)(2,1)}, bf16[5...) custom-call(bf16[576,896]{1,0:T(8,128)(2,1)} %bitcast.10.refs_0_, ...), custom_call_target="tpu_custom_call" | custom-call | flops 1000 | bytes 1000 | tf_op jit(solution)/shard_map/pallas_call | solution.py:282
  132.8 1.7 convert_add_fusion.1
  134.5 5.2 %all-to-all-start.2 = ((bf16[8,72,896]{2,1,0:T(8,128)(2,1)}), bf16[8,72,896]{2,1,0:T(8,128)(2,1)}, u32[]{:S(2)}, u32[]{:S(2)}) async-start(bf16[8,72,896]{2,1,0:T(8,128)(2,1)} %bitcast.105), calls=%async_computation.2 | async-start | bytes 2064384 | tf_op jit(solution)/shard_map/all_to_all | solution.py:134
  139.7 7.6 %shard_map.303 = (bf16[768,768]{1,0:T(8,128)(2,1)}, bf16[768,768]{1,0:T(8,128)(2,1)}, bf16[768,768]{1,0:T(8,128)(2,1)}, bf16[768,768]{1,0:T(8,128)(2,1)}) custom-call(bf16[576,896]{1,0:T(8,128)(2,1)} %bitcast.10.refs_0_, bf16[576,768]{1,0:T(8,128)(2,1)} %get-tuple-element.100.refs_1_, bf16[576,768]{1,0:T(8,128)(2,1)} %get-tuple-element.105.refs_2_, ...), custom_call_target="tpu_custom_call" | custom-call | flops 1000 | bytes 1000 | tf_op jit(solution)/shard_map/pallas_call | solution.py:312
  150.1 1.6 convert_add_fusion.3
  151.8 1.6 collective-permute-start.16
  157.1 9.0 %shard_map.304 = (bf16[768,768]{1,0:T(8,128)(2,1)}, bf16[768,768]{1,0:T(8,128)(2,1)}, bf16[768,768]{1,0:T(8,128)(2,1)}, bf16[768,768]{1,0:T(8,128)(2,1)}) custom-call(bf16[576,896]{1,0:T(8,128)(2,1)} %bitcast.10.refs_0_, bf16[576,768]{1,0:T(8,128)(2,1)} %get-tuple-element.100.refs_1_, bf16[576,768]{1,0:T(8,128)(2,1)} %get-tuple-element.101.refs_2_, ...), custom_call_target="tpu_custom_call" | custom-call | flops 1000 | bytes 1000 | tf_op jit(solution)/shard_map/pallas_call | solution.py:312
  166.1 6.5 %all-to-all-start.3 = ((bf16[8,72,768]{2,1,0:T(8,128)(2,1)}), bf16[8,72,768]{2,1,0:T(8,128)(2,1)}, u32[]{:S(2)}, u32[]{:S(2)}) async-start(bf16[8,72,768]{2,1,0:T(8,128)(2,1)} %bitcast.107), calls=%async_computation.3 | async-start | bytes 1769472 | tf_op jit(solution)/shard_map/all_to_all | solution.py:134
  172.6 2.4 fusion.41
  175.0 2.0 collective-permute-start.17
  177.0 2.4 collective-permute-start.18
  179.6 1.6 collective-permute-start.20
  181.2 2.1 fusion.47
  184.0 1.7 multiply_reduce_fusion
  185.7 2.1 convolution_convert_fusion.7
  189.0 2.0 slice_add_fusion.1
  193.5 13.2 %collective-permute-done.20 = bf16[768,768]{1,0:T(8,128)(2,1)} collective-permute-done((bf16[768,768]{1,0:T(8,128)(2,1)}, bf16[768,768]{1,0:T(8,128)(2,1)}, u32[]{:S(2)}, u32[]{:S(2)}) %collective-permute-start.20) | collective-permute-done | bytes 1179680 | tf_op jit(solution)/shard_map/ppermute | solution.py:63
  208.2 1.9 dynamic-slice_bitcast_fusion.1
  211.9 1.5 convolution_convert_fusion.3
  213.5 7.8 %shard_map.305 = bf16[256,2304]{1,0:T(8,128)(2,1)} custom-call(bf16[256,2304]{1,0:T(8,128)(2,1)} %convolution_convert_fusion.2.rows_ref, bf16[256,768]{1,0:T(8,128)(2,1)} %convolution_convert_fusion.6.grad_ref), custom_call_target="tpu_custom_call" | custom-call | flops 1000 | bytes 1000 | tf_op jit(solution)/shard_map/pallas_call | solution.py:392
  221.9 2.8 convolution_convert_fusion.1
  225.2 1.6 dynamic-slice_bitcast_fusion
  228.2 2.6 fusion.20
  232.0 2.0 fusion.46
  237.7 1.7 collective-permute-start.23
  240.7 2.6 fusion.19
  247.9 7.0 %collective-permute-done.29 = bf16[192,768]{1,0:T(8,128)(2,1)S(1)} collective-permute-done((bf16[192,768]{1,0:T(8,128)(2,1)S(1)}, bf16[192,768]{1,0:T(8,128)(2,1)S(1)}, u32[]{:S(2)}, u32[]{:S(2)}) %collective-permute-start.29) | collective-permute-done | bytes 294944 | tf_op jit(solution)/shard_map/ppermute | solution.py:63
  256.3 2.9 convert_add_fusion
  259.4 3.8 %collective-permute-done.30 = bf16[192,768]{1,0:T(8,128)(2,1)S(1)} collective-permute-done((bf16[192,768]{1,0:T(8,128)(2,1)S(1)}, bf16[192,768]{1,0:T(8,128)(2,1)S(1)}, u32[]{:S(2)}, u32[]{:S(2)}) %collective-permute-start.30) | collective-permute-done | bytes 294944 | tf_op jit(solution)/shard_map/ppermute | solution.py:63
  264.7 1.5 collective-permute-start.25
  267.0 2.6 collective-permute-done.25
  270.3 20.2 %collective-permute-done.31 = bf16[8,1,24,3200]{3,2,1,0:T(8,128)(2,1)S(1)} collective-permute-done((bf16[8,1,24,3200]{3,2,1,0:T(8,128)(2,1)S(1)}, bf16[8,1,24,3200]{3,2,1,0:T(8,128)(2,1)S(1)}, u32[]{:S(2)}, u32[]{:S(2)}) %collective-permute-start.31) | collective-permute-done | bytes 1228832 | tf_op jit(solution)/shard_map/ppermute | solution.py:63
  291.9 4.8 %all-to-all-start.4 = ((bf16[8,24,3200]{2,1,0:T(8,128)(2,1)}), bf16[8,24,3200]{2,1,0:T(8,128)(2,1)}, u32[]{:S(2)}, u32[]{:S(2)}) async-start(bf16[8,24,3200]{2,1,0:T(8,128)(2,1)} %bitcast.98), calls=%async_computation.4 | async-start | bytes 2457600 | tf_op jit(solution)/shard_map/all_to_all | solution.py:134
  298.0 3.5 %add_bitcast_fusion.1 = f32[1,768,768]{2,1,0:T(8,128)} fusion(bf16[768,768]{1,0:T(8,128)(2,1)} %get-tuple-element.144, bf16[768,768]{1,0:T(8,128)(2,1)} %collective-permute-done.20, pred[]{:T(512)} %bitcast.41), kind=kLoop, calls=%fused_computation.10 | loop fusion | flops 2359296 | bytes 4718593 | tf_op jit(solution)/shard_map/broadcast_in_dim | solution.py:695
  302.4 1.5 collective-permute-start.33
  303.9 2.8 add_bitcast_fusion
  314.4 1.8 add_divide_fusion
  316.2 5.7 %fusion.94 = (f32[768]{0:T(1024)}, bf16[32,768]{1,0:T(8,128)(2,1)S(1)}) fusion(f32[32,768]{1,0:T(8,128)S(1)} %get-tuple-element.237, bf16[768,4608]{1,0:T(8,128)(2,1)} %param.28, bf16[32,4736]{1,0:T(8,128)(2,1)S(1)} %copy-done.29), kind=kOutput, calls=%fused_computation.216 | convolution fusion | flops 226761984 | bytes 7523328 | tf_op jit(solution)/shard_map/dot_general | solution.py:32
  322.8 1.7 fusion.42
  324.5 2.3 fusion.48
  326.9 2.2 reduce_sum.221
  331.1 1.6 convert_reduce_fusion.1
  332.7 1.8 collective-permute-done.34
  (310 shorter events, 67.1 us)
Async XLA Ops:
  0.6 27.4 %copy-start = (bf16[768,2304]{1,0:T(8,128)(2,1)S(1)}, bf16[768,2304]{1,0:T(8,128)(2,1)}, u32[]{:S(2)}) copy-start(bf16[768,2304]{1,0:T(8,128)(2,1)} %param.30) | copy-start | bytes 10616836
  0.7 6.2 %copy-start.31 = (bf16[256,768]{1,0:T(8,128)(2,1)S(1)}, bf16[256,768]{1,0:T(8,128)(2,1)}, u32[]{:S(2)}) copy-start(bf16[256,768]{1,0:T(8,128)(2,1)} %param.25) | copy-start | bytes 1179652
  0.7 6.4 %copy-start.59 = (f32[768]{0:T(1024)S(1)}, f32[768]{0:T(1024)}, u32[]{:S(2)}) copy-start(f32[768]{0:T(1024)} %param.26) | copy-start | bytes 9220
  0.7 30.6 %collective-permute-start = (bf16[768,768]{1,0:T(8,128)(2,1)}, bf16[768,768]{1,0:T(8,128)(2,1)}, u32[]{:S(2)}, u32[]{:S(2)}) collective-permute-start(bf16[768,768]{1,0:T(8,128)(2,1)} %bitcast.2.refs_2_), channel_id=1, source_target_pairs={{0,2},{1,3},{2,0},{3,1},{4,6},{5,7},{6,4},{7,5},{8,10},{9,11},{10,... | collective-permute-start | bytes 3538952 | tf_op jit(solution)/shard_map/ppermute | solution.py:63
  7.1 5.4 %copy-start.16 = (bf16[256,768]{1,0:T(8,128)(2,1)S(1)}, bf16[256,768]{1,0:T(8,128)(2,1)}, u32[]{:S(2)}) copy-start(bf16[256,768]{1,0:T(8,128)(2,1)} %param.20) | copy-start | bytes 1179652
  14.9 35.4 %all-to-all-start = ((bf16[8,72,768]{2,1,0:T(8,128)(2,1)}), bf16[8,72,768]{2,1,0:T(8,128)(2,1)}, u32[]{:S(2)}, u32[]{:S(2)}) async-start(bf16[8,72,768]{2,1,0:T(8,128)(2,1)} %bitcast.108), calls=%async_computation | async-start | bytes 1769472 | tf_op jit(solution)/shard_map/all_to_all | solution.py:134
  25.0 6.3 %copy-start.52 = (f32[256]{0:T(256)}, f32[256]{0:T(256)S(1)}, u32[]{:S(2)}) copy-start(f32[256]{0:T(256)S(1)} %broadcast_multiply_fusion.5) | copy-start | bytes 3076
  41.8 5.4 %copy-start.78 = (pred[128]{0:T(512)(128)(4,1)S(1)}, pred[128]{0:T(512)(128)(4,1)}, u32[]{:S(2)}) copy-start(pred[128]{0:T(512)(128)(4,1)} %get-tuple-element.242) | copy-start | bytes 388
  41.8 5.4 %copy-start.79 = (pred[128]{0:T(512)(128)(4,1)S(1)}, pred[128]{0:T(512)(128)(4,1)}, u32[]{:S(2)}) copy-start(pred[128]{0:T(512)(128)(4,1)} %get-tuple-element.243) | copy-start | bytes 388
  41.8 5.6 %copy-start.22 = (bf16[256,576]{1,0:T(8,128)(2,1)S(1)}, bf16[256,576]{1,0:T(8,128)(2,1)}, u32[]{:S(2)}) copy-start(bf16[256,576]{1,0:T(8,128)(2,1)} %get-tuple-element.238) | copy-start | bytes 884740
  41.8 5.6 %copy-start.25 = (bf16[256,576]{1,0:T(8,128)(2,1)S(1)}, bf16[256,576]{1,0:T(8,128)(2,1)}, u32[]{:S(2)}) copy-start(bf16[256,576]{1,0:T(8,128)(2,1)} %get-tuple-element.239) | copy-start | bytes 884740
  41.8 5.4 %copy-start.54 = (f32[256]{0:T(256)}, f32[256]{0:T(256)S(1)}, u32[]{:S(2)}) copy-start(f32[256]{0:T(256)S(1)} %broadcast_multiply_fusion.4) | copy-start | bytes 3076
  43.6 14.5 %collective-permute-start.1 = (bf16[256,768]{1,0:T(8,128)(2,1)}, bf16[256,768]{1,0:T(8,128)(2,1)}, u32[]{:S(2)}, u32[]{:S(2)}) collective-permute-start(bf16[256,768]{1,0:T(8,128)(2,1)} %add_convert_fusion.2), channel_id=1, source_target_pairs={{0,2},{1,3},{2,0},{3,1},{4,6},{5,7},{6,4},{7,5},{8,10},{9,11},{10,... | collective-permute-start | bytes 1179656 | tf_op jit(solution)/shard_map/ppermute | solution.py:63
  50.3 45.5 %all-to-all-start.1 = ((bf16[8,72,896]{2,1,0:T(8,128)(2,1)}), bf16[8,72,896]{2,1,0:T(8,128)(2,1)}, u32[]{:S(2)}, u32[]{:S(2)}) async-start(bf16[8,72,896]{2,1,0:T(8,128)(2,1)} %bitcast.106), calls=%async_computation.1 | async-start | bytes 2064384 | tf_op jit(solution)/shard_map/all_to_all | solution.py:134
  56.6 12.3 %copy-start.33 = (bf16[256,768]{1,0:T(8,128)(2,1)S(1)}, bf16[256,768]{1,0:T(8,128)(2,1)}, u32[]{:S(2)}) copy-start(bf16[256,768]{1,0:T(8,128)(2,1)} %copy-done.32) | copy-start | bytes 1179652
  56.6 12.3 %collective-permute-start.3 = (bf16[256,768]{1,0:T(8,128)(2,1)}, bf16[256,768]{1,0:T(8,128)(2,1)S(1)}, u32[]{:S(2)}, u32[]{:S(2)}) collective-permute-start(bf16[256,768]{1,0:T(8,128)(2,1)} %copy-done.32), channel_id=1, source_target_pairs={{0,2},{1,3},{2,0},{3,1},{4,6},{5,7},{6,4},{7,5},{8,10},{9,11},{10,... | collective-permute-start | bytes 1179656 | tf_op jit(solution)/shard_map/ppermute | solution.py:63
  63.0 32.3 %collective-permute-start.8 = (bf16[768,768]{1,0:T(8,128)(2,1)}, bf16[768,768]{1,0:T(8,128)(2,1)}, u32[]{:S(2)}, u32[]{:S(2)}) collective-permute-start(bf16[768,768]{1,0:T(8,128)(2,1)} %broadcast_select_fusion), channel_id=1, source_target_pairs={{0,2},{1,3},{2,0},{3,1},{4,6},{5,7},{6,4},{7,5},{8,10},{9,11},{10,... | collective-permute-start | bytes 3538952 | tf_op jit(solution)/shard_map/ppermute | solution.py:63
  69.8 10.8 %collective-permute-start.4 = (bf16[512,768]{1,0:T(8,128)(2,1)}, bf16[512,768]{1,0:T(8,128)(2,1)}, u32[]{:S(2)}, u32[]{:S(2)}) collective-permute-start(bf16[512,768]{1,0:T(8,128)(2,1)} %pad_maximum_fusion.2.refs_1_.grads_a), channel_id=1, source_target_pairs={{0,1},{1,0},{2,3},{3,2},{4,5},{5,4},{6,7},{7,6},{8,9},{9,8},{10,11... | collective-permute-start | bytes 2359304 | tf_op jit(solution)/shard_map/ppermute | solution.py:63
  71.8 8.8 %collective-permute-start.2 = (bf16[512,768]{1,0:T(8,128)(2,1)}, bf16[512,768]{1,0:T(8,128)(2,1)}, u32[]{:S(2)}, u32[]{:S(2)}) collective-permute-start(bf16[512,768]{1,0:T(8,128)(2,1)} %pad_maximum_fusion.1.refs_0_.rows_a), channel_id=1, source_target_pairs={{0,1},{1,0},{2,3},{3,2},{4,5},{5,4},{6,7},{7,6},{8,9},{9,8},{10,11... | collective-permute-start | bytes 2359304 | tf_op jit(solution)/shard_map/ppermute | solution.py:63
  72.3 27.3 %collective-permute-start.5 = (bf16[768,768]{1,0:T(8,128)(2,1)}, bf16[768,768]{1,0:T(8,128)(2,1)}, u32[]{:S(2)}, u32[]{:S(2)}) collective-permute-start(bf16[768,768]{1,0:T(8,128)(2,1)} %bitcast.2.refs_2_), channel_id=1, source_target_pairs={{0,1},{1,0},{2,3},{3,2},{4,5},{5,4},{6,7},{7,6},{8,9},{9,8},{10,11... | collective-permute-start | bytes 3538952 | tf_op jit(solution)/shard_map/ppermute | solution.py:63
  72.3 27.3 %collective-permute-start.7 = (bf16[768,768]{1,0:T(8,128)(2,1)}, bf16[768,768]{1,0:T(8,128)(2,1)}, u32[]{:S(2)}, u32[]{:S(2)}) collective-permute-start(bf16[768,768]{1,0:T(8,128)(2,1)} %bitcast.11.refs_6_), channel_id=1, source_target_pairs={{0,1},{1,0},{2,3},{3,2},{4,5},{5,4},{6,7},{7,6},{8,9},{9,8},{10,11... | collective-permute-start | bytes 3538952 | tf_op jit(solution)/shard_map/ppermute | solution.py:63
  80.6 19.0 %collective-permute-start.6 = (bf16[768,768]{1,0:T(8,128)(2,1)}, bf16[768,768]{1,0:T(8,128)(2,1)}, u32[]{:S(2)}, u32[]{:S(2)}) collective-permute-start(bf16[768,768]{1,0:T(8,128)(2,1)} %collective-permute-done.refs_4_), channel_id=1, source_target_pairs={{0,1},{1,0},{2,3},{3,2},{4,5},{5,4},{6,7},{7,6},{8,9},{9,8},{10,11... | collective-permute-start | bytes 3538952 | tf_op jit(solution)/shard_map/ppermute | solution.py:63
  95.3 4.4 %collective-permute-start.9 = (bf16[768,768]{1,0:T(8,128)(2,1)}, bf16[768,768]{1,0:T(8,128)(2,1)}, u32[]{:S(2)}, u32[]{:S(2)}) collective-permute-start(bf16[768,768]{1,0:T(8,128)(2,1)} %collective-permute-done.8.refs_8_), channel_id=1, source_target_pairs={{0,1},{1,0},{2,3},{3,2},{4,5},{5,4},{6,7},{7,6},{8,9},{9,8},{10,11... | collective-permute-start | bytes 3538952 | tf_op jit(solution)/shard_map/ppermute | solution.py:63
  97.7 35.2 %collective-permute-start.10 = (bf16[2,4,96,768]{3,2,0,1:T(8,128)(2,1)S(1)}, bf16[2,4,96,768]{3,2,0,1:T(8,128)(2,1)S(1)}, u32[]{:S(2)}, u32[]{:S(2)}) collective-permute-start(bf16[2,4,96,768]{3,2,0,1:T(8,128)(2,1)S(1)} %bitcast.104), channel_id=1, source_target_pairs={{0,4},{4,0},{8,12},{12,8},{16,20},{20,16},{24,28},{28,24},{1,5},{5... | collective-permute-start | bytes 3538952 | tf_op jit(solution)/shard_map/ppermute | solution.py:63
  134.5 5.2 %collective-permute-start.11 = (bf16[512,768]{1,0:T(8,128)(2,1)}, bf16[512,768]{1,0:T(8,128)(2,1)}, u32[]{:S(2)}, u32[]{:S(2)}) collective-permute-start(bf16[512,768]{1,0:T(8,128)(2,1)} %get-tuple-element.99), channel_id=1, source_target_pairs={{0,1},{1,0},{2,3},{3,2},{4,5},{5,4},{6,7},{7,6},{8,9},{9,8},{10,11... | collective-permute-start | bytes 2359304 | tf_op jit(solution)/shard_map/ppermute | solution.py:63
  134.5 31.6 %all-to-all-start.2 = ((bf16[8,72,896]{2,1,0:T(8,128)(2,1)}), bf16[8,72,896]{2,1,0:T(8,128)(2,1)}, u32[]{:S(2)}, u32[]{:S(2)}) async-start(bf16[8,72,896]{2,1,0:T(8,128)(2,1)} %bitcast.105), calls=%async_computation.2 | async-start | bytes 2064384 | tf_op jit(solution)/shard_map/all_to_all | solution.py:134
  139.7 12.1 %collective-permute-start.21 = (bf16[512,768]{1,0:T(8,128)(2,1)}, bf16[512,768]{1,0:T(8,128)(2,1)}, u32[]{:S(2)}, u32[]{:S(2)}) collective-permute-start(bf16[512,768]{1,0:T(8,128)(2,1)} %get-tuple-element.125), channel_id=1, source_target_pairs={{0,1},{1,0},{2,3},{3,2},{4,5},{5,4},{6,7},{7,6},{8,9},{9,8},{10,11... | collective-permute-start | bytes 2359304 | tf_op jit(solution)/shard_map/ppermute | solution.py:63
  147.3 9.3 %collective-permute-start.12 = (bf16[768,768]{1,0:T(8,128)(2,1)}, bf16[768,768]{1,0:T(8,128)(2,1)}, u32[]{:S(2)}, u32[]{:S(2)}) collective-permute-start(bf16[768,768]{1,0:T(8,128)(2,1)} %get-tuple-element.109), channel_id=1, source_target_pairs={{0,1},{1,0},{2,3},{3,2},{4,5},{5,4},{6,7},{7,6},{8,9},{9,8},{10,11... | collective-permute-start | bytes 3538952 | tf_op jit(solution)/shard_map/ppermute | solution.py:63
  147.8 9.3 %collective-permute-start.13 = (bf16[768,768]{1,0:T(8,128)(2,1)}, bf16[768,768]{1,0:T(8,128)(2,1)}, u32[]{:S(2)}, u32[]{:S(2)}) collective-permute-start(bf16[768,768]{1,0:T(8,128)(2,1)} %get-tuple-element.110), channel_id=1, source_target_pairs={{0,1},{1,0},{2,3},{3,2},{4,5},{5,4},{6,7},{7,6},{8,9},{9,8},{10,11... | collective-permute-start | bytes 3538952 | tf_op jit(solution)/shard_map/ppermute | solution.py:63
  147.9 9.2 %collective-permute-start.14 = (bf16[768,768]{1,0:T(8,128)(2,1)}, bf16[768,768]{1,0:T(8,128)(2,1)}, u32[]{:S(2)}, u32[]{:S(2)}) collective-permute-start(bf16[768,768]{1,0:T(8,128)(2,1)} %get-tuple-element.111), channel_id=1, source_target_pairs={{0,1},{1,0},{2,3},{3,2},{4,5},{5,4},{6,7},{7,6},{8,9},{9,8},{10,11... | collective-permute-start | bytes 3538952 | tf_op jit(solution)/shard_map/ppermute | solution.py:63
  148.3 8.8 %collective-permute-start.15 = (bf16[768,768]{1,0:T(8,128)(2,1)}, bf16[768,768]{1,0:T(8,128)(2,1)}, u32[]{:S(2)}, u32[]{:S(2)}) collective-permute-start(bf16[768,768]{1,0:T(8,128)(2,1)} %get-tuple-element.112), channel_id=1, source_target_pairs={{0,1},{1,0},{2,3},{3,2},{4,5},{5,4},{6,7},{7,6},{8,9},{9,8},{10,11... | collective-permute-start | bytes 3538952 | tf_op jit(solution)/shard_map/ppermute | solution.py:63
  151.8 14.3 %collective-permute-start.16 = (bf16[256,768]{1,0:T(8,128)(2,1)S(1)}, bf16[256,768]{1,0:T(8,128)(2,1)}, u32[]{:S(2)}, u32[]{:S(2)}) collective-permute-start(bf16[256,768]{1,0:T(8,128)(2,1)S(1)} %slice.260), channel_id=1, source_target_pairs={{0,2},{1,3},{2,0},{3,1},{4,6},{5,7},{6,4},{7,5},{8,10},{9,11},{10,... | collective-permute-start | bytes 1179656 | tf_op jit(solution)/shard_map/ppermute | solution.py:63
  156.6 27.2 %collective-permute-start.22 = (bf16[256,768]{1,0:T(8,128)(2,1)}, bf16[256,768]{1,0:T(8,128)(2,1)}, u32[]{:S(2)}, u32[]{:S(2)}) collective-permute-start(bf16[256,768]{1,0:T(8,128)(2,1)} %slice.259), channel_id=1, source_target_pairs={{0,2},{1,3},{2,0},{3,1},{4,6},{5,7},{6,4},{7,5},{8,10},{9,11},{10,... | collective-permute-start | bytes 1179656 | tf_op jit(solution)/shard_map/ppermute | solution.py:63
  166.1 55.8 %all-to-all-start.3 = ((bf16[8,72,768]{2,1,0:T(8,128)(2,1)}), bf16[8,72,768]{2,1,0:T(8,128)(2,1)}, u32[]{:S(2)}, u32[]{:S(2)}) async-start(bf16[8,72,768]{2,1,0:T(8,128)(2,1)} %bitcast.107), calls=%async_computation.3 | async-start | bytes 1769472 | tf_op jit(solution)/shard_map/all_to_all | solution.py:134
  172.6 8.6 %copy-start.23 = (bf16[256,576]{1,0:T(8,128)(2,1)S(1)}, bf16[256,576]{1,0:T(8,128)(2,1)}, u32[]{:S(2)}) copy-start(bf16[256,576]{1,0:T(8,128)(2,1)} %get-tuple-element.238) | copy-start | bytes 884740
  172.6 8.6 %copy-start.26 = (bf16[256,576]{1,0:T(8,128)(2,1)S(1)}, bf16[256,576]{1,0:T(8,128)(2,1)}, u32[]{:S(2)}) copy-start(bf16[256,576]{1,0:T(8,128)(2,1)} %get-tuple-element.239) | copy-start | bytes 884740
  175.0 46.9 %collective-permute-start.17 = (bf16[2,96,768]{2,1,0:T(8,128)(2,1)}, bf16[2,96,768]{2,1,0:T(8,128)(2,1)}, u32[]{:S(2)}, u32[]{:S(2)}) collective-permute-start(bf16[2,96,768]{2,1,0:T(8,128)(2,1)} %get-tuple-element.211), channel_id=1, source_target_pairs={{0,8},{4,12},{8,0},{12,4},{16,24},{20,28},{24,16},{28,20},{1,9},{5... | collective-permute-start | bytes 884744 | tf_op jit(solution)/shard_map/ppermute | solution.py:63
  177.0 44.8 %collective-permute-start.18 = (bf16[2,96,768]{2,1,0:T(8,128)(2,1)}, bf16[2,96,768]{2,1,0:T(8,128)(2,1)}, u32[]{:S(2)}, u32[]{:S(2)}) collective-permute-start(bf16[2,96,768]{2,1,0:T(8,128)(2,1)} %get-tuple-element.210), channel_id=1, source_target_pairs={{0,16},{4,20},{8,24},{12,28},{16,0},{20,4},{24,8},{28,12},{1,17},{... | collective-permute-start | bytes 884744 | tf_op jit(solution)/shard_map/ppermute | solution.py:63
  179.5 42.4 %collective-permute-start.19 = (bf16[2,96,768]{2,1,0:T(8,128)(2,1)}, bf16[2,96,768]{2,1,0:T(8,128)(2,1)}, u32[]{:S(2)}, u32[]{:S(2)}) collective-permute-start(bf16[2,96,768]{2,1,0:T(8,128)(2,1)} %get-tuple-element.209), channel_id=1, source_target_pairs={{0,24},{4,28},{8,16},{12,20},{16,8},{20,12},{24,0},{28,4},{1,25},{... | collective-permute-start | bytes 884744 | tf_op jit(solution)/shard_map/ppermute | solution.py:63
  179.6 27.2 %collective-permute-start.20 = (bf16[768,768]{1,0:T(8,128)(2,1)}, bf16[768,768]{1,0:T(8,128)(2,1)}, u32[]{:S(2)}, u32[]{:S(2)}) collective-permute-start(bf16[768,768]{1,0:T(8,128)(2,1)} %get-tuple-element.120), channel_id=1, source_target_pairs={{0,2},{1,3},{2,0},{3,1},{4,6},{5,7},{6,4},{7,5},{8,10},{9,11},{10,... | collective-permute-start | bytes 3538952 | tf_op jit(solution)/shard_map/ppermute | solution.py:63
  191.4 20.5 %copy-start.6 = (f32[256,768]{1,0:T(8,128)}, f32[256,768]{1,0:T(8,128)S(1)}, u32[]{:S(2)}) copy-start(f32[256,768]{1,0:T(8,128)S(1)} %get-tuple-element.203) | copy-start | bytes 2359300
  192.3 19.6 %copy-start.15 = (bf16[256,768]{1,0:T(8,128)(2,1)S(1)}, bf16[256,768]{1,0:T(8,128)(2,1)}, u32[]{:S(2)}) copy-start(bf16[256,768]{1,0:T(8,128)(2,1)} %shard_map.298) | copy-start | bytes 1179652
  206.8 14.5 %collective-permute-start.27 = (bf16[192,768]{1,0:T(8,128)(2,1)}, bf16[192,768]{1,0:T(8,128)(2,1)}, u32[]{:S(2)}, u32[]{:S(2)}) collective-permute-start(bf16[192,768]{1,0:T(8,128)(2,1)} %get-tuple-element.130), channel_id=1, source_target_pairs={{0,2},{1,3},{2,0},{3,1},{4,6},{5,7},{6,4},{7,5},{8,10},{9,11},{10,... | collective-permute-start | bytes 884744 | tf_op jit(solution)/shard_map/ppermute | solution.py:63
  213.4 8.5 %copy-start.53 = (f32[256]{0:T(256)S(1)}, f32[256]{0:T(256)}, u32[]{:S(2)}) copy-start(f32[256]{0:T(256)} %copy-done.52) | copy-start | bytes 3076
  213.5 8.5 %copy-start.58 = (f32[256]{0:T(256)S(1)}, f32[256]{0:T(256)}, u32[]{:S(2)}) copy-start(f32[256]{0:T(256)} %copy-done.57) | copy-start | bytes 3076
  221.3 24.4 %collective-permute-start.28 = (bf16[192,768]{1,0:T(8,128)(2,1)}, bf16[192,768]{1,0:T(8,128)(2,1)}, u32[]{:S(2)}, u32[]{:S(2)}) collective-permute-start(bf16[192,768]{1,0:T(8,128)(2,1)} %get-tuple-element.132), channel_id=1, source_target_pairs={{0,2},{1,3},{2,0},{3,1},{4,6},{5,7},{6,4},{7,5},{8,10},{9,11},{10,... | collective-permute-start | bytes 884744 | tf_op jit(solution)/shard_map/ppermute | solution.py:63
  228.2 28.2 %collective-permute-start.26 = (bf16[8,2,24,3200]{3,2,1,0:T(8,128)(2,1)}, bf16[8,2,24,3200]{3,2,1,0:T(8,128)(2,1)}, u32[]{:S(2)}, u32[]{:S(2)}) collective-permute-start(bf16[8,2,24,3200]{3,2,1,0:T(8,128)(2,1)} %dynamic-slice_bitcast_fusion), channel_id=1, source_target_pairs={{0,1},{1,0},{2,3},{3,2},{4,5},{5,4},{6,7},{7,6},{8,9},{9,8},{10,11... | collective-permute-start | bytes 7372808 | tf_op jit(solution)/shard_map/ppermute | solution.py:63
  237.7 5.6 %copy-start.30 = (f32[2,96,768]{2,1,0:T(8,128)S(1)}, f32[2,96,768]{2,1,0:T(8,128)}, u32[]{:S(2)}) copy-start(f32[2,96,768]{2,1,0:T(8,128)} %dynamic-slice_bitcast_fusion.1) | copy-start | bytes 1769476
  237.7 9.5 %collective-permute-start.23 = (bf16[1,4736]{1,0:T(2,128)(2,1)}, bf16[1,4736]{1,0:T(2,128)(2,1)S(1)}, u32[]{:S(2)}, u32[]{:S(2)}) collective-permute-start(bf16[1,4736]{1,0:T(2,128)(2,1)} %concatenate.119), channel_id=1, source_target_pairs={{0,4},{4,0},{8,12},{12,8},{16,20},{20,16},{24,28},{28,24},{1,5},{5... | collective-permute-start | bytes 28424 | tf_op jit(solution)/shard_map/ppermute | solution.py:63
  243.3 11.6 %copy-start.39 = (bf16[192,768]{1,0:T(8,128)(2,1)S(1)}, bf16[192,768]{1,0:T(8,128)(2,1)}, u32[]{:S(2)}) copy-start(bf16[192,768]{1,0:T(8,128)(2,1)} %get-tuple-element.136) | copy-start | bytes 884740
  245.7 9.1 %collective-permute-start.29 = (bf16[192,768]{1,0:T(8,128)(2,1)S(1)}, bf16[192,768]{1,0:T(8,128)(2,1)S(1)}, u32[]{:S(2)}, u32[]{:S(2)}) collective-permute-start(bf16[192,768]{1,0:T(8,128)(2,1)S(1)} %copy-done.40), channel_id=1, source_target_pairs={{0,2},{1,3},{2,0},{3,1},{4,6},{5,7},{6,4},{7,5},{8,10},{9,11},{10,... | collective-permute-start | bytes 884744 | tf_op jit(solution)/shard_map/ppermute | solution.py:63
  247.2 17.4 %collective-permute-start.24 = (bf16[2,4736]{1,0:T(2,128)(2,1)S(1)}, bf16[2,4736]{1,0:T(2,128)(2,1)S(1)}, u32[]{:S(2)}, u32[]{:S(2)}) collective-permute-start(bf16[2,4736]{1,0:T(2,128)(2,1)S(1)} %pad_maximum_fusion.10), channel_id=1, source_target_pairs={{0,8},{4,12},{8,0},{12,4},{16,24},{20,28},{24,16},{28,20},{1,9},{5... | collective-permute-start | bytes 56840 | tf_op jit(solution)/shard_map/ppermute | solution.py:63
  254.9 8.3 %collective-permute-start.30 = (bf16[192,768]{1,0:T(8,128)(2,1)S(1)}, bf16[192,768]{1,0:T(8,128)(2,1)S(1)}, u32[]{:S(2)}, u32[]{:S(2)}) collective-permute-start(bf16[192,768]{1,0:T(8,128)(2,1)S(1)} %copy-done.39), channel_id=1, source_target_pairs={{0,2},{1,3},{2,0},{3,1},{4,6},{5,7},{6,4},{7,5},{8,10},{9,11},{10,... | collective-permute-start | bytes 884744 | tf_op jit(solution)/shard_map/ppermute | solution.py:63
  263.1 27.7 %copy-start.43 = (bf16[192,768]{1,0:T(8,128)(2,1)}, bf16[192,768]{1,0:T(8,128)(2,1)S(1)}, u32[]{:S(2)}) copy-start(bf16[192,768]{1,0:T(8,128)(2,1)S(1)} %collective-permute-done.30) | copy-start | bytes 884740
  263.1 27.4 %collective-permute-start.31 = (bf16[8,1,24,3200]{3,2,1,0:T(8,128)(2,1)S(1)}, bf16[8,1,24,3200]{3,2,1,0:T(8,128)(2,1)S(1)}, u32[]{:S(2)}, u32[]{:S(2)}) collective-permute-start(bf16[8,1,24,3200]{3,2,1,0:T(8,128)(2,1)S(1)} %dynamic-slice_convert_fusion), channel_id=1, source_target_pairs={{0,2},{1,3},{2,0},{3,1},{4,6},{5,7},{6,4},{7,5},{8,10},{9,11},{10,... | collective-permute-start | bytes 3686408 | tf_op jit(solution)/shard_map/ppermute | solution.py:63
  264.7 4.9 %collective-permute-start.25 = (bf16[4,4736]{1,0:T(4,128)(2,1)S(1)}, bf16[4,4736]{1,0:T(4,128)(2,1)S(1)}, u32[]{:S(2)}, u32[]{:S(2)}) collective-permute-start(bf16[4,4736]{1,0:T(4,128)(2,1)S(1)} %pad_maximum_fusion.9), channel_id=1, source_target_pairs={{0,16},{4,20},{8,24},{12,28},{16,0},{20,4},{24,8},{28,12},{1,17},{... | collective-permute-start | bytes 113672 | tf_op jit(solution)/shard_map/ppermute | solution.py:63
  291.4 10.1 %collective-permute-start.32 = (bf16[8,4736]{1,0:T(8,128)(2,1)}, bf16[8,4736]{1,0:T(8,128)(2,1)}, u32[]{:S(2)}, u32[]{:S(2)}) collective-permute-start(bf16[8,4736]{1,0:T(8,128)(2,1)} %pad_maximum_fusion.8), channel_id=1, source_target_pairs={{0,1},{1,0},{2,3},{3,2},{4,5},{5,4},{6,7},{7,6},{8,9},{9,8},{10,11... | collective-permute-start | bytes 227336 | tf_op jit(solution)/shard_map/ppermute | solution.py:63
  291.9 35.0 %all-to-all-start.4 = ((bf16[8,24,3200]{2,1,0:T(8,128)(2,1)}), bf16[8,24,3200]{2,1,0:T(8,128)(2,1)}, u32[]{:S(2)}, u32[]{:S(2)}) async-start(bf16[8,24,3200]{2,1,0:T(8,128)(2,1)} %bitcast.98), calls=%async_computation.4 | async-start | bytes 2457600 | tf_op jit(solution)/shard_map/all_to_all | solution.py:134
  298.0 5.9 %copy-start.34 = (bf16[768,768]{1,0:T(8,128)(2,1)S(1)}, bf16[768,768]{1,0:T(8,128)(2,1)}, u32[]{:S(2)}) copy-start(bf16[768,768]{1,0:T(8,128)(2,1)} %get-tuple-element.146) | copy-start | bytes 3538948
  298.0 5.9 %copy-start.42 = (bf16[192,768]{1,0:T(8,128)(2,1)S(1)}, bf16[192,768]{1,0:T(8,128)(2,1)}, u32[]{:S(2)}) copy-start(bf16[192,768]{1,0:T(8,128)(2,1)} %copy-done.41) | copy-start | bytes 884740
  298.0 5.9 %copy-start.44 = (bf16[192,768]{1,0:T(8,128)(2,1)S(1)}, bf16[192,768]{1,0:T(8,128)(2,1)}, u32[]{:S(2)}) copy-start(bf16[192,768]{1,0:T(8,128)(2,1)} %copy-done.43) | copy-start | bytes 884740
  302.4 5.6 %collective-permute-start.33 = (bf16[16,4736]{1,0:T(8,128)(2,1)S(1)}, bf16[16,4736]{1,0:T(8,128)(2,1)S(1)}, u32[]{:S(2)}, u32[]{:S(2)}) collective-permute-start(bf16[16,4736]{1,0:T(8,128)(2,1)S(1)} %pad_maximum_fusion.7), channel_id=1, source_target_pairs={{0,2},{1,3},{2,0},{3,1},{4,6},{5,7},{6,4},{7,5},{8,10},{9,11},{10,... | collective-permute-start | bytes 454664 | tf_op jit(solution)/shard_map/ppermute | solution.py:63
  329.0 5.4 %collective-permute-start.34 = (bf16[24,3200]{1,0:T(8,128)(2,1)}, bf16[24,3200]{1,0:T(8,128)(2,1)S(1)}, u32[]{:S(2)}, u32[]{:S(2)}) collective-permute-start(bf16[24,3200]{1,0:T(8,128)(2,1)} %reduce_sum.221), channel_id=1, source_target_pairs={{0,2},{1,3},{2,0},{3,1},{4,6},{5,7},{6,4},{7,5},{8,10},{9,11},{10,... | collective-permute-start | bytes 460808 | tf_op jit(solution)/shard_map/ppermute | solution.py:63
  335.5 1.7 collective-permute-start.35
  (58 other events, 176.7 us)
